TPU v7x, 256 devices: a whole 4x4x8 slice. The times are simulated.
256 devices in a mesh: atom: 8 (over x_lo, y), tm: 32 (over z, x_hi, core).
Axes of the slice: x: 4 (x_hi: 2, x_lo: 2; x = x_hi * 2 + x_lo), y: 4, z: 8, core: 2. Of those that a mesh axis runs over, the one named last changes fastest.
Arguments:
- signal: bfloat16 [306, 32768], P(None, 'tm'), may hold values from -6 to 6
- spatial: bfloat16 [256, 306], P('atom'), may hold values from -0.3125 to 0.3125
- temporal: bfloat16 [256, 256], P('atom'), may hold values from -0.375 to 0.375
- code_values: bfloat16 [256, 32768], P('atom', 'tm'), may hold values from 0 to 2
- block_mask: int32 [256, 128], P('atom', 'tm'), may hold values 0 or 1
Outputs:
- grad_spatial: float32 [256, 306], P('atom')
- grad_temporal: float32 [256, 256], P('atom')
All inputs are finite; a program needn't handle non-finite values. No bound on the sum of `block_mask` on one device may be relied on, other than what follows from the above.
Results may differ from a plain program's by a relative error of at most 0.0025.
Values may be sent and summed in bfloat16 or wider, within the bound.
No kernel may reach another device: no remote copies, remote signals or barrier semaphores. Data moves between devices by JAX's collectives and lax.ppermute only.
A program may use at most 64 MiB of HBM per device.

v0:
```python
import math

import jax
import jax.numpy as jnp
from jax import lax
from jax.sharding import PartitionSpec as P


def shifted(block, axis, distance):
    devices = range(lax.axis_size(axis))
    route = [(i - distance, i) for i in devices if i - distance in devices]
    return lax.ppermute(block, axis, route)


def cut_along(value, dim, length):
    before, after = (value.shape[:dim], value.shape[dim + 1 :])
    return jnp.moveaxis(value.reshape(*before, length, -1, *after), dim, 0)


def summed_on_arrival(value, axis, dim):
    pieces = cut_along(value, dim, lax.axis_size(axis))
    arrived = lax.all_to_all(pieces, axis, split_axis=0, concat_axis=0, tiled=True)
    return arrived.astype(jnp.float32).sum(axis=0)


def from_everyone(value, axis):
    copies = jnp.broadcast_to(value, (lax.axis_size(axis), *value.shape))
    return lax.all_to_all(copies, axis, split_axis=0, concat_axis=0, tiled=True)


def laid_out(pieces, dim):
    dims = list(pieces.shape[1:])
    dims[dim] *= pieces.shape[0]
    return jnp.moveaxis(pieces, 0, dim).reshape(dims)


def gather_directly(value, axis, dim):
    pieces = from_everyone(value, axis)
    return laid_out(pieces, dim)


def taken_together(value, axis):
    everything = from_everyone(value, axis)
    return jnp.sum(everything, axis=0)


def packed_total(arrays, axis):
    vector, at, finished = (jnp.concatenate([a.reshape(-1) for a in arrays]), 0, [])
    total = taken_together(vector, axis)
    for a in arrays:
        finished.append(total[at : at + a.size].reshape(a.shape))
        at += a.size
    return tuple(finished)


def toeplitz(kernels):
    count, length = kernels.shape
    heads = jnp.concatenate([jnp.zeros((count, 2 * length), kernels.dtype), kernels], axis=1)
    tiled = jnp.tile(heads, (1, 2 * length))[:, : 2 * length * (3 * length - 1)]
    return tiled.reshape(count, 2 * length, 3 * length - 1)[:, :, :length]


def diagonals(products):
    count, rows_all, length = products.shape
    padded = jnp.concatenate(
        [jnp.zeros((count, rows_all, 2 * length), products.dtype), products], axis=2
    )
    padded = padded.reshape(count, rows_all * 3 * length)
    padded = jnp.concatenate([padded, jnp.zeros((count, rows_all), products.dtype)], axis=1)
    skewed = padded.reshape(count, rows_all, 3 * length + 1)
    return jnp.sum(skewed, axis=1)[:, length : 2 * length]


def windows_of(extended, length):
    count, total = extended.shape
    blocks = extended.reshape(count, total // length, length)
    return jnp.concatenate([blocks[:, :-1], blocks[:, 1:]], axis=2)


def courses_of(extended, kernels, length, samples):
    count = extended.shape[0]

    def forward_group(operands):
        ext_group, group_kernels = operands
        windows = windows_of(ext_group, length)
        matrix = toeplitz(group_kernels)
        course_group = jnp.einsum(
            "gbm,gms->gbs", windows, matrix, preferred_element_type=jnp.float32
        )
        return course_group.reshape(4, samples).astype(jnp.bfloat16)

    result = lax.map(
        forward_group,
        (extended.reshape(count // 4, 4, length + samples), kernels.reshape(count // 4, 4, length)),
    )
    return result.reshape(count, samples)


def local(signal, spatial, temporal, code_values, block_mask):
    atoms, channels = spatial.shape
    length = temporal.shape[1]
    samples = signal.shape[1]
    nblocks = samples // length
    groups = atoms // 4
    codes = (
        code_values.reshape(atoms, nblocks, length) * block_mask[:, :, None].astype(jnp.bfloat16)
    ).reshape(atoms, samples)
    previous = shifted(codes[:, samples - length :], "tm", 1)
    extended = jnp.concatenate([previous, codes], axis=1)
    ext_groups = extended.reshape(groups, 4, length + samples)
    course = courses_of(extended, temporal, length, samples)
    partial_value = jnp.dot(spatial.T, course, preferred_element_type=jnp.float32)
    share = summed_on_arrival(partial_value.astype(jnp.bfloat16), "atom", 1)
    width = share.shape[1]
    start = lax.axis_index("atom") * width
    own_signal = lax.dynamic_slice_in_dim(signal, start, width, 1)
    residual_part = (share - own_signal.astype(jnp.float32)).astype(jnp.bfloat16)
    residual = gather_directly(residual_part, "atom", 1)
    projected = jnp.dot(spatial, residual, preferred_element_type=jnp.float32).astype(jnp.bfloat16)
    spatial_part = lax.dot_general(
        course, residual, (((1,), (1,)), ((), ())), preferred_element_type=jnp.float32
    )

    def adjoint_group(operands):
        ext_group, proj_group = operands
        windows = windows_of(ext_group, length)
        proj_blocks = proj_group.reshape(4, nblocks, length)
        products = jnp.einsum(
            "gbm,gbs->gms", windows, proj_blocks, preferred_element_type=jnp.float32
        )
        return diagonals(products)

    temporal_part = lax.map(
        adjoint_group, (ext_groups, projected.reshape(groups, 4, samples))
    ).reshape(atoms, length)
    spatial_sum, temporal_sum = packed_total((spatial_part, temporal_part), "tm")
    factor = 1.0 / math.sqrt(samples * lax.axis_size("tm"))
    return (spatial_sum * factor, temporal_sum * factor)


def solution(mesh):
    in_specs = (P(None, "tm"), P("atom", None), P("atom", None), P("atom", "tm"), P("atom", "tm"))
    out_specs = (P("atom", None), P("atom", None))
    return jax.shard_map(local, mesh=mesh, in_specs=in_specs, out_specs=out_specs, check_vma=False)
```

profile of v0, /device:TPU:1, one launch (start us, length us, event | category | flops | bytes accessed | tf_op | source)
XLA Modules:
  0.0 455.5 jit_solution(15938708789744694108)
XLA Ops:
  2.4 6.0 %collective-permute-start = (bf16[32,256]{1,0:T(8,128)(2,1)S(1)}, bf16[32,256]{1,0:T(8,128)(2,1)S(1)}, u32[]{:S(2)}, u32[]{:S(2)}) collective-permute-start(bf16[32,256]{1,0:T(8,128)(2,1)S(1)} %slice.40), channel_id=1, source_target_pairs={{0,1},{1,2},{2,3},{3,4},{4,5},{5,6},{6,7},{7,8},{8,9},{9,10},{10,1... | collective-permute-start | bytes 49160 | tf_op jit(solution)/shard_map/ppermute | solution.py:12
  9.4 126.7 %while.20 = (s32[]{:T(128)}, bf16[8,4,1024]{2,1,0:T(4,128)(2,1)S(1)}, bf16[8,4,1280]{2,1,0:T(4,128)(2,1)S(1)}, bf16[8,4,256]{2,1,0:T(4,128)(2,1)S(1)}, s32[]{:T(128)}, /*index=5*/bf16[]{:T(256)}) while((s32[]{:T(128)}, bf16[8,4,1024]{2,1,0:T(4,128)(2,1)S(1)}, bf16[8,4,1280]{2,1,0:T(4,128)(2,1)S(1)}, bf16[8,4,256]{2,1,0:T(4,128)(2,1)S(1)}, ...), condition=%wide.region_1.2_spmd, body=%wide.region_0.1_spmd.sunk | while | flops 4231170 | bytes 29485140 | solution.py:92
  9.7 2.4 copy.32
  13.3 2.8 reshape.92
  16.2 8.8 %reshape.93 = bf16[4,512,767]{2,1,0:T(8,128)(2,1)S(1)} reshape(bf16[1570816]{0:T(1024)(128)(2,1)} %reshape.92) | data formatting | bytes 6283264 | tf_op jit(solution)/shard_map/while/body/eval_jaxpr/reshape | solution.py:60
  25.6 2.4 copy.32
  29.2 2.8 reshape.92
  32.0 8.8 %reshape.93 = bf16[4,512,767]{2,1,0:T(8,128)(2,1)S(1)} reshape(bf16[1570816]{0:T(1024)(128)(2,1)} %reshape.92) | data formatting | bytes 6283264 | tf_op jit(solution)/shard_map/while/body/eval_jaxpr/reshape | solution.py:60
  41.4 2.4 copy.32
  45.0 2.8 reshape.92
  47.8 8.8 %reshape.93 = bf16[4,512,767]{2,1,0:T(8,128)(2,1)S(1)} reshape(bf16[1570816]{0:T(1024)(128)(2,1)} %reshape.92) | data formatting | bytes 6283264 | tf_op jit(solution)/shard_map/while/body/eval_jaxpr/reshape | solution.py:60
  57.2 2.4 copy.32
  60.8 2.8 reshape.92
  63.7 8.8 %reshape.93 = bf16[4,512,767]{2,1,0:T(8,128)(2,1)S(1)} reshape(bf16[1570816]{0:T(1024)(128)(2,1)} %reshape.92) | data formatting | bytes 6283264 | tf_op jit(solution)/shard_map/while/body/eval_jaxpr/reshape | solution.py:60
  73.1 2.4 copy.32
  76.7 2.8 reshape.92
  79.5 8.8 %reshape.93 = bf16[4,512,767]{2,1,0:T(8,128)(2,1)S(1)} reshape(bf16[1570816]{0:T(1024)(128)(2,1)} %reshape.92) | data formatting | bytes 6283264 | tf_op jit(solution)/shard_map/while/body/eval_jaxpr/reshape | solution.py:60
  88.9 2.4 copy.32
  92.5 2.8 reshape.92
  95.4 8.8 %reshape.93 = bf16[4,512,767]{2,1,0:T(8,128)(2,1)S(1)} reshape(bf16[1570816]{0:T(1024)(128)(2,1)} %reshape.92) | data formatting | bytes 6283264 | tf_op jit(solution)/shard_map/while/body/eval_jaxpr/reshape | solution.py:60
  104.8 2.4 copy.32
  108.4 2.8 reshape.92
  111.2 8.8 %reshape.93 = bf16[4,512,767]{2,1,0:T(8,128)(2,1)S(1)} reshape(bf16[1570816]{0:T(1024)(128)(2,1)} %reshape.92) | data formatting | bytes 6283264 | tf_op jit(solution)/shard_map/while/body/eval_jaxpr/reshape | solution.py:60
  120.6 2.4 copy.32
  124.2 2.8 reshape.92
  127.0 8.8 %reshape.93 = bf16[4,512,767]{2,1,0:T(8,128)(2,1)S(1)} reshape(bf16[1570816]{0:T(1024)(128)(2,1)} %reshape.92) | data formatting | bytes 6283264 | tf_op jit(solution)/shard_map/while/body/eval_jaxpr/reshape | solution.py:60
  137.6 4.2 all-to-all-start
  141.9 9.6 %all-to-all-done = bf16[8,306,128]{2,1,0:T(8,128)(2,1)S(1)} async-done(((bf16[8,306,128]{2,1,0:T(8,128)(2,1)}), bf16[8,306,128]{2,1,0:T(8,128)(2,1)S(1)}, u32[]{:S(2)}, u32[]{:S(2)}) %all-to-all-start) | async-done | bytes 626720 | tf_op jit(solution)/shard_map/all_to_all | solution.py:22
  153.4 3.5 all-to-all-start.1
  156.9 9.4 %all-to-all-done.1 = bf16[8,306,128]{2,1,0:T(8,128)(2,1)S(1)} async-done(((bf16[8,306,128]{2,1,0:T(8,128)(2,1)}), bf16[8,306,128]{2,1,0:T(8,128)(2,1)S(1)}, u32[]{:S(2)}, u32[]{:S(2)}) %all-to-all-start.1) | async-done | bytes 626720 | tf_op jit(solution)/shard_map/all_to_all | solution.py:28
  167.3 214.4 %while.21 = (s32[]{:T(128)}, f32[8,4,256]{2,1,0:T(4,128)S(1)}, bf16[8,4,1280]{2,1,0:T(4,128)(2,1)S(1)}, bf16[8,4,1024]{2,1,0:T(4,128)(2,1)S(1)}, s32[]{:T(128)}, /*index=5*/f32[]{:T(128)}) while((s32[]{:T(128)}, f32[8,4,256]{2,1,0:T(4,128)S(1)}, bf16[8,4,1280]{2,1,0:T(4,128)(2,1)S(1)}, bf16[8,4,1024]{2,1,0:T(4,128)(2,1)S(1)}, s32[]{:T(128)}, ...), condition=%wide.region_5.6_spmd, body=%wide.region_3.5_spmd.sunk | while | flops 5798910 | bytes 54710376 | solution.py:133
  168.6 4.0 copy.33
  172.7 3.6 concatenate.36
  176.2 14.5 %reshape.97 = f32[4,512,769]{2,1,0:T(8,128)} reshape(f32[4,393728]{1,0:T(4,128)} %concatenate.36) | data formatting | bytes 12599296 | tf_op jit(solution)/shard_map/while/body/eval_jaxpr/reshape | solution.py:70
  190.8 3.5 reduce_sum.31
  195.4 4.0 copy.33
  199.4 3.6 concatenate.36
  203.0 14.5 %reshape.97 = f32[4,512,769]{2,1,0:T(8,128)} reshape(f32[4,393728]{1,0:T(4,128)} %concatenate.36) | data formatting | bytes 12599296 | tf_op jit(solution)/shard_map/while/body/eval_jaxpr/reshape | solution.py:70
  217.5 3.5 reduce_sum.31
  222.1 4.0 copy.33
  226.2 3.6 concatenate.36
  229.7 14.5 %reshape.97 = f32[4,512,769]{2,1,0:T(8,128)} reshape(f32[4,393728]{1,0:T(4,128)} %concatenate.36) | data formatting | bytes 12599296 | tf_op jit(solution)/shard_map/while/body/eval_jaxpr/reshape | solution.py:70
  244.3 3.5 reduce_sum.31
  248.9 4.0 copy.33
  252.9 3.6 concatenate.36
  256.5 14.5 %reshape.97 = f32[4,512,769]{2,1,0:T(8,128)} reshape(f32[4,393728]{1,0:T(4,128)} %concatenate.36) | data formatting | bytes 12599296 | tf_op jit(solution)/shard_map/while/body/eval_jaxpr/reshape | solution.py:70
  271.0 3.5 reduce_sum.31
  275.6 4.0 copy.33
  279.7 3.6 concatenate.36
  283.3 14.5 %reshape.97 = f32[4,512,769]{2,1,0:T(8,128)} reshape(f32[4,393728]{1,0:T(4,128)} %concatenate.36) | data formatting | bytes 12599296 | tf_op jit(solution)/shard_map/while/body/eval_jaxpr/reshape | solution.py:70
  297.8 3.5 reduce_sum.31
  302.4 4.0 copy.33
  306.4 3.6 concatenate.36
  310.0 14.5 %reshape.97 = f32[4,512,769]{2,1,0:T(8,128)} reshape(f32[4,393728]{1,0:T(4,128)} %concatenate.36) | data formatting | bytes 12599296 | tf_op jit(solution)/shard_map/while/body/eval_jaxpr/reshape | solution.py:70
  324.5 3.5 reduce_sum.31
  329.1 4.0 copy.33
  333.2 3.6 concatenate.36
  336.8 14.5 %reshape.97 = f32[4,512,769]{2,1,0:T(8,128)} reshape(f32[4,393728]{1,0:T(4,128)} %concatenate.36) | data formatting | bytes 12599296 | tf_op jit(solution)/shard_map/while/body/eval_jaxpr/reshape | solution.py:70
  351.3 3.5 reduce_sum.31
  355.9 4.0 copy.33
  360.0 3.6 concatenate.36
  363.5 14.5 %reshape.97 = f32[4,512,769]{2,1,0:T(8,128)} reshape(f32[4,393728]{1,0:T(4,128)} %concatenate.36) | data formatting | bytes 12599296 | tf_op jit(solution)/shard_map/while/body/eval_jaxpr/reshape | solution.py:70
  378.0 3.5 reduce_sum.31
  383.0 69.7 %all_to_all.16 = f32[32,1,17984]{2,1,0:T(1,128)S(1)} all-to-all(f32[32,1,17984]{2,1,0:T(1,128)S(1)} %broadcast_in_dim.22), channel_id=1, replica_groups=mesh['atom'=8,'tm'=32] {'tm'}, dimensions={0} | all-to-all | bytes 4603904 | tf_op jit(solution)/shard_map/all_to_all | solution.py:28
  (183 shorter events, 33.4 us)
Async XLA Ops:
  0.6 135.5 %copy-start = (bf16[32,306]{1,0:T(8,128)(2,1)S(1)}, bf16[32,306]{1,0:T(8,128)(2,1)}, u32[]{:S(2)}) copy-start(bf16[32,306]{1,0:T(8,128)(2,1)} %param.10) | copy-start | bytes 58756
  2.4 6.9 %collective-permute-start = (bf16[32,256]{1,0:T(8,128)(2,1)S(1)}, bf16[32,256]{1,0:T(8,128)(2,1)S(1)}, u32[]{:S(2)}, u32[]{:S(2)}) collective-permute-start(bf16[32,256]{1,0:T(8,128)(2,1)S(1)} %slice.40), channel_id=1, source_target_pairs={{0,1},{1,2},{2,3},{3,4},{4,5},{5,6},{6,7},{7,8},{8,9},{9,10},{10,1... | collective-permute-start | bytes 49160 | tf_op jit(solution)/shard_map/ppermute | solution.py:12
  137.6 13.8 %all-to-all-start = ((bf16[8,306,128]{2,1,0:T(8,128)(2,1)}), bf16[8,306,128]{2,1,0:T(8,128)(2,1)S(1)}, u32[]{:S(2)}, u32[]{:S(2)}) async-start(bf16[8,306,128]{2,1,0:T(8,128)(2,1)} %bitcast.35), calls=%async_computation | async-start | bytes 1277952 | tf_op jit(solution)/shard_map/all_to_all | solution.py:22
  153.4 13.0 %all-to-all-start.1 = ((bf16[8,306,128]{2,1,0:T(8,128)(2,1)}), bf16[8,306,128]{2,1,0:T(8,128)(2,1)S(1)}, u32[]{:S(2)}, u32[]{:S(2)}) async-start(bf16[8,306,128]{2,1,0:T(8,128)(2,1)} %broadcast_in_dim.20), calls=%async_computation.1 | async-start | bytes 1277952 | tf_op jit(solution)/shard_map/all_to_all | solution.py:28
where the time goes:
time: 457 us; the launch traced here: 456 us
  local copies, waits for them, and re-layouts  312 us (68%)
  blocking collectives  69.7 us (15%)
  other arithmetic  31.7 us (7%)
  waiting for transfers between devices  19.1 us (4%)
  starting transfers between devices  13.8 us (3%)
  matrix products  6.71 us (1%)
    reshape x8, local copies, waits for them, and re-layouts, diagonals(): skewed = padded.reshape(count, rows_all, 3 * length + 1)  116 us
    while x40, local copies, waits for them, and re-layouts  80.4 us
    reshape x8, local copies, waits for them, and re-layouts, toeplitz(): return tiled.reshape(count, 2 * length, 3 * length - 1)[:, :, :length]  70.4 us
    all_to_all x1, blocking collectives, from_everyone(): return lax.all_to_all(copies, axis, split_axis=0, concat_axis=0, tiled=True)  69.7 us
    concatenate x8, local copies, waits for them, and re-layouts, diagonals(): jnp.concatenate([padded, jnp.zeros((count, rows_all), products.dtype)], a...  28.5 us
    reduce_sum x8, other arithmetic, diagonals(): return jnp.sum(skewed, axis=1)[:, length:2 * length]  27.6 us
    all_to_all x1, waiting for transfers between devices, summed_on_arrival(): lax.all_to_all(pieces, axis, split_axis=0, concat_axis=0, tiled=True)  9.57 us
    all_to_all x1, waiting for transfers between devices, from_everyone(): return lax.all_to_all(copies, axis, split_axis=0, concat_axis=0, tiled=True)  9.41 us
  transfers between devices with their start and end apart: 3, of which 3 were waited for; matrix products, arithmetic and copies ran while one was open for 0% of the time, Pallas kernels for 0%

commit v1 on v0

v1 whole, which is shorter than its diff:
```python
import math

import jax
import jax.numpy as jnp
from jax import lax
from jax.experimental import pallas as pl
from jax.experimental.pallas import tpu as pltpu
from jax.sharding import PartitionSpec as P

LANES = 128


def up(n, m):
    return -(-n // m) * m


def lower_band(size):
    rows = lax.broadcasted_iota(jnp.int32, (size, size), 0)
    cols = lax.broadcasted_iota(jnp.int32, (size, size), 1)
    return cols >= rows


def course_kernel(cv_ref, mask_ref, halo_ref, temporal_ref, spatial_ref, send_ref, xs_ref, tf_ref, cs_ref):
    copies, atoms, width = send_ref.shape
    length = temporal_ref.shape[1]
    samples = cv_ref.shape[1]
    channels = spatial_ref.shape[1]
    for j in range(length // LANES):
        xs_ref[j * atoms : (j + 1) * atoms, :] = halo_ref[:, j * LANES : (j + 1) * LANES].astype(jnp.float32)
    for b in range(samples // length):
        on = mask_ref[:, b : b + 1].astype(jnp.float32)
        block = cv_ref[:, b * length : (b + 1) * length].astype(jnp.float32) * on
        for j in range(length // LANES):
            at = (length // LANES * (b + 1) + j) * atoms
            xs_ref[at : at + atoms, :] = block[:, j * LANES : (j + 1) * LANES]
    tf_ref[...] = temporal_ref[...].astype(jnp.float32)
    band = lower_band(LANES)
    rows = samples // LANES
    for k in range(atoms):
        near = pltpu.roll(
            jnp.broadcast_to(tf_ref[k : k + 1, :LANES], (LANES, LANES)), 0, 1, stride=1, stride_axis=0
        )
        far = pltpu.roll(
            jnp.broadcast_to(tf_ref[k : k + 1, LANES:], (LANES, LANES)), 0, 1, stride=1, stride_axis=0
        )
        matrix = jnp.concatenate(
            [jnp.where(band, 0.0, far), jnp.where(band, far, near), jnp.where(band, near, 0.0)], axis=0
        ).astype(jnp.bfloat16)
        windows = jnp.concatenate(
            [xs_ref[pl.ds(j * atoms + k, rows, stride=atoms), :] for j in range(3)], axis=1
        ).astype(jnp.bfloat16)
        cs_ref[pl.ds(k, rows, stride=atoms), :] = jnp.dot(
            windows, matrix, preferred_element_type=jnp.float32
        )
    padded = jnp.concatenate(
        [spatial_ref[...], jnp.zeros((atoms, width - samples - channels), jnp.bfloat16)], axis=1
    )
    for c in range(copies):
        send_ref[c, :, samples:] = padded
    for i in range(rows):
        part = cs_ref[i * atoms : (i + 1) * atoms, :].astype(jnp.bfloat16)
        for c in range(copies):
            send_ref[c, :, i * LANES : (i + 1) * LANES] = part


def gradient_kernel(factor, all_ref, own_ref, xs_ref, signal_ref, out_ref, res_ref, pr_ref, lo_ref, hi_ref):
    groups, atoms, width = all_ref.shape
    channels, samples = signal_ref.shape
    wide = width - samples
    everything = all_ref[...].reshape(groups * atoms, width)
    model = lax.dot_general(
        everything[:, samples:],
        everything[:, :samples],
        (((0,), (0,)), ((), ())),
        preferred_element_type=jnp.float32,
    )
    res_ref[channels:, :] = jnp.zeros((wide - channels, samples), jnp.bfloat16)
    res_ref[:channels, :] = (model[:channels] - signal_ref[...].astype(jnp.float32)).astype(jnp.bfloat16)
    own = own_ref[0]
    projected = jnp.dot(own[:, samples:], res_ref[...], preferred_element_type=jnp.float32)
    out_ref[:, :wide] = factor * lax.dot_general(
        own[:, :samples], res_ref[...], (((1,), (1,)), ((), ())), preferred_element_type=jnp.float32
    )
    rows = samples // LANES
    for i in range(rows):
        pr_ref[i * atoms : (i + 1) * atoms, :] = projected[:, i * LANES : (i + 1) * LANES]
    band = lower_band(LANES)
    for k in range(atoms):
        proj = pr_ref[pl.ds(k, rows, stride=atoms), :].astype(jnp.bfloat16)
        windows = jnp.concatenate(
            [xs_ref[pl.ds(j * atoms + k, rows, stride=atoms), :] for j in range(3)], axis=1
        ).astype(jnp.bfloat16)
        products = lax.dot_general(
            windows, proj, (((0,), (0,)), ((), ())), preferred_element_type=jnp.float32
        )
        old, mid, new = products[:LANES], products[LANES : 2 * LANES], products[2 * LANES :]
        for ref, total in ((lo_ref, jnp.where(band, new, mid)), (hi_ref, jnp.where(band, mid, old))):
            parts = [total[:8]]
            for a in range(1, LANES // 8):
                parts.append(pltpu.roll(total[8 * a : 8 * a + 8], LANES - 8 * a, 1))
            while len(parts) > 1:
                parts = [x + y for x, y in zip(parts[::2], parts[1::2], strict=True)]
            ref[8 * k : 8 * k + 8, :] = parts[0]
    row = lax.broadcasted_iota(jnp.int32, (8 * atoms, LANES), 0)
    for at, ref in ((wide, lo_ref), (wide + LANES, hi_ref)):
        total = ref[...]
        for bit in (1, 2, 4):
            total = jnp.where((row & bit) != 0, pltpu.roll(total, LANES - bit, 1), total)
        out_ref[:, at : at + LANES] = factor * total.reshape(atoms, 8, LANES).sum(axis=1)


def local(signal, spatial, temporal, code_values, block_mask):
    atoms, channels = spatial.shape
    length = temporal.shape[1]
    samples = signal.shape[1]
    groups, slabs = lax.axis_size("atom"), lax.axis_size("tm")
    rows = samples // LANES
    wide = up(channels, LANES)
    factor = 1.0 / math.sqrt(samples * slabs)

    tail = code_values[:, samples - length :] * block_mask[:, -1:].astype(code_values.dtype)
    halo = lax.ppermute(tail, "tm", [(i, i + 1) for i in range(slabs - 1)])
    send, xs = pl.pallas_call(
        course_kernel,
        out_shape=(
            jax.ShapeDtypeStruct((groups, atoms, samples + wide), jnp.bfloat16),
            jax.ShapeDtypeStruct(((rows + length // LANES) * atoms, LANES), jnp.float32),
        ),
        scratch_shapes=[
            pltpu.VMEM((atoms, length), jnp.float32),
            pltpu.VMEM((rows * atoms, LANES), jnp.float32),
        ],
        compiler_params=pltpu.CompilerParams(vmem_limit_bytes=32 << 20),
        name="course",
    )(code_values, block_mask, halo, temporal, spatial)
    everything = lax.all_to_all(send, "atom", split_axis=0, concat_axis=0, tiled=True)
    part = pl.pallas_call(
        lambda *refs: gradient_kernel(factor, *refs),
        grid=(1,),
        in_specs=[
            pl.BlockSpec(everything.shape, lambda i: (0, 0, 0)),
            pl.BlockSpec((1, *send.shape[1:]), lambda i: (0, 0, 0)),
            pl.BlockSpec(xs.shape, lambda i: (0, 0)),
            pl.BlockSpec(signal.shape, lambda i: (0, 0)),
        ],
        out_specs=pl.BlockSpec((atoms, wide + length), lambda i: (0, 0)),
        out_shape=jax.ShapeDtypeStruct((atoms, wide + length), jnp.float32),
        scratch_shapes=[
            pltpu.VMEM((wide, samples), jnp.bfloat16),
            pltpu.VMEM((rows * atoms, LANES), jnp.float32),
            pltpu.VMEM((8 * atoms, LANES), jnp.float32),
            pltpu.VMEM((8 * atoms, LANES), jnp.float32),
        ],
        compiler_params=pltpu.CompilerParams(vmem_limit_bytes=32 << 20),
        name="gradients",
    )(everything, send, xs, signal)
    bit = 1
    while bit < slabs:
        part = part + lax.ppermute(part, "tm", [(i, i ^ bit) for i in range(slabs)])
        bit *= 2
    return (part[:, :channels], part[:, wide:])


def solution(mesh):
    in_specs = (P(None, "tm"), P("atom", None), P("atom", None), P("atom", "tm"), P("atom", "tm"))
    out_specs = (P("atom", None), P("atom", None))
    return jax.shard_map(local, mesh=mesh, in_specs=in_specs, out_specs=out_specs, check_vma=False)
```

time: 457 us -> 58.9 us (0.13)
  the two profiles are of different devices: /device:TPU:1 before, /device:TPU:64 now
where the time goes in v1:
time: 58.9 us; the launch traced here: 58.6 us
  waiting for transfers between devices  22.3 us (38%)
  blocking collectives  15.2 us (26%)
  starting transfers between devices  13.2 us (22%)
  Pallas kernels  3.31 us (6%)
  local copies, waits for them, and re-layouts  2.2 us (4%)
  other arithmetic  1.55 us (3%)
  between operations  0.72 us (1%)
    ppermute x5, waiting for transfers between devices, local(): part = part + lax.ppermute(part, 'tm', [(i, i ^ bit) for i in range(slabs)])  16.9 us
    all_to_all x1, blocking collectives, local(): lax.all_to_all(send, 'atom', split_axis=0, concat_axis=0, tiled=True)  15.2 us
    ppermute x5, starting transfers between devices, local(): part = part + lax.ppermute(part, 'tm', [(i, i ^ bit) for i in range(slabs)])  11.2 us
    ppermute x1, waiting for transfers between devices, local(): halo = lax.ppermute(tail, 'tm', [(i, i + 1) for i in range(slabs - 1)])  5.43 us
    pallas_call x1, Pallas kernels, local(): pl.pallas_call(lambda *refs: gradient_kernel(factor, *refs), grid=(1,), i...  2.49 us
    ppermute x1, starting transfers between devices, local(): halo = lax.ppermute(tail, 'tm', [(i, i + 1) for i in range(slabs - 1)])  2.04 us
    slice x2, local copies, waits for them, and re-layouts, local(): return (part[:, :channels], part[:, wide:])  1.24 us
  transfers between devices with their start and end apart: 6, of which 6 were waited for; matrix products, arithmetic and copies ran while one was open for 0% of the time, Pallas kernels for 0%

profile of v1, /device:TPU:64, one launch (start us, length us, event | category | flops | bytes accessed | tf_op | source)
XLA Modules:
  0.0 58.6 jit_solution(15618491870520944717)
XLA Ops:
  0.6 0.7 %convert.3 = bf16[32,4]{0,1:T(4,128)(2,1)S(1)} convert(s32[32,4]{0,1:T(4,128)} %param.9) | non-fusion elementwise | flops 128 | bytes 768 | tf_op jit(solution)/shard_map/convert
  1.3 0.0 copy-start.4
  1.3 0.0 copy-start.2
  1.3 0.8 %slice_multiply_fusion = bf16[32,256]{1,0:T(8,128)(2,1)S(1)} fusion(bf16[32,1024]{1,0:T(8,128)(2,1)} %cv_ref.1, bf16[32]{0:T(256)(128)(2,1)S(1)} %slice_bitcast_fusion), kind=kLoop, calls=%fused_computation | loop fusion | flops 8192 | bytes 32832 | tf_op jit(solution)/shard_map/mul | solution.py:121
  2.1 0.0 copy-start.3
  2.1 2.0 %collective-permute-start = (bf16[32,256]{1,0:T(8,128)(2,1)S(1)}, bf16[32,256]{1,0:T(8,128)(2,1)S(1)}, u32[]{:S(2)}, u32[]{:S(2)}) collective-permute-start(bf16[32,256]{1,0:T(8,128)(2,1)S(1)} %slice_multiply_fusion), channel_id=1, source_target_pairs={{0,1},{1,2},{2,3},{3,4},{4,5},{5,6},{6,7},{7,8},{8,9},{9,10},{10,1... | collective-permute-start | bytes 49160 | tf_op jit(solution)/shard_map/ppermute | solution.py:122
  4.2 0.0 copy-done.4
  4.2 0.1 copy.7.mask_ref
  4.3 5.4 %collective-permute-done.halo_ref = bf16[32,256]{1,0:T(8,128)(2,1)S(1)} collective-permute-done((bf16[32,256]{1,0:T(8,128)(2,1)S(1)}, bf16[32,256]{1,0:T(8,128)(2,1)S(1)}, u32[]{:S(2)}, u32[]{:S(2)}) %collective-permute-start) | collective-permute-done | bytes 16416 | tf_op jit(solution)/shard_map/ppermute | solution.py:122
  9.7 0.0 copy-done.2
  9.7 0.0 copy-done.3
  9.7 0.0 copy-start.1
  9.7 0.8 %copy-done.1 = bf16[32,1024]{1,0:T(8,128)(2,1)S(1)} copy-done((bf16[32,1024]{1,0:T(8,128)(2,1)S(1)}, bf16[32,1024]{1,0:T(8,128)(2,1)}, u32[]{:S(2)}) %copy-start.1) | copy-done | bytes 65560
  10.6 0.8 %course.1 = (bf16[8,32,1408]{2,1,0:T(8,128)(2,1)S(1)}, f32[320,128]{1,0:T(8,128)S(1)}) custom-call(bf16[32,1024]{1,0:T(8,128)(2,1)S(1)} %copy-done.1, s32[32,4]{1,0:T(8,128)S(1)} %copy.7.mask_ref, bf16[32,256]{1,0:T(8,128)(2,1)S(1)} %collective-permute-done.halo_ref, bf16[32,256]{1,0:T(8,128)(2,1)S(1)} %copy-done.3, bf16[32,306]{1,0:T(8,128)(2,1)S(1)} %copy-done.2), custom_call_target="tpu_custom_call" | custom-call | tf_op jit(solution)/shard_map/course/pallas_call | solution.py:123
  11.4 0.0 copy-start
  11.4 15.2 %all_to_all.5.refs_0_ = bf16[8,32,1408]{2,1,0:T(8,128)(2,1)S(1)} all-to-all(bf16[8,32,1408]{2,1,0:T(8,128)(2,1)S(1)} %get-tuple-element.4.refs_1_), channel_id=1, replica_groups=mesh['atom'=8,'tm'=32] {'atom'}, dimensions={0} | all-to-all | bytes 1441792 | tf_op jit(solution)/shard_map/all_to_all | solution.py:136
  26.6 0.0 copy-done
  26.7 2.5 %gradients.1 = f32[32,640]{1,0:T(8,128)S(1)} custom-call(bf16[8,32,1408]{2,1,0:T(8,128)(2,1)S(1)} %all_to_all.5.refs_0_, bf16[8,32,1408]{2,1,0:T(8,128)(2,1)S(1)} %get-tuple-element.4.refs_1_, f32[320,128]{1,0:T(8,128)S(1)} %get-tuple-element.5.refs_2_, bf16[306,1024]{1,0:T(8,128)(2,1)S(1)} %copy-done), custom_call_target="tpu_custom_call" | custom-call | tf_op jit(solution)/shard_map/gradients/pallas_call | solution.py:137
  29.1 0.1 collective-permute-start.1
  29.2 1.3 %collective-permute-done.1 = f32[32,640]{1,0:T(8,128)S(1)} collective-permute-done((f32[32,640]{1,0:T(8,128)S(1)}, f32[32,640]{1,0:T(8,128)S(1)}, u32[]{:S(2)}, u32[]{:S(2)}) %collective-permute-start.1) | collective-permute-done | bytes 81952 | tf_op jit(solution)/shard_map/ppermute | solution.py:159
  30.5 3.5 %collective-permute-start.2 = (f32[32,640]{1,0:T(8,128)S(1)}, f32[32,640]{1,0:T(8,128)S(1)}, u32[]{:S(2)}, u32[]{:S(2)}) collective-permute-start(f32[32,640]{1,0:T(8,128)S(1)} %add.15), channel_id=1, source_target_pairs={{0,2},{1,3},{2,0},{3,1},{4,6},{5,7},{6,4},{7,5},{8,10},{9,11},{10,... | collective-permute-start | bytes 245768 | tf_op jit(solution)/shard_map/ppermute | solution.py:159
  34.0 2.8 %collective-permute-done.2 = f32[32,640]{1,0:T(8,128)S(1)} collective-permute-done((f32[32,640]{1,0:T(8,128)S(1)}, f32[32,640]{1,0:T(8,128)S(1)}, u32[]{:S(2)}, u32[]{:S(2)}) %collective-permute-start.2) | collective-permute-done | bytes 81952 | tf_op jit(solution)/shard_map/ppermute | solution.py:159
  36.8 3.2 %collective-permute-start.3 = (f32[32,640]{1,0:T(8,128)S(1)}, f32[32,640]{1,0:T(8,128)S(1)}, u32[]{:S(2)}, u32[]{:S(2)}) collective-permute-start(f32[32,640]{1,0:T(8,128)S(1)} %add.16), channel_id=1, source_target_pairs={{0,4},{1,5},{2,6},{3,7},{4,0},{5,1},{6,2},{7,3},{8,12},{9,13},{10,... | collective-permute-start | bytes 245768 | tf_op jit(solution)/shard_map/ppermute | solution.py:159
  40.0 2.4 %collective-permute-done.3 = f32[32,640]{1,0:T(8,128)S(1)} collective-permute-done((f32[32,640]{1,0:T(8,128)S(1)}, f32[32,640]{1,0:T(8,128)S(1)}, u32[]{:S(2)}, u32[]{:S(2)}) %collective-permute-start.3) | collective-permute-done | bytes 81952 | tf_op jit(solution)/shard_map/ppermute | solution.py:159
  42.4 0.1 collective-permute-start.4
  42.5 5.4 %collective-permute-done.4 = f32[32,640]{1,0:T(8,128)S(1)} collective-permute-done((f32[32,640]{1,0:T(8,128)S(1)}, f32[32,640]{1,0:T(8,128)S(1)}, u32[]{:S(2)}, u32[]{:S(2)}) %collective-permute-start.4) | collective-permute-done | bytes 81952 | tf_op jit(solution)/shard_map/ppermute | solution.py:159
  47.9 4.3 %collective-permute-start.5 = (f32[32,640]{1,0:T(8,128)S(1)}, f32[32,640]{1,0:T(8,128)S(1)}, u32[]{:S(2)}, u32[]{:S(2)}) collective-permute-start(f32[32,640]{1,0:T(8,128)S(1)} %add.18), channel_id=1, source_target_pairs={{0,16},{1,17},{2,18},{3,19},{4,20},{5,21},{6,22},{7,23},{8,24},{9,... | collective-permute-start | bytes 245768 | tf_op jit(solution)/shard_map/ppermute | solution.py:159
  52.2 5.1 %collective-permute-done.5 = f32[32,640]{1,0:T(8,128)S(1)} collective-permute-done((f32[32,640]{1,0:T(8,128)S(1)}, f32[32,640]{1,0:T(8,128)S(1)}, u32[]{:S(2)}, u32[]{:S(2)}) %collective-permute-start.5) | collective-permute-done | bytes 81952 | tf_op jit(solution)/shard_map/ppermute | solution.py:159
  57.3 0.6 %slice.18 = f32[32,256]{1,0:T(8,128)} slice(f32[32,640]{1,0:T(8,128)S(1)} %add.19), slice={[0:32], [384:640]} | slice | bytes 65536 | tf_op jit(solution)/shard_map/slice | solution.py:161
  57.9 0.6 %slice.17 = f32[32,306]{1,0:T(8,128)} slice(f32[32,640]{1,0:T(8,128)S(1)} %add.19), slice={[0:32], [0:306]} | slice | bytes 78336 | tf_op jit(solution)/shard_map/slice | solution.py:161
  (6 shorter events, 0.1 us)
Async XLA Ops:
  1.3 2.9 %copy-start.4 = (s32[32,4]{0,1:T(4,128)S(1)}, s32[32,4]{0,1:T(4,128)}, u32[]{:S(2)}) copy-start(s32[32,4]{0,1:T(4,128)} %param.9) | copy-start | bytes 1540
  1.3 8.4 %copy-start.2 = (bf16[32,306]{1,0:T(8,128)(2,1)S(1)}, bf16[32,306]{1,0:T(8,128)(2,1)}, u32[]{:S(2)}) copy-start(bf16[32,306]{1,0:T(8,128)(2,1)} %spatial_ref.1) | copy-start | bytes 58756
  2.1 7.6 %copy-start.3 = (bf16[32,256]{1,0:T(8,128)(2,1)S(1)}, bf16[32,256]{1,0:T(8,128)(2,1)}, u32[]{:S(2)}) copy-start(bf16[32,256]{1,0:T(8,128)(2,1)} %temporal_ref.1) | copy-start | bytes 49156
  2.1 7.6 %collective-permute-start = (bf16[32,256]{1,0:T(8,128)(2,1)S(1)}, bf16[32,256]{1,0:T(8,128)(2,1)S(1)}, u32[]{:S(2)}, u32[]{:S(2)}) collective-permute-start(bf16[32,256]{1,0:T(8,128)(2,1)S(1)} %slice_multiply_fusion), channel_id=1, source_target_pairs={{0,1},{1,2},{2,3},{3,4},{4,5},{5,6},{6,7},{7,8},{8,9},{9,10},{10,1... | collective-permute-start | bytes 49160 | tf_op jit(solution)/shard_map/ppermute | solution.py:122
  9.7 0.8 %copy-start.1 = (bf16[32,1024]{1,0:T(8,128)(2,1)S(1)}, bf16[32,1024]{1,0:T(8,128)(2,1)}, u32[]{:S(2)}) copy-start(bf16[32,1024]{1,0:T(8,128)(2,1)} %cv_ref.1) | copy-start | bytes 196612
  11.4 15.2 %copy-start = (bf16[306,1024]{1,0:T(8,128)(2,1)S(1)}, bf16[306,1024]{1,0:T(8,128)(2,1)}, u32[]{:S(2)}) copy-start(bf16[306,1024]{1,0:T(8,128)(2,1)} %refs_3_.1) | copy-start | bytes 1880068
  29.1 1.4 %collective-permute-start.1 = (f32[32,640]{1,0:T(8,128)S(1)}, f32[32,640]{1,0:T(8,128)S(1)}, u32[]{:S(2)}, u32[]{:S(2)}) collective-permute-start(f32[32,640]{1,0:T(8,128)S(1)} %gradients.1), channel_id=1, source_target_pairs={{0,1},{1,0},{2,3},{3,2},{4,5},{5,4},{6,7},{7,6},{8,9},{9,8},{10,11... | collective-permute-start | bytes 245768 | tf_op jit(solution)/shard_map/ppermute | solution.py:159
  30.5 6.2 %collective-permute-start.2 = (f32[32,640]{1,0:T(8,128)S(1)}, f32[32,640]{1,0:T(8,128)S(1)}, u32[]{:S(2)}, u32[]{:S(2)}) collective-permute-start(f32[32,640]{1,0:T(8,128)S(1)} %add.15), channel_id=1, source_target_pairs={{0,2},{1,3},{2,0},{3,1},{4,6},{5,7},{6,4},{7,5},{8,10},{9,11},{10,... | collective-permute-start | bytes 245768 | tf_op jit(solution)/shard_map/ppermute | solution.py:159
  36.8 5.6 %collective-permute-start.3 = (f32[32,640]{1,0:T(8,128)S(1)}, f32[32,640]{1,0:T(8,128)S(1)}, u32[]{:S(2)}, u32[]{:S(2)}) collective-permute-start(f32[32,640]{1,0:T(8,128)S(1)} %add.16), channel_id=1, source_target_pairs={{0,4},{1,5},{2,6},{3,7},{4,0},{5,1},{6,2},{7,3},{8,12},{9,13},{10,... | collective-permute-start | bytes 245768 | tf_op jit(solution)/shard_map/ppermute | solution.py:159
  42.4 5.5 %collective-permute-start.4 = (f32[32,640]{1,0:T(8,128)S(1)}, f32[32,640]{1,0:T(8,128)S(1)}, u32[]{:S(2)}, u32[]{:S(2)}) collective-permute-start(f32[32,640]{1,0:T(8,128)S(1)} %add.17), channel_id=1, source_target_pairs={{0,8},{1,9},{2,10},{3,11},{4,12},{5,13},{6,14},{7,15},{8,0},{9,1},... | collective-permute-start | bytes 245768 | tf_op jit(solution)/shard_map/ppermute | solution.py:159
  47.9 9.4 %collective-permute-start.5 = (f32[32,640]{1,0:T(8,128)S(1)}, f32[32,640]{1,0:T(8,128)S(1)}, u32[]{:S(2)}, u32[]{:S(2)}) collective-permute-start(f32[32,640]{1,0:T(8,128)S(1)} %add.18), channel_id=1, source_target_pairs={{0,16},{1,17},{2,18},{3,19},{4,20},{5,21},{6,22},{7,23},{8,24},{9,... | collective-permute-start | bytes 245768 | tf_op jit(solution)/shard_map/ppermute | solution.py:159

commit v2 on v1

v2 whole, which is shorter than its diff:
```python
import math

import jax
import jax.numpy as jnp
from jax import lax
from jax.experimental import pallas as pl
from jax.experimental.pallas import tpu as pltpu
from jax.sharding import PartitionSpec as P

LANES = 128
HALF = LANES // 2
PARTNERS = (2, 4, 8, 24)
VMEM_BYTES = 16 << 20


def up(n, m):
    return -(-n // m) * m


def lower_band(size):
    rows = lax.broadcasted_iota(jnp.int32, (size, size), 0)
    cols = lax.broadcasted_iota(jnp.int32, (size, size), 1)
    return cols >= rows


def codes_kernel(cv_ref, mask_ref, tail_ref, own_ref):
    atoms, samples = cv_ref.shape
    length = tail_ref.shape[1]
    per = length // LANES
    for b in reversed(range(samples // length)):
        on = mask_ref[:, b : b + 1].astype(jnp.float32)
        block = cv_ref[:, b * length : (b + 1) * length].astype(jnp.float32) * on
        if (b + 1) * length == samples:
            tail_ref[...] = block.astype(jnp.bfloat16)
        for j in range(per):
            at = (per * b + j) * atoms
            own_ref[at : at + atoms, :] = block[:, j * LANES : (j + 1) * LANES]


def course_kernel(
    own_ref, halo_ref, temporal_ref, spatial_ref, send_ref, xs_ref, tf_ref, cs_ref
):
    copies, atoms, width = send_ref.shape
    length = temporal_ref.shape[1]
    channels = spatial_ref.shape[1]
    rows = own_ref.shape[0] // atoms
    samples = rows * LANES
    per = length // LANES
    for j in range(per):
        xs_ref[j * atoms : (j + 1) * atoms, :] = halo_ref[
            :, j * LANES : (j + 1) * LANES
        ].astype(jnp.float32)
    xs_ref[per * atoms :, :] = own_ref[...]
    tf_ref[...] = temporal_ref[...].astype(jnp.float32)
    band = lower_band(LANES)

    def turned(k, at):
        row = tf_ref[k : k + 1, at : at + LANES]
        return pltpu.roll(
            jnp.broadcast_to(row, (LANES, LANES)), 0, 1, stride=1, stride_axis=0
        )

    for k in range(atoms):
        near, far = turned(k, 0), turned(k, LANES)
        matrix = jnp.concatenate(
            [jnp.where(band, 0.0, far), jnp.where(band, far, near), jnp.where(band, near, 0.0)],
            axis=0,
        ).astype(jnp.bfloat16)
        windows = jnp.concatenate(
            [xs_ref[pl.ds(j * atoms + k, rows, stride=atoms), :] for j in range(per + 1)],
            axis=1,
        ).astype(jnp.bfloat16)
        cs_ref[pl.ds(k, rows, stride=atoms), :] = jnp.dot(
            windows, matrix, preferred_element_type=jnp.float32
        )
    padded = jnp.concatenate(
        [spatial_ref[...], jnp.zeros((atoms, width - samples - channels), jnp.bfloat16)],
        axis=1,
    )
    for c in range(copies):
        send_ref[c, :, samples:] = padded
    for i in range(rows):
        part = cs_ref[i * atoms : (i + 1) * atoms, :].astype(jnp.bfloat16)
        for c in range(copies):
            send_ref[c, :, i * LANES : (i + 1) * LANES] = part


def gradient_kernel(
    factor, all_ref, own_ref, xs_ref, signal_ref, mine_ref, other_ref, res_ref, pr_ref, lo_ref, hi_ref, full_ref
):
    groups, atoms, width = all_ref.shape
    channels, samples = signal_ref.shape
    wide = width - samples
    everything = all_ref[...].reshape(groups * atoms, width)
    model = lax.dot_general(
        everything[:, samples:],
        everything[:, :samples],
        (((0,), (0,)), ((), ())),
        preferred_element_type=jnp.float32,
    )
    res_ref[channels:, :] = jnp.zeros((wide - channels, samples), jnp.bfloat16)
    res_ref[:channels, :] = (model[:channels] - signal_ref[...].astype(jnp.float32)).astype(
        jnp.bfloat16
    )
    own = own_ref[0]
    projected = jnp.dot(own[:, samples:], res_ref[...], preferred_element_type=jnp.float32)
    by_channel = factor * lax.dot_general(
        own[:, :samples], res_ref[...], (((1,), (1,)), ((), ())), preferred_element_type=jnp.float32
    )
    rows = samples // LANES
    for i in range(rows):
        pr_ref[i * atoms : (i + 1) * atoms, :] = projected[:, i * LANES : (i + 1) * LANES]
    band = lower_band(LANES)
    for k in range(atoms):
        proj = pr_ref[pl.ds(k, rows, stride=atoms), :].astype(jnp.bfloat16)
        windows = jnp.concatenate(
            [xs_ref[pl.ds(j * atoms + k, rows, stride=atoms), :] for j in range(3)], axis=1
        ).astype(jnp.bfloat16)
        products = lax.dot_general(
            windows, proj, (((0,), (0,)), ((), ())), preferred_element_type=jnp.float32
        )
        old, mid, new = products[:LANES], products[LANES : 2 * LANES], products[2 * LANES :]
        for ref, total in (
            (lo_ref, jnp.where(band, new, mid)),
            (hi_ref, jnp.where(band, mid, old)),
        ):
            parts = [total[:8]]
            for a in range(1, LANES // 8):
                parts.append(pltpu.roll(total[8 * a : 8 * a + 8], LANES - 8 * a, 1))
            while len(parts) > 1:
                parts = [x + y for x, y in zip(parts[::2], parts[1::2], strict=True)]
            ref[8 * k : 8 * k + 8, :] = parts[0]
    row = lax.broadcasted_iota(jnp.int32, (8 * atoms, LANES), 0)
    by_lag = []
    for ref in (lo_ref, hi_ref):
        total = ref[...]
        for bit in (1, 2, 4):
            total = jnp.where((row & bit) != 0, pltpu.roll(total, LANES - bit, 1), total)
        by_lag.append(factor * total.reshape(atoms, 8, LANES).sum(axis=1))
    half = atoms // 2
    lane = lax.broadcasted_iota(jnp.int32, (half // 2, LANES), 1)
    for h in range(2):
        at = h * mine_ref.shape[0]
        tiles = [by_channel[:, :LANES], by_channel[:, LANES : 2 * LANES], *by_lag]
        for t, tile in enumerate(tiles):
            full_ref[at + t * half : at + (t + 1) * half, :] = tile[h * half : (h + 1) * half]
        rest = by_channel[h * half : (h + 1) * half, 2 * LANES :]
        full_ref[at + 4 * half : at + 4 * half + half // 2, :] = jnp.where(
            lane < HALF, rest[: half // 2], pltpu.roll(rest[half // 2 :], HALF, 1)
        )
    size = mine_ref.shape[0]
    core = lax.axis_index("tm") % 2
    mine_ref[...] = full_ref[pl.ds(pl.multiple_of(core * size, 8), size), :]
    other_ref[...] = full_ref[pl.ds(pl.multiple_of((1 - core) * size, 8), size), :]


def outputs_kernel(mine_ref, other_ref, space_ref, time_ref):
    half = space_ref.shape[0] // 2
    channels = space_ref.shape[1]
    core = lax.axis_index("tm") % 2
    for ref, which in ((mine_ref, core), (other_ref, 1 - core)):
        at = pl.multiple_of(which * half, 8)
        tile = [ref[t * half : (t + 1) * half, :] for t in range(4)]
        space_ref[pl.ds(at, half), :LANES] = tile[0]
        space_ref[pl.ds(at, half), LANES : 2 * LANES] = tile[1]
        time_ref[pl.ds(at, half), :LANES] = tile[2]
        time_ref[pl.ds(at, half), LANES:] = tile[3]
        rest = ref[4 * half :, :]
        both = jnp.concatenate([rest, pltpu.roll(rest, HALF, 1)], axis=0)
        space_ref[pl.ds(at, half), 2 * LANES :] = both[:, : channels - 2 * LANES]


def local(signal, spatial, temporal, code_values, block_mask):
    atoms, channels = spatial.shape
    length = temporal.shape[1]
    samples = signal.shape[1]
    groups, slabs = lax.axis_size("atom"), lax.axis_size("tm")
    rows = samples // LANES
    wide = up(channels, LANES)
    factor = 1.0 / math.sqrt(samples * slabs)
    params = pltpu.CompilerParams(vmem_limit_bytes=VMEM_BYTES)

    def swapped(value, bit):
        return lax.ppermute(value, "tm", [(i, i ^ bit) for i in range(slabs)])

    tail, codes = pl.pallas_call(
        codes_kernel,
        out_shape=(
            jax.ShapeDtypeStruct((atoms, length), jnp.bfloat16),
            jax.ShapeDtypeStruct((rows * atoms, LANES), jnp.float32),
        ),
        compiler_params=params,
        name="codes",
    )(code_values, block_mask)
    halo = lax.ppermute(tail, "tm", [(i, i + 1) for i in range(slabs - 1)])
    send, xs = pl.pallas_call(
        course_kernel,
        out_shape=(
            jax.ShapeDtypeStruct((groups, atoms, samples + wide), jnp.bfloat16),
            jax.ShapeDtypeStruct(((rows + length // LANES) * atoms, LANES), jnp.float32),
        ),
        scratch_shapes=[
            pltpu.VMEM((atoms, length), jnp.float32),
            pltpu.VMEM((rows * atoms, LANES), jnp.float32),
        ],
        compiler_params=params,
        name="course",
    )(codes, halo, temporal, spatial)
    everything = lax.all_to_all(send, "atom", split_axis=0, concat_axis=0, tiled=True)
    size = atoms // 2 * 4 + atoms // 4
    share = jax.ShapeDtypeStruct((size, LANES), jnp.float32)
    mine, other = pl.pallas_call(
        lambda *refs: gradient_kernel(factor, *refs),
        out_shape=(share, share),
        scratch_shapes=[
            pltpu.VMEM((wide, samples), jnp.bfloat16),
            pltpu.VMEM((rows * atoms, LANES), jnp.float32),
            pltpu.VMEM((8 * atoms, LANES), jnp.float32),
            pltpu.VMEM((8 * atoms, LANES), jnp.float32),
            pltpu.VMEM((2 * size, LANES), jnp.float32),
        ],
        compiler_params=params,
        name="gradients",
    )(everything, send, xs, signal)
    mine = mine + swapped(other, 1)
    for bit in PARTNERS:
        mine = mine + swapped(mine, bit)
    return pl.pallas_call(
        outputs_kernel,
        out_shape=(
            jax.ShapeDtypeStruct((atoms, channels), jnp.float32),
            jax.ShapeDtypeStruct((atoms, length), jnp.float32),
        ),
        compiler_params=params,
        name="outputs",
    )(mine, swapped(mine, 1))


def solution(mesh):
    in_specs = (P(None, "tm"), P("atom", None), P("atom", None), P("atom", "tm"), P("atom", "tm"))
    out_specs = (P("atom", None), P("atom", None))
    return jax.shard_map(local, mesh=mesh, in_specs=in_specs, out_specs=out_specs, check_vma=False)
```

time: 58.9 us -> 55.6 us (0.944)
  the two profiles are of different devices: /device:TPU:64 before, /device:TPU:1 now
where the time goes in v2:
time: 55.6 us; the launch traced here: 55.4 us
  starting transfers between devices  25.1 us (45%)
  blocking collectives  15.5 us (28%)
  waiting for transfers between devices  8.4 us (15%)
  Pallas kernels  4.1 us (7%)
  local copies, waits for them, and re-layouts  1.62 us (3%)
  between operations  0.68 us (1%)
    ppermute x6, starting transfers between devices, swapped(): return lax.ppermute(value, 'tm', [(i, i ^ bit) for i in range(slabs)])  19 us
    all_to_all x1, blocking collectives, local(): lax.all_to_all(send, 'atom', split_axis=0, concat_axis=0, tiled=True)  15.5 us
    ppermute x6, waiting for transfers between devices, swapped(): return lax.ppermute(value, 'tm', [(i, i ^ bit) for i in range(slabs)])  7.55 us
    ppermute x1, starting transfers between devices, local(): halo = lax.ppermute(tail, 'tm', [(i, i + 1) for i in range(slabs - 1)])  6.04 us
    pallas_call x1, Pallas kernels, local(): pl.pallas_call(lambda *refs: gradient_kernel(factor, *refs), out_shape=(s...  2.52 us
    unnamed x9, local copies, waits for them, and re-layouts  1.62 us
  transfers between devices with their start and end apart: 7, of which 7 were waited for; matrix products, arithmetic and copies ran while one was open for 0% of the time, Pallas kernels for 0%

profile of v2, /device:TPU:1, one launch (start us, length us, event | category | flops | bytes accessed | tf_op | source)
XLA Modules:
  0.0 55.4 jit_solution(13529416651940495097)
XLA Ops:
  0.6 0.8 %copy.7.mask_ref = s32[32,4]{1,0:T(8,128)S(1)} copy(s32[32,4]{0,1:T(4,128)} %param.9) | data formatting | bytes 1024 | tf_op args[4]
  1.4 0.0 copy-start.1
  1.4 0.8 %copy-done.1 = bf16[32,1024]{1,0:T(8,128)(2,1)S(1)} copy-done((bf16[32,1024]{1,0:T(8,128)(2,1)S(1)}, bf16[32,1024]{1,0:T(8,128)(2,1)}, u32[]{:S(2)}) %copy-start.1) | copy-done | bytes 65560
  2.2 0.0 copy-start.2
  2.2 0.0 copy-start.3
  2.2 0.1 codes.1
  2.3 6.0 %collective-permute-start = (bf16[32,256]{1,0:T(8,128)(2,1)S(1)}, bf16[32,256]{1,0:T(8,128)(2,1)S(1)}, u32[]{:S(2)}, u32[]{:S(2)}) collective-permute-start(bf16[32,256]{1,0:T(8,128)(2,1)S(1)} %get-tuple-element.9), channel_id=1, source_target_pairs={{0,1},{1,2},{2,3},{3,4},{4,5},{5,6},{6,7},{7,8},{8,9},{9,10},{10,1... | collective-permute-start | bytes 49160 | tf_op jit(solution)/shard_map/ppermute | solution.py:195
  8.4 0.8 %collective-permute-done.halo_ref = bf16[32,256]{1,0:T(8,128)(2,1)S(1)} collective-permute-done((bf16[32,256]{1,0:T(8,128)(2,1)S(1)}, bf16[32,256]{1,0:T(8,128)(2,1)S(1)}, u32[]{:S(2)}, u32[]{:S(2)}) %collective-permute-start) | collective-permute-done | bytes 16416 | tf_op jit(solution)/shard_map/ppermute | solution.py:195
  9.2 0.0 copy-done.2
  9.2 0.0 copy-done.3
  9.2 0.8 %course.1 = (bf16[8,32,1408]{2,1,0:T(8,128)(2,1)S(1)}, f32[320,128]{1,0:T(8,128)S(1)}) custom-call(f32[256,128]{1,0:T(8,128)S(1)} %get-tuple-element.8.own_ref, bf16[32,256]{1,0:T(8,128)(2,1)S(1)} %collective-permute-done.halo_ref, bf16[32,256]{1,0:T(8,128)(2,1)S(1)} %copy-done.3, bf16[32,306]{1,0:T(8,128)(2,1)S(1)} %copy-done.2), custom_call_target="tpu_custom_call" | custom-call | tf_op jit(solution)/shard_map/course/pallas_call | solution.py:196
  10.0 0.0 copy-start
  10.1 15.5 %all_to_all.5.refs_0_ = bf16[8,32,1408]{2,1,0:T(8,128)(2,1)S(1)} all-to-all(bf16[8,32,1408]{2,1,0:T(8,128)(2,1)S(1)} %get-tuple-element.10.refs_1_), channel_id=1, replica_groups=mesh['atom'=8,'tm'=32] {'atom'}, dimensions={0} | all-to-all | bytes 1441792 | tf_op jit(solution)/shard_map/all_to_all | solution.py:209
  25.5 0.0 copy-done
  25.5 2.5 %gradients.1 = (f32[72,128]{1,0:T(8,128)S(1)}, f32[72,128]{1,0:T(8,128)S(1)}) custom-call(bf16[8,32,1408]{2,1,0:T(8,128)(2,1)S(1)} %all_to_all.5.refs_0_, bf16[8,32,1408]{2,1,0:T(8,128)(2,1)S(1)} %get-tuple-element.10.refs_1_, f32[320,128]{1,0:T(8,128)S(1)} %get-tuple-element.11.refs_2_, bf16[306,1024]{1,0:T(8,128)(2,1)S(1)} %copy-done), custom_call_target="tpu_custom_call" | custom-call | tf_op jit(solution)/shard_map/gradients/pallas_call | solution.py:212
  28.0 0.1 collective-permute-start.1
  28.1 1.2 %collective-permute-done.1 = f32[72,128]{1,0:T(8,128)S(1)} collective-permute-done((f32[72,128]{1,0:T(8,128)S(1)}, f32[72,128]{1,0:T(8,128)S(1)}, u32[]{:S(2)}, u32[]{:S(2)}) %collective-permute-start.1) | collective-permute-done | bytes 36896 | tf_op jit(solution)/shard_map/ppermute | solution.py:184
  29.4 4.6 %collective-permute-start.2 = (f32[72,128]{1,0:T(8,128)S(1)}, f32[72,128]{1,0:T(8,128)S(1)}, u32[]{:S(2)}, u32[]{:S(2)}) collective-permute-start(f32[72,128]{1,0:T(8,128)S(1)} %add.15), channel_id=1, source_target_pairs={{0,2},{1,3},{2,0},{3,1},{4,6},{5,7},{6,4},{7,5},{8,10},{9,11},{10,... | collective-permute-start | bytes 110600 | tf_op jit(solution)/shard_map/ppermute | solution.py:184
  33.9 1.3 %collective-permute-done.2 = f32[72,128]{1,0:T(8,128)S(1)} collective-permute-done((f32[72,128]{1,0:T(8,128)S(1)}, f32[72,128]{1,0:T(8,128)S(1)}, u32[]{:S(2)}, u32[]{:S(2)}) %collective-permute-start.2) | collective-permute-done | bytes 36896 | tf_op jit(solution)/shard_map/ppermute | solution.py:184
  35.3 1.6 %collective-permute-start.3 = (f32[72,128]{1,0:T(8,128)S(1)}, f32[72,128]{1,0:T(8,128)S(1)}, u32[]{:S(2)}, u32[]{:S(2)}) collective-permute-start(f32[72,128]{1,0:T(8,128)S(1)} %add.16), channel_id=1, source_target_pairs={{0,4},{1,5},{2,6},{3,7},{4,0},{5,1},{6,2},{7,3},{8,12},{9,13},{10,... | collective-permute-start | bytes 110600 | tf_op jit(solution)/shard_map/ppermute | solution.py:184
  36.9 1.3 %collective-permute-done.3 = f32[72,128]{1,0:T(8,128)S(1)} collective-permute-done((f32[72,128]{1,0:T(8,128)S(1)}, f32[72,128]{1,0:T(8,128)S(1)}, u32[]{:S(2)}, u32[]{:S(2)}) %collective-permute-start.3) | collective-permute-done | bytes 36896 | tf_op jit(solution)/shard_map/ppermute | solution.py:184
  38.3 4.2 %collective-permute-start.4 = (f32[72,128]{1,0:T(8,128)S(1)}, f32[72,128]{1,0:T(8,128)S(1)}, u32[]{:S(2)}, u32[]{:S(2)}) collective-permute-start(f32[72,128]{1,0:T(8,128)S(1)} %add.17), channel_id=1, source_target_pairs={{0,8},{1,9},{2,10},{3,11},{4,12},{5,13},{6,14},{7,15},{8,0},{9,1},... | collective-permute-start | bytes 110600 | tf_op jit(solution)/shard_map/ppermute | solution.py:184
  42.5 1.3 %collective-permute-done.4 = f32[72,128]{1,0:T(8,128)S(1)} collective-permute-done((f32[72,128]{1,0:T(8,128)S(1)}, f32[72,128]{1,0:T(8,128)S(1)}, u32[]{:S(2)}, u32[]{:S(2)}) %collective-permute-start.4) | collective-permute-done | bytes 36896 | tf_op jit(solution)/shard_map/ppermute | solution.py:184
  43.8 3.9 %collective-permute-start.5 = (f32[72,128]{1,0:T(8,128)S(1)}, f32[72,128]{1,0:T(8,128)S(1)}, u32[]{:S(2)}, u32[]{:S(2)}) collective-permute-start(f32[72,128]{1,0:T(8,128)S(1)} %add.18), channel_id=1, source_target_pairs={{0,24},{1,25},{2,26},{3,27},{4,28},{5,29},{6,30},{7,31},{8,16},{9,... | collective-permute-start | bytes 110600 | tf_op jit(solution)/shard_map/ppermute | solution.py:184
  47.7 1.4 %collective-permute-done.5 = f32[72,128]{1,0:T(8,128)S(1)} collective-permute-done((f32[72,128]{1,0:T(8,128)S(1)}, f32[72,128]{1,0:T(8,128)S(1)}, u32[]{:S(2)}, u32[]{:S(2)}) %collective-permute-start.5) | collective-permute-done | bytes 36896 | tf_op jit(solution)/shard_map/ppermute | solution.py:184
  49.2 4.6 %collective-permute-start.6 = (f32[72,128]{1,0:T(8,128)S(1)}, f32[72,128]{1,0:T(8,128)S(1)}, u32[]{:S(2)}, u32[]{:S(2)}) collective-permute-start(f32[72,128]{1,0:T(8,128)S(1)} %add.19.mine_ref), channel_id=1, source_target_pairs={{0,1},{1,0},{2,3},{3,2},{4,5},{5,4},{6,7},{7,6},{8,9},{9,8},{10,11... | collective-permute-start | bytes 110600 | tf_op jit(solution)/shard_map/ppermute | solution.py:184
  53.8 0.9 %collective-permute-done.6.other_ref = f32[72,128]{1,0:T(8,128)S(1)} collective-permute-done((f32[72,128]{1,0:T(8,128)S(1)}, f32[72,128]{1,0:T(8,128)S(1)}, u32[]{:S(2)}, u32[]{:S(2)}) %collective-permute-start.6) | collective-permute-done | bytes 36896 | tf_op jit(solution)/shard_map/ppermute | solution.py:184
  54.7 0.7 %outputs.1 = (f32[32,306]{1,0:T(8,128)}, f32[32,256]{1,0:T(8,128)}) custom-call(f32[72,128]{1,0:T(8,128)S(1)} %add.19.mine_ref, f32[72,128]{1,0:T(8,128)S(1)} %collective-permute-done.6.other_ref), custom_call_target="tpu_custom_call" | custom-call | tf_op jit(solution)/shard_map/outputs/pallas_call | solution.py:228
  (5 shorter events, 0.0 us)
Async XLA Ops:
  1.4 0.8 %copy-start.1 = (bf16[32,1024]{1,0:T(8,128)(2,1)S(1)}, bf16[32,1024]{1,0:T(8,128)(2,1)}, u32[]{:S(2)}) copy-start(bf16[32,1024]{1,0:T(8,128)(2,1)} %cv_ref.1) | copy-start | bytes 196612
  2.2 7.0 %copy-start.2 = (bf16[32,306]{1,0:T(8,128)(2,1)S(1)}, bf16[32,306]{1,0:T(8,128)(2,1)}, u32[]{:S(2)}) copy-start(bf16[32,306]{1,0:T(8,128)(2,1)} %spatial_ref.1) | copy-start | bytes 58756
  2.2 7.0 %copy-start.3 = (bf16[32,256]{1,0:T(8,128)(2,1)S(1)}, bf16[32,256]{1,0:T(8,128)(2,1)}, u32[]{:S(2)}) copy-start(bf16[32,256]{1,0:T(8,128)(2,1)} %temporal_ref.1) | copy-start | bytes 49156
  2.3 6.9 %collective-permute-start = (bf16[32,256]{1,0:T(8,128)(2,1)S(1)}, bf16[32,256]{1,0:T(8,128)(2,1)S(1)}, u32[]{:S(2)}, u32[]{:S(2)}) collective-permute-start(bf16[32,256]{1,0:T(8,128)(2,1)S(1)} %get-tuple-element.9), channel_id=1, source_target_pairs={{0,1},{1,2},{2,3},{3,4},{4,5},{5,6},{6,7},{7,8},{8,9},{9,10},{10,1... | collective-permute-start | bytes 49160 | tf_op jit(solution)/shard_map/ppermute | solution.py:195
  10.0 15.5 %copy-start = (bf16[306,1024]{1,0:T(8,128)(2,1)S(1)}, bf16[306,1024]{1,0:T(8,128)(2,1)}, u32[]{:S(2)}) copy-start(bf16[306,1024]{1,0:T(8,128)(2,1)} %refs_3_.1) | copy-start | bytes 1880068
  28.0 1.3 %collective-permute-start.1 = (f32[72,128]{1,0:T(8,128)S(1)}, f32[72,128]{1,0:T(8,128)S(1)}, u32[]{:S(2)}, u32[]{:S(2)}) collective-permute-start(f32[72,128]{1,0:T(8,128)S(1)} %get-tuple-element.13), channel_id=1, source_target_pairs={{0,1},{1,0},{2,3},{3,2},{4,5},{5,4},{6,7},{7,6},{8,9},{9,8},{10,11... | collective-permute-start | bytes 110600 | tf_op jit(solution)/shard_map/ppermute | solution.py:184
  29.4 5.9 %collective-permute-start.2 = (f32[72,128]{1,0:T(8,128)S(1)}, f32[72,128]{1,0:T(8,128)S(1)}, u32[]{:S(2)}, u32[]{:S(2)}) collective-permute-start(f32[72,128]{1,0:T(8,128)S(1)} %add.15), channel_id=1, source_target_pairs={{0,2},{1,3},{2,0},{3,1},{4,6},{5,7},{6,4},{7,5},{8,10},{9,11},{10,... | collective-permute-start | bytes 110600 | tf_op jit(solution)/shard_map/ppermute | solution.py:184
  35.3 3.0 %collective-permute-start.3 = (f32[72,128]{1,0:T(8,128)S(1)}, f32[72,128]{1,0:T(8,128)S(1)}, u32[]{:S(2)}, u32[]{:S(2)}) collective-permute-start(f32[72,128]{1,0:T(8,128)S(1)} %add.16), channel_id=1, source_target_pairs={{0,4},{1,5},{2,6},{3,7},{4,0},{5,1},{6,2},{7,3},{8,12},{9,13},{10,... | collective-permute-start | bytes 110600 | tf_op jit(solution)/shard_map/ppermute | solution.py:184
  38.3 5.5 %collective-permute-start.4 = (f32[72,128]{1,0:T(8,128)S(1)}, f32[72,128]{1,0:T(8,128)S(1)}, u32[]{:S(2)}, u32[]{:S(2)}) collective-permute-start(f32[72,128]{1,0:T(8,128)S(1)} %add.17), channel_id=1, source_target_pairs={{0,8},{1,9},{2,10},{3,11},{4,12},{5,13},{6,14},{7,15},{8,0},{9,1},... | collective-permute-start | bytes 110600 | tf_op jit(solution)/shard_map/ppermute | solution.py:184
  43.8 5.3 %collective-permute-start.5 = (f32[72,128]{1,0:T(8,128)S(1)}, f32[72,128]{1,0:T(8,128)S(1)}, u32[]{:S(2)}, u32[]{:S(2)}) collective-permute-start(f32[72,128]{1,0:T(8,128)S(1)} %add.18), channel_id=1, source_target_pairs={{0,24},{1,25},{2,26},{3,27},{4,28},{5,29},{6,30},{7,31},{8,16},{9,... | collective-permute-start | bytes 110600 | tf_op jit(solution)/shard_map/ppermute | solution.py:184
  49.2 5.5 %collective-permute-start.6 = (f32[72,128]{1,0:T(8,128)S(1)}, f32[72,128]{1,0:T(8,128)S(1)}, u32[]{:S(2)}, u32[]{:S(2)}) collective-permute-start(f32[72,128]{1,0:T(8,128)S(1)} %add.19.mine_ref), channel_id=1, source_target_pairs={{0,1},{1,0},{2,3},{3,2},{4,5},{5,4},{6,7},{7,6},{8,9},{9,8},{10,11... | collective-permute-start | bytes 110600 | tf_op jit(solution)/shard_map/ppermute | solution.py:184

commit v3 on v2

--- a/solution.py
+++ b/solution.py
@@ -9,7 +9,7 @@
 
 LANES = 128
 HALF = LANES // 2
-PARTNERS = (2, 4, 8, 24)
+PARTNERS = (2, 4, 8, 28)
 VMEM_BYTES = 16 << 20
 
 
@@ -27,8 +27,11 @@
     atoms, samples = cv_ref.shape
     length = tail_ref.shape[1]
     per = length // LANES
+    down = lax.broadcasted_iota(jnp.int32, (atoms, atoms), 0)
+    along = lax.broadcasted_iota(jnp.int32, (atoms, atoms), 1)
     for b in reversed(range(samples // length)):
-        on = mask_ref[:, b : b + 1].astype(jnp.float32)
+        across = jnp.broadcast_to(mask_ref[b : b + 1, :], (atoms, atoms))
+        on = jnp.sum(jnp.where(down == along, across, 0).astype(jnp.float32), axis=1, keepdims=True)
         block = cv_ref[:, b * length : (b + 1) * length].astype(jnp.float32) * on
         if (b + 1) * length == samples:
             tail_ref[...] = block.astype(jnp.bfloat16)
@@ -86,7 +89,7 @@
 
 
 def gradient_kernel(
-    factor, all_ref, own_ref, xs_ref, signal_ref, mine_ref, other_ref, res_ref, pr_ref, lo_ref, hi_ref, full_ref
+    factor, all_ref, own_ref, xs_ref, signal_ref, mine_ref, other_ref, res_ref, pr_ref, lo_ref, hi_ref, full_ref, turned_ref
 ):
     groups, atoms, width = all_ref.shape
     channels, samples = signal_ref.shape
@@ -111,13 +114,31 @@
     for i in range(rows):
         pr_ref[i * atoms : (i + 1) * atoms, :] = projected[:, i * LANES : (i + 1) * LANES]
     band = lower_band(LANES)
+    group = LANES // rows
     for k in range(atoms):
-        proj = pr_ref[pl.ds(k, rows, stride=atoms), :].astype(jnp.bfloat16)
-        windows = jnp.concatenate(
-            [xs_ref[pl.ds(j * atoms + k, rows, stride=atoms), :] for j in range(3)], axis=1
-        ).astype(jnp.bfloat16)
-        products = lax.dot_general(
-            windows, proj, (((0,), (0,)), ((), ())), preferred_element_type=jnp.float32
+        if k % group == 0:
+            turned = []
+            for j in range(3):
+                stacked = jnp.concatenate(
+                    [
+                        xs_ref[pl.ds(j * atoms + k + g, rows, stride=atoms), :]
+                        for g in range(group)
+                    ],
+                    axis=0,
+                )
+                turned.append(stacked.T.astype(jnp.bfloat16))
+            turned_ref[...] = jnp.concatenate(turned, axis=0)
+        proj = pr_ref[pl.ds(k, rows, stride=atoms), :]
+        above, below = (k % group) * rows, LANES - (k % group + 1) * rows
+        placed = [proj]
+        if above:
+            placed.insert(0, jnp.zeros((above, LANES), jnp.float32))
+        if below:
+            placed.append(jnp.zeros((below, LANES), jnp.float32))
+        products = jnp.dot(
+            turned_ref[...],
+            jnp.concatenate(placed, axis=0).astype(jnp.bfloat16),
+            preferred_element_type=jnp.float32,
         )
         old, mid, new = products[:LANES], products[LANES : 2 * LANES], products[2 * LANES :]
         for ref, total in (
@@ -191,7 +212,7 @@
         ),
         compiler_params=params,
         name="codes",
-    )(code_values, block_mask)
+    )(code_values, block_mask.T)
     halo = lax.ppermute(tail, "tm", [(i, i + 1) for i in range(slabs - 1)])
     send, xs = pl.pallas_call(
         course_kernel,
@@ -218,6 +239,7 @@
             pltpu.VMEM((8 * atoms, LANES), jnp.float32),
             pltpu.VMEM((8 * atoms, LANES), jnp.float32),
             pltpu.VMEM((2 * size, LANES), jnp.float32),
+            pltpu.VMEM(((length // LANES + 1) * LANES, LANES), jnp.bfloat16),
         ],
         compiler_params=params,
         name="gradients",

time: 55.6 us -> 55 us (0.989)
    unnamed x9 -> x10, local copies, waits for them, and re-layouts: 1.62 us -> 1.53 us
where the time goes in v3:
time: 55 us; the launch traced here: 54.6 us
  starting transfers between devices  24.7 us (45%)
  blocking collectives  15.5 us (28%)
  waiting for transfers between devices  8.3 us (15%)
  Pallas kernels  3.81 us (7%)
  local copies, waits for them, and re-layouts  1.53 us (3%)
  between operations  0.69 us (1%)
    ppermute x6, starting transfers between devices, swapped(): return lax.ppermute(value, 'tm', [(i, i ^ bit) for i in range(slabs)])  18.7 us
    all_to_all x1, blocking collectives, local(): lax.all_to_all(send, 'atom', split_axis=0, concat_axis=0, tiled=True)  15.5 us
    ppermute x6, waiting for transfers between devices, swapped(): return lax.ppermute(value, 'tm', [(i, i ^ bit) for i in range(slabs)])  7.45 us
    ppermute x1, starting transfers between devices, local(): halo = lax.ppermute(tail, 'tm', [(i, i + 1) for i in range(slabs - 1)])  6.04 us
    pallas_call x1, Pallas kernels, local(): pl.pallas_call(lambda *refs: gradient_kernel(factor, *refs), out_shape=(s...  2.22 us
    unnamed x10, local copies, waits for them, and re-layouts  1.53 us
  transfers between devices with their start and end apart: 7, of which 7 were waited for; matrix products, arithmetic and copies ran while one was open for 0% of the time, Pallas kernels for 0%

profile of v3, /device:TPU:1, one launch (start us, length us, event | category | flops | bytes accessed | tf_op | source)
XLA Modules:
  0.0 54.6 jit_solution(10562628333012387533)
XLA Ops:
  0.6 0.0 copy-start.1
  0.6 0.8 %copy-done.1 = bf16[32,1024]{1,0:T(8,128)(2,1)S(1)} copy-done((bf16[32,1024]{1,0:T(8,128)(2,1)S(1)}, bf16[32,1024]{1,0:T(8,128)(2,1)}, u32[]{:S(2)}) %copy-start.1) | copy-done | bytes 65560
  1.5 0.0 copy-start.4
  1.5 0.7 %copy-done.4 = s32[32,4]{0,1:T(4,128)S(1)} copy-done((s32[32,4]{0,1:T(4,128)S(1)}, s32[32,4]{0,1:T(4,128)}, u32[]{:S(2)}) %copy-start.4) | copy-done | bytes 536
  2.2 0.0 copy-start.2
  2.2 0.0 copy-start.3
  2.2 0.1 codes.1
  2.3 6.0 %collective-permute-start = (bf16[32,256]{1,0:T(8,128)(2,1)S(1)}, bf16[32,256]{1,0:T(8,128)(2,1)S(1)}, u32[]{:S(2)}, u32[]{:S(2)}) collective-permute-start(bf16[32,256]{1,0:T(8,128)(2,1)S(1)} %get-tuple-element.9), channel_id=1, source_target_pairs={{0,1},{1,2},{2,3},{3,4},{4,5},{5,6},{6,7},{7,8},{8,9},{9,10},{10,1... | collective-permute-start | bytes 49160 | tf_op jit(solution)/shard_map/ppermute | solution.py:216
  8.3 0.8 %collective-permute-done.halo_ref = bf16[32,256]{1,0:T(8,128)(2,1)S(1)} collective-permute-done((bf16[32,256]{1,0:T(8,128)(2,1)S(1)}, bf16[32,256]{1,0:T(8,128)(2,1)S(1)}, u32[]{:S(2)}, u32[]{:S(2)}) %collective-permute-start) | collective-permute-done | bytes 16416 | tf_op jit(solution)/shard_map/ppermute | solution.py:216
  9.2 0.0 copy-done.2
  9.2 0.0 copy-done.3
  9.2 0.8 %course.1 = (bf16[8,32,1408]{2,1,0:T(8,128)(2,1)S(1)}, f32[320,128]{1,0:T(8,128)S(1)}) custom-call(f32[256,128]{1,0:T(8,128)S(1)} %get-tuple-element.8.own_ref, bf16[32,256]{1,0:T(8,128)(2,1)S(1)} %collective-permute-done.halo_ref, bf16[32,256]{1,0:T(8,128)(2,1)S(1)} %copy-done.3, bf16[32,306]{1,0:T(8,128)(2,1)S(1)} %copy-done.2), custom_call_target="tpu_custom_call" | custom-call | tf_op jit(solution)/shard_map/course/pallas_call | solution.py:217
  10.0 0.0 copy-start
  10.0 15.5 %all_to_all.5.refs_0_ = bf16[8,32,1408]{2,1,0:T(8,128)(2,1)S(1)} all-to-all(bf16[8,32,1408]{2,1,0:T(8,128)(2,1)S(1)} %get-tuple-element.10.refs_1_), channel_id=1, replica_groups=mesh['atom'=8,'tm'=32] {'atom'}, dimensions={0} | all-to-all | bytes 1441792 | tf_op jit(solution)/shard_map/all_to_all | solution.py:230
  25.5 0.0 copy-done
  25.5 2.2 %gradients.1 = (f32[72,128]{1,0:T(8,128)S(1)}, f32[72,128]{1,0:T(8,128)S(1)}) custom-call(bf16[8,32,1408]{2,1,0:T(8,128)(2,1)S(1)} %all_to_all.5.refs_0_, bf16[8,32,1408]{2,1,0:T(8,128)(2,1)S(1)} %get-tuple-element.10.refs_1_, f32[320,128]{1,0:T(8,128)S(1)} %get-tuple-element.11.refs_2_, bf16[306,1024]{1,0:T(8,128)(2,1)S(1)} %copy-done), custom_call_target="tpu_custom_call" | custom-call | tf_op jit(solution)/shard_map/gradients/pallas_call | solution.py:233
  27.7 0.1 collective-permute-start.1
  27.8 1.2 %collective-permute-done.1 = f32[72,128]{1,0:T(8,128)S(1)} collective-permute-done((f32[72,128]{1,0:T(8,128)S(1)}, f32[72,128]{1,0:T(8,128)S(1)}, u32[]{:S(2)}, u32[]{:S(2)}) %collective-permute-start.1) | collective-permute-done | bytes 36896 | tf_op jit(solution)/shard_map/ppermute | solution.py:205
  29.0 4.6 %collective-permute-start.2 = (f32[72,128]{1,0:T(8,128)S(1)}, f32[72,128]{1,0:T(8,128)S(1)}, u32[]{:S(2)}, u32[]{:S(2)}) collective-permute-start(f32[72,128]{1,0:T(8,128)S(1)} %add.15), channel_id=1, source_target_pairs={{0,2},{1,3},{2,0},{3,1},{4,6},{5,7},{6,4},{7,5},{8,10},{9,11},{10,... | collective-permute-start | bytes 110600 | tf_op jit(solution)/shard_map/ppermute | solution.py:205
  33.5 1.3 %collective-permute-done.2 = f32[72,128]{1,0:T(8,128)S(1)} collective-permute-done((f32[72,128]{1,0:T(8,128)S(1)}, f32[72,128]{1,0:T(8,128)S(1)}, u32[]{:S(2)}, u32[]{:S(2)}) %collective-permute-start.2) | collective-permute-done | bytes 36896 | tf_op jit(solution)/shard_map/ppermute | solution.py:205
  34.9 1.6 %collective-permute-start.3 = (f32[72,128]{1,0:T(8,128)S(1)}, f32[72,128]{1,0:T(8,128)S(1)}, u32[]{:S(2)}, u32[]{:S(2)}) collective-permute-start(f32[72,128]{1,0:T(8,128)S(1)} %add.16), channel_id=1, source_target_pairs={{0,4},{1,5},{2,6},{3,7},{4,0},{5,1},{6,2},{7,3},{8,12},{9,13},{10,... | collective-permute-start | bytes 110600 | tf_op jit(solution)/shard_map/ppermute | solution.py:205
  36.5 1.3 %collective-permute-done.3 = f32[72,128]{1,0:T(8,128)S(1)} collective-permute-done((f32[72,128]{1,0:T(8,128)S(1)}, f32[72,128]{1,0:T(8,128)S(1)}, u32[]{:S(2)}, u32[]{:S(2)}) %collective-permute-start.3) | collective-permute-done | bytes 36896 | tf_op jit(solution)/shard_map/ppermute | solution.py:205
  37.9 4.2 %collective-permute-start.4 = (f32[72,128]{1,0:T(8,128)S(1)}, f32[72,128]{1,0:T(8,128)S(1)}, u32[]{:S(2)}, u32[]{:S(2)}) collective-permute-start(f32[72,128]{1,0:T(8,128)S(1)} %add.17), channel_id=1, source_target_pairs={{0,8},{1,9},{2,10},{3,11},{4,12},{5,13},{6,14},{7,15},{8,0},{9,1},... | collective-permute-start | bytes 110600 | tf_op jit(solution)/shard_map/ppermute | solution.py:205
  42.1 1.3 %collective-permute-done.4 = f32[72,128]{1,0:T(8,128)S(1)} collective-permute-done((f32[72,128]{1,0:T(8,128)S(1)}, f32[72,128]{1,0:T(8,128)S(1)}, u32[]{:S(2)}, u32[]{:S(2)}) %collective-permute-start.4) | collective-permute-done | bytes 36896 | tf_op jit(solution)/shard_map/ppermute | solution.py:205
  43.4 3.4 %collective-permute-start.5 = (f32[72,128]{1,0:T(8,128)S(1)}, f32[72,128]{1,0:T(8,128)S(1)}, u32[]{:S(2)}, u32[]{:S(2)}) collective-permute-start(f32[72,128]{1,0:T(8,128)S(1)} %add.18), channel_id=1, source_target_pairs={{0,28},{1,29},{2,30},{3,31},{4,24},{5,25},{6,26},{7,27},{8,20},{9,... | collective-permute-start | bytes 110600 | tf_op jit(solution)/shard_map/ppermute | solution.py:205
  46.9 1.3 %collective-permute-done.5 = f32[72,128]{1,0:T(8,128)S(1)} collective-permute-done((f32[72,128]{1,0:T(8,128)S(1)}, f32[72,128]{1,0:T(8,128)S(1)}, u32[]{:S(2)}, u32[]{:S(2)}) %collective-permute-start.5) | collective-permute-done | bytes 36896 | tf_op jit(solution)/shard_map/ppermute | solution.py:205
  48.2 4.8 %collective-permute-start.6 = (f32[72,128]{1,0:T(8,128)S(1)}, f32[72,128]{1,0:T(8,128)S(1)}, u32[]{:S(2)}, u32[]{:S(2)}) collective-permute-start(f32[72,128]{1,0:T(8,128)S(1)} %add.19.mine_ref), channel_id=1, source_target_pairs={{0,1},{1,0},{2,3},{3,2},{4,5},{5,4},{6,7},{7,6},{8,9},{9,8},{10,11... | collective-permute-start | bytes 110600 | tf_op jit(solution)/shard_map/ppermute | solution.py:205
  53.0 0.9 %collective-permute-done.6.other_ref = f32[72,128]{1,0:T(8,128)S(1)} collective-permute-done((f32[72,128]{1,0:T(8,128)S(1)}, f32[72,128]{1,0:T(8,128)S(1)}, u32[]{:S(2)}, u32[]{:S(2)}) %collective-permute-start.6) | collective-permute-done | bytes 36896 | tf_op jit(solution)/shard_map/ppermute | solution.py:205
  53.9 0.7 %outputs.1 = (f32[32,306]{1,0:T(8,128)}, f32[32,256]{1,0:T(8,128)}) custom-call(f32[72,128]{1,0:T(8,128)S(1)} %add.19.mine_ref, f32[72,128]{1,0:T(8,128)S(1)} %collective-permute-done.6.other_ref), custom_call_target="tpu_custom_call" | custom-call | tf_op jit(solution)/shard_map/outputs/pallas_call | solution.py:250
  (5 shorter events, 0.0 us)
Async XLA Ops:
  0.6 0.8 %copy-start.1 = (bf16[32,1024]{1,0:T(8,128)(2,1)S(1)}, bf16[32,1024]{1,0:T(8,128)(2,1)}, u32[]{:S(2)}) copy-start(bf16[32,1024]{1,0:T(8,128)(2,1)} %cv_ref.1) | copy-start | bytes 196612
  1.5 0.7 %copy-start.4 = (s32[32,4]{0,1:T(4,128)S(1)}, s32[32,4]{0,1:T(4,128)}, u32[]{:S(2)}) copy-start(s32[32,4]{0,1:T(4,128)} %param.9) | copy-start | bytes 1540
  2.2 7.0 %copy-start.2 = (bf16[32,306]{1,0:T(8,128)(2,1)S(1)}, bf16[32,306]{1,0:T(8,128)(2,1)}, u32[]{:S(2)}) copy-start(bf16[32,306]{1,0:T(8,128)(2,1)} %spatial_ref.1) | copy-start | bytes 58756
  2.2 7.0 %copy-start.3 = (bf16[32,256]{1,0:T(8,128)(2,1)S(1)}, bf16[32,256]{1,0:T(8,128)(2,1)}, u32[]{:S(2)}) copy-start(bf16[32,256]{1,0:T(8,128)(2,1)} %temporal_ref.1) | copy-start | bytes 49156
  2.3 6.9 %collective-permute-start = (bf16[32,256]{1,0:T(8,128)(2,1)S(1)}, bf16[32,256]{1,0:T(8,128)(2,1)S(1)}, u32[]{:S(2)}, u32[]{:S(2)}) collective-permute-start(bf16[32,256]{1,0:T(8,128)(2,1)S(1)} %get-tuple-element.9), channel_id=1, source_target_pairs={{0,1},{1,2},{2,3},{3,4},{4,5},{5,6},{6,7},{7,8},{8,9},{9,10},{10,1... | collective-permute-start | bytes 49160 | tf_op jit(solution)/shard_map/ppermute | solution.py:216
  10.0 15.5 %copy-start = (bf16[306,1024]{1,0:T(8,128)(2,1)S(1)}, bf16[306,1024]{1,0:T(8,128)(2,1)}, u32[]{:S(2)}) copy-start(bf16[306,1024]{1,0:T(8,128)(2,1)} %refs_3_.1) | copy-start | bytes 1880068
  27.7 1.3 %collective-permute-start.1 = (f32[72,128]{1,0:T(8,128)S(1)}, f32[72,128]{1,0:T(8,128)S(1)}, u32[]{:S(2)}, u32[]{:S(2)}) collective-permute-start(f32[72,128]{1,0:T(8,128)S(1)} %get-tuple-element.13), channel_id=1, source_target_pairs={{0,1},{1,0},{2,3},{3,2},{4,5},{5,4},{6,7},{7,6},{8,9},{9,8},{10,11... | collective-permute-start | bytes 110600 | tf_op jit(solution)/shard_map/ppermute | solution.py:205
  29.0 5.9 %collective-permute-start.2 = (f32[72,128]{1,0:T(8,128)S(1)}, f32[72,128]{1,0:T(8,128)S(1)}, u32[]{:S(2)}, u32[]{:S(2)}) collective-permute-start(f32[72,128]{1,0:T(8,128)S(1)} %add.15), channel_id=1, source_target_pairs={{0,2},{1,3},{2,0},{3,1},{4,6},{5,7},{6,4},{7,5},{8,10},{9,11},{10,... | collective-permute-start | bytes 110600 | tf_op jit(solution)/shard_map/ppermute | solution.py:205
  34.9 3.0 %collective-permute-start.3 = (f32[72,128]{1,0:T(8,128)S(1)}, f32[72,128]{1,0:T(8,128)S(1)}, u32[]{:S(2)}, u32[]{:S(2)}) collective-permute-start(f32[72,128]{1,0:T(8,128)S(1)} %add.16), channel_id=1, source_target_pairs={{0,4},{1,5},{2,6},{3,7},{4,0},{5,1},{6,2},{7,3},{8,12},{9,13},{10,... | collective-permute-start | bytes 110600 | tf_op jit(solution)/shard_map/ppermute | solution.py:205
  37.9 5.5 %collective-permute-start.4 = (f32[72,128]{1,0:T(8,128)S(1)}, f32[72,128]{1,0:T(8,128)S(1)}, u32[]{:S(2)}, u32[]{:S(2)}) collective-permute-start(f32[72,128]{1,0:T(8,128)S(1)} %add.17), channel_id=1, source_target_pairs={{0,8},{1,9},{2,10},{3,11},{4,12},{5,13},{6,14},{7,15},{8,0},{9,1},... | collective-permute-start | bytes 110600 | tf_op jit(solution)/shard_map/ppermute | solution.py:205
  43.4 4.8 %collective-permute-start.5 = (f32[72,128]{1,0:T(8,128)S(1)}, f32[72,128]{1,0:T(8,128)S(1)}, u32[]{:S(2)}, u32[]{:S(2)}) collective-permute-start(f32[72,128]{1,0:T(8,128)S(1)} %add.18), channel_id=1, source_target_pairs={{0,28},{1,29},{2,30},{3,31},{4,24},{5,25},{6,26},{7,27},{8,20},{9,... | collective-permute-start | bytes 110600 | tf_op jit(solution)/shard_map/ppermute | solution.py:205
  48.2 5.6 %collective-permute-start.6 = (f32[72,128]{1,0:T(8,128)S(1)}, f32[72,128]{1,0:T(8,128)S(1)}, u32[]{:S(2)}, u32[]{:S(2)}) collective-permute-start(f32[72,128]{1,0:T(8,128)S(1)} %add.19.mine_ref), channel_id=1, source_target_pairs={{0,1},{1,0},{2,3},{3,2},{4,5},{5,4},{6,7},{7,6},{8,9},{9,8},{10,11... | collective-permute-start | bytes 110600 | tf_op jit(solution)/shard_map/ppermute | solution.py:205

commit v4 on v3

--- a/solution.py
+++ b/solution.py
@@ -88,49 +88,30 @@
             send_ref[c, :, i * LANES : (i + 1) * LANES] = part
 
 
-def gradient_kernel(
-    factor, all_ref, own_ref, xs_ref, signal_ref, mine_ref, other_ref, res_ref, pr_ref, lo_ref, hi_ref, full_ref, turned_ref
-):
-    groups, atoms, width = all_ref.shape
-    channels, samples = signal_ref.shape
-    wide = width - samples
-    everything = all_ref[...].reshape(groups * atoms, width)
-    model = lax.dot_general(
-        everything[:, samples:],
-        everything[:, :samples],
-        (((0,), (0,)), ((), ())),
-        preferred_element_type=jnp.float32,
-    )
-    res_ref[channels:, :] = jnp.zeros((wide - channels, samples), jnp.bfloat16)
-    res_ref[:channels, :] = (model[:channels] - signal_ref[...].astype(jnp.float32)).astype(
-        jnp.bfloat16
-    )
-    own = own_ref[0]
-    projected = jnp.dot(own[:, samples:], res_ref[...], preferred_element_type=jnp.float32)
-    by_channel = factor * lax.dot_general(
-        own[:, :samples], res_ref[...], (((1,), (1,)), ((), ())), preferred_element_type=jnp.float32
-    )
-    rows = samples // LANES
+def half_of(out_ref, core, space_ref, xs_ref, pr_ref, xh_ref, ph_ref, lo_ref, hi_ref, turned_ref, factor):
+    atoms = space_ref.shape[0]
+    half = atoms // 2
+    rows, blocks = pr_ref.shape[0] // atoms, xs_ref.shape[0] // atoms
+    for e in range(blocks):
+        at = pl.multiple_of(e * atoms + core * half, half)
+        xh_ref[e * half : (e + 1) * half, :] = xs_ref[pl.ds(at, half), :]
     for i in range(rows):
-        pr_ref[i * atoms : (i + 1) * atoms, :] = projected[:, i * LANES : (i + 1) * LANES]
+        at = pl.multiple_of(i * atoms + core * half, half)
+        ph_ref[i * half : (i + 1) * half, :] = pr_ref[pl.ds(at, half), :]
+    group = LANES // rows
     band = lower_band(LANES)
-    group = LANES // rows
-    for k in range(atoms):
+    for k in range(half):
         if k % group == 0:
             turned = []
             for j in range(3):
                 stacked = jnp.concatenate(
-                    [
-                        xs_ref[pl.ds(j * atoms + k + g, rows, stride=atoms), :]
-                        for g in range(group)
-                    ],
+                    [xh_ref[pl.ds(j * half + k + g, rows, stride=half), :] for g in range(group)],
                     axis=0,
                 )
                 turned.append(stacked.T.astype(jnp.bfloat16))
             turned_ref[...] = jnp.concatenate(turned, axis=0)
-        proj = pr_ref[pl.ds(k, rows, stride=atoms), :]
         above, below = (k % group) * rows, LANES - (k % group + 1) * rows
-        placed = [proj]
+        placed = [ph_ref[pl.ds(k, rows, stride=half), :]]
         if above:
             placed.insert(0, jnp.zeros((above, LANES), jnp.float32))
         if below:
@@ -151,28 +132,54 @@
             while len(parts) > 1:
                 parts = [x + y for x, y in zip(parts[::2], parts[1::2], strict=True)]
             ref[8 * k : 8 * k + 8, :] = parts[0]
-    row = lax.broadcasted_iota(jnp.int32, (8 * atoms, LANES), 0)
-    by_lag = []
+    row = lax.broadcasted_iota(jnp.int32, (8 * half, LANES), 0)
+    start = pl.multiple_of(core * half, half)
+    tiles = [space_ref[pl.ds(start, half), :LANES], space_ref[pl.ds(start, half), LANES : 2 * LANES]]
     for ref in (lo_ref, hi_ref):
         total = ref[...]
         for bit in (1, 2, 4):
             total = jnp.where((row & bit) != 0, pltpu.roll(total, LANES - bit, 1), total)
-        by_lag.append(factor * total.reshape(atoms, 8, LANES).sum(axis=1))
-    half = atoms // 2
+        tiles.append(factor * total.reshape(half, 8, LANES).sum(axis=1))
+    for t, tile in enumerate(tiles):
+        out_ref[t * half : (t + 1) * half, :] = tile
     lane = lax.broadcasted_iota(jnp.int32, (half // 2, LANES), 1)
-    for h in range(2):
-        at = h * mine_ref.shape[0]
-        tiles = [by_channel[:, :LANES], by_channel[:, LANES : 2 * LANES], *by_lag]
-        for t, tile in enumerate(tiles):
-            full_ref[at + t * half : at + (t + 1) * half, :] = tile[h * half : (h + 1) * half]
-        rest = by_channel[h * half : (h + 1) * half, 2 * LANES :]
-        full_ref[at + 4 * half : at + 4 * half + half // 2, :] = jnp.where(
-            lane < HALF, rest[: half // 2], pltpu.roll(rest[half // 2 :], HALF, 1)
-        )
-    size = mine_ref.shape[0]
+    rest = space_ref[pl.ds(start, half), 2 * LANES :]
+    out_ref[4 * half :, :] = jnp.where(
+        lane < HALF, rest[: half // 2], pltpu.roll(rest[half // 2 :], HALF, 1)
+    )
+
+
+def other_half_kernel(
+    factor, all_ref, own_ref, xs_ref, signal_ref, other_ref, space_ref, pr_ref, res_ref, *scratch
+):
+    groups, atoms, width = all_ref.shape
+    channels, samples = signal_ref.shape
+    wide = width - samples
+    everything = all_ref[...].reshape(groups * atoms, width)
+    model = lax.dot_general(
+        everything[:, samples:],
+        everything[:, :samples],
+        (((0,), (0,)), ((), ())),
+        preferred_element_type=jnp.float32,
+    )
+    res_ref[channels:, :] = jnp.zeros((wide - channels, samples), jnp.bfloat16)
+    res_ref[:channels, :] = (model[:channels] - signal_ref[...].astype(jnp.float32)).astype(
+        jnp.bfloat16
+    )
+    own = own_ref[0]
+    projected = jnp.dot(own[:, samples:], res_ref[...], preferred_element_type=jnp.float32)
+    for i in range(samples // LANES):
+        pr_ref[i * atoms : (i + 1) * atoms, :] = projected[:, i * LANES : (i + 1) * LANES]
+    space_ref[...] = factor * lax.dot_general(
+        own[:, :samples], res_ref[...], (((1,), (1,)), ((), ())), preferred_element_type=jnp.float32
+    )
     core = lax.axis_index("tm") % 2
-    mine_ref[...] = full_ref[pl.ds(pl.multiple_of(core * size, 8), size), :]
-    other_ref[...] = full_ref[pl.ds(pl.multiple_of((1 - core) * size, 8), size), :]
+    half_of(other_ref, 1 - core, space_ref, xs_ref, pr_ref, *scratch, factor)
+
+
+def own_half_kernel(factor, space_ref, xs_ref, pr_ref, mine_ref, *scratch):
+    core = lax.axis_index("tm") % 2
+    half_of(mine_ref, core, space_ref, xs_ref, pr_ref, *scratch, factor)
 
 
 def outputs_kernel(mine_ref, other_ref, space_ref, time_ref):
@@ -229,21 +236,34 @@
     )(codes, halo, temporal, spatial)
     everything = lax.all_to_all(send, "atom", split_axis=0, concat_axis=0, tiled=True)
     size = atoms // 2 * 4 + atoms // 4
+    half, per = atoms // 2, length // LANES
     share = jax.ShapeDtypeStruct((size, LANES), jnp.float32)
-    mine, other = pl.pallas_call(
-        lambda *refs: gradient_kernel(factor, *refs),
-        out_shape=(share, share),
-        scratch_shapes=[
-            pltpu.VMEM((wide, samples), jnp.bfloat16),
-            pltpu.VMEM((rows * atoms, LANES), jnp.float32),
-            pltpu.VMEM((8 * atoms, LANES), jnp.float32),
-            pltpu.VMEM((8 * atoms, LANES), jnp.float32),
-            pltpu.VMEM((2 * size, LANES), jnp.float32),
-            pltpu.VMEM(((length // LANES + 1) * LANES, LANES), jnp.bfloat16),
-        ],
-        compiler_params=params,
-        name="gradients",
+    scratch = [
+        pltpu.VMEM(((rows + per) * half, LANES), jnp.float32),
+        pltpu.VMEM((rows * half, LANES), jnp.float32),
+        pltpu.VMEM((8 * half, LANES), jnp.float32),
+        pltpu.VMEM((8 * half, LANES), jnp.float32),
+        pltpu.VMEM(((per + 1) * LANES, LANES), jnp.bfloat16),
+    ]
+    other, space, projected = pl.pallas_call(
+        lambda *refs: other_half_kernel(factor, *refs),
+        out_shape=(
+            share,
+            jax.ShapeDtypeStruct((atoms, wide), jnp.float32),
+            jax.ShapeDtypeStruct((rows * atoms, LANES), jnp.float32),
+        ),
+        scratch_shapes=[pltpu.VMEM((wide, samples), jnp.bfloat16), *scratch],
+        compiler_params=params,
+        name="other_half",
     )(everything, send, xs, signal)
+    mine = pl.pallas_call(
+        lambda *refs: own_half_kernel(factor, *refs),
+        out_shape=share,
+        scratch_shapes=scratch,
+        compiler_params=params,
+        cost_estimate=pl.CostEstimate(flops=200_000_000, bytes_accessed=1_000_000, transcendentals=0),
+        name="own_half",
+    )(space, xs, projected)
     mine = mine + swapped(other, 1)
     for bit in PARTNERS:
         mine = mine + swapped(mine, bit)

time: 55 us -> 54.4 us (0.989)
  starting transfers between devices: 24.7 us -> 24 us
    ppermute x6, starting transfers between devices: 18.7 us -> 17.9 us  [swapped(): return lax.ppermute(value, 'tm', [(i, i ^ bit) for i in range(slabs)])]
    pallas_call x1 -> x2, Pallas kernels: 2.22 us -> 2.66 us  [the longest x1 1.58 us: local(): pl.pallas_call(lambda *refs: other_half_kernel(factor, *refs), out_shape=...]
  transfers between devices with their start and end apart: 7 -> 7, of which waited for: 7 -> 7; matrix products, arithmetic and copies ran while one was open for 0% -> 0% of each run, Pallas kernels for 0% -> 2%
where the time goes in v4:
time: 54.4 us; the launch traced here: 53.9 us
  starting transfers between devices  24 us (44%)
  blocking collectives  15.5 us (28%)
  waiting for transfers between devices  7.91 us (15%)
  Pallas kernels  4.26 us (8%)
  local copies, waits for them, and re-layouts  1.53 us (3%)
  between operations  0.69 us (1%)
    ppermute x6, starting transfers between devices, swapped(): return lax.ppermute(value, 'tm', [(i, i ^ bit) for i in range(slabs)])  17.9 us
    all_to_all x1, blocking collectives, local(): lax.all_to_all(send, 'atom', split_axis=0, concat_axis=0, tiled=True)  15.5 us
    ppermute x6, waiting for transfers between devices, swapped(): return lax.ppermute(value, 'tm', [(i, i ^ bit) for i in range(slabs)])  7.06 us
    ppermute x1, starting transfers between devices, local(): halo = lax.ppermute(tail, 'tm', [(i, i + 1) for i in range(slabs - 1)])  6.04 us
    pallas_call x1, Pallas kernels, local(): pl.pallas_call(lambda *refs: other_half_kernel(factor, *refs), out_shape=...  1.58 us
    unnamed x10, local copies, waits for them, and re-layouts  1.53 us
  transfers between devices with their start and end apart: 7, of which 7 were waited for; matrix products, arithmetic and copies ran while one was open for 0% of the time, Pallas kernels for 2%

profile of v4, /device:TPU:1, one launch (start us, length us, event | category | flops | bytes accessed | tf_op | source)
XLA Modules:
  0.0 53.9 jit_solution(12120120657904509629)
XLA Ops:
  0.6 0.0 copy-start.1
  0.6 0.8 %copy-done.1 = bf16[32,1024]{1,0:T(8,128)(2,1)S(1)} copy-done((bf16[32,1024]{1,0:T(8,128)(2,1)S(1)}, bf16[32,1024]{1,0:T(8,128)(2,1)}, u32[]{:S(2)}) %copy-start.1) | copy-done | bytes 65560
  1.5 0.0 copy-start.4
  1.5 0.7 %copy-done.4 = s32[32,4]{0,1:T(4,128)S(1)} copy-done((s32[32,4]{0,1:T(4,128)S(1)}, s32[32,4]{0,1:T(4,128)}, u32[]{:S(2)}) %copy-start.4) | copy-done | bytes 536
  2.2 0.0 copy-start.2
  2.2 0.0 copy-start.3
  2.2 0.1 codes.1
  2.3 6.0 %collective-permute-start = (bf16[32,256]{1,0:T(8,128)(2,1)S(1)}, bf16[32,256]{1,0:T(8,128)(2,1)S(1)}, u32[]{:S(2)}, u32[]{:S(2)}) collective-permute-start(bf16[32,256]{1,0:T(8,128)(2,1)S(1)} %get-tuple-element.10), channel_id=1, source_target_pairs={{0,1},{1,2},{2,3},{3,4},{4,5},{5,6},{6,7},{7,8},{8,9},{9,10},{10,1... | collective-permute-start | bytes 49160 | tf_op jit(solution)/shard_map/ppermute | solution.py:223
  8.3 0.8 %collective-permute-done.halo_ref = bf16[32,256]{1,0:T(8,128)(2,1)S(1)} collective-permute-done((bf16[32,256]{1,0:T(8,128)(2,1)S(1)}, bf16[32,256]{1,0:T(8,128)(2,1)S(1)}, u32[]{:S(2)}, u32[]{:S(2)}) %collective-permute-start) | collective-permute-done | bytes 16416 | tf_op jit(solution)/shard_map/ppermute | solution.py:223
  9.2 0.0 copy-done.2
  9.2 0.0 copy-done.3
  9.2 0.8 %course.1 = (bf16[8,32,1408]{2,1,0:T(8,128)(2,1)S(1)}, f32[320,128]{1,0:T(8,128)S(1)}) custom-call(f32[256,128]{1,0:T(8,128)S(1)} %get-tuple-element.9.own_ref, bf16[32,256]{1,0:T(8,128)(2,1)S(1)} %collective-permute-done.halo_ref, bf16[32,256]{1,0:T(8,128)(2,1)S(1)} %copy-done.3, bf16[32,306]{1,0:T(8,128)(2,1)S(1)} %copy-done.2), custom_call_target="tpu_custom_call" | custom-call | tf_op jit(solution)/shard_map/course/pallas_call | solution.py:224
  10.0 0.0 copy-start
  10.0 15.5 %all_to_all.5.refs_0_ = bf16[8,32,1408]{2,1,0:T(8,128)(2,1)S(1)} all-to-all(bf16[8,32,1408]{2,1,0:T(8,128)(2,1)S(1)} %get-tuple-element.11.refs_1_), channel_id=1, replica_groups=mesh['atom'=8,'tm'=32] {'atom'}, dimensions={0} | all-to-all | bytes 1441792 | tf_op jit(solution)/shard_map/all_to_all | solution.py:237
  25.5 0.0 copy-done
  25.5 1.6 %other_half.1 = (f32[72,128]{1,0:T(8,128)S(1)}, f32[32,384]{1,0:T(8,128)S(1)}, f32[256,128]{1,0:T(8,128)S(1)}) custom-call(bf16[8,32,1408]{2,1,0:T(8,128)(2,1)S(1)} %all_to_all.5.refs_0_, bf16[8,32,1408]{2,1,0:T(8,128)(2,1)S(1)} %get-tuple-element.11.refs_1_, f32[320,128]{1,0:T(8,128)S(1)} %get-tuple-element.12.refs_2_.refs_1_, bf16[306,1024]{1,0:T(8,128)(2,1)S(1)} %copy-done), custom_call_target="tpu_custom_call" | custom-call | tf_op jit(solution)/shard_map/other_half/pallas_call | solution.py:248
  27.0 0.1 collective-permute-start.1
  27.1 1.1 %own_half.1 = f32[72,128]{1,0:T(8,128)S(1)} custom-call(f32[32,384]{1,0:T(8,128)S(1)} %get-tuple-element.13.refs_0_, f32[320,128]{1,0:T(8,128)S(1)} %get-tuple-element.12.refs_2_.refs_1_, f32[256,128]{1,0:T(8,128)S(1)} %get-tuple-element.14.refs_2_), custom_call_target="tpu_custom_call" | custom-call | flops 200000000 | bytes 1000000 | tf_op jit(solution)/shard_map/own_half/pallas_call | solution.py:259
  28.2 0.1 collective-permute-done.1
  28.3 4.9 %collective-permute-start.2 = (f32[72,128]{1,0:T(8,128)S(1)}, f32[72,128]{1,0:T(8,128)S(1)}, u32[]{:S(2)}, u32[]{:S(2)}) collective-permute-start(f32[72,128]{1,0:T(8,128)S(1)} %add.15), channel_id=1, source_target_pairs={{0,2},{1,3},{2,0},{3,1},{4,6},{5,7},{6,4},{7,5},{8,10},{9,11},{10,... | collective-permute-start | bytes 110600 | tf_op jit(solution)/shard_map/ppermute | solution.py:212
  33.2 1.8 %collective-permute-done.2 = f32[72,128]{1,0:T(8,128)S(1)} collective-permute-done((f32[72,128]{1,0:T(8,128)S(1)}, f32[72,128]{1,0:T(8,128)S(1)}, u32[]{:S(2)}, u32[]{:S(2)}) %collective-permute-start.2) | collective-permute-done | bytes 36896 | tf_op jit(solution)/shard_map/ppermute | solution.py:212
  35.0 1.2 %collective-permute-start.3 = (f32[72,128]{1,0:T(8,128)S(1)}, f32[72,128]{1,0:T(8,128)S(1)}, u32[]{:S(2)}, u32[]{:S(2)}) collective-permute-start(f32[72,128]{1,0:T(8,128)S(1)} %add.16), channel_id=1, source_target_pairs={{0,4},{1,5},{2,6},{3,7},{4,0},{5,1},{6,2},{7,3},{8,12},{9,13},{10,... | collective-permute-start | bytes 110600 | tf_op jit(solution)/shard_map/ppermute | solution.py:212
  36.2 1.6 %collective-permute-done.3 = f32[72,128]{1,0:T(8,128)S(1)} collective-permute-done((f32[72,128]{1,0:T(8,128)S(1)}, f32[72,128]{1,0:T(8,128)S(1)}, u32[]{:S(2)}, u32[]{:S(2)}) %collective-permute-start.3) | collective-permute-done | bytes 36896 | tf_op jit(solution)/shard_map/ppermute | solution.py:212
  37.8 4.4 %collective-permute-start.4 = (f32[72,128]{1,0:T(8,128)S(1)}, f32[72,128]{1,0:T(8,128)S(1)}, u32[]{:S(2)}, u32[]{:S(2)}) collective-permute-start(f32[72,128]{1,0:T(8,128)S(1)} %add.17), channel_id=1, source_target_pairs={{0,8},{1,9},{2,10},{3,11},{4,12},{5,13},{6,14},{7,15},{8,0},{9,1},... | collective-permute-start | bytes 110600 | tf_op jit(solution)/shard_map/ppermute | solution.py:212
  42.2 1.3 %collective-permute-done.4 = f32[72,128]{1,0:T(8,128)S(1)} collective-permute-done((f32[72,128]{1,0:T(8,128)S(1)}, f32[72,128]{1,0:T(8,128)S(1)}, u32[]{:S(2)}, u32[]{:S(2)}) %collective-permute-start.4) | collective-permute-done | bytes 36896 | tf_op jit(solution)/shard_map/ppermute | solution.py:212
  43.5 3.0 %collective-permute-start.5 = (f32[72,128]{1,0:T(8,128)S(1)}, f32[72,128]{1,0:T(8,128)S(1)}, u32[]{:S(2)}, u32[]{:S(2)}) collective-permute-start(f32[72,128]{1,0:T(8,128)S(1)} %add.18), channel_id=1, source_target_pairs={{0,28},{1,29},{2,30},{3,31},{4,24},{5,25},{6,26},{7,27},{8,20},{9,... | collective-permute-start | bytes 110600 | tf_op jit(solution)/shard_map/ppermute | solution.py:212
  46.6 1.3 %collective-permute-done.5 = f32[72,128]{1,0:T(8,128)S(1)} collective-permute-done((f32[72,128]{1,0:T(8,128)S(1)}, f32[72,128]{1,0:T(8,128)S(1)}, u32[]{:S(2)}, u32[]{:S(2)}) %collective-permute-start.5) | collective-permute-done | bytes 36896 | tf_op jit(solution)/shard_map/ppermute | solution.py:212
  47.9 4.4 %collective-permute-start.6 = (f32[72,128]{1,0:T(8,128)S(1)}, f32[72,128]{1,0:T(8,128)S(1)}, u32[]{:S(2)}, u32[]{:S(2)}) collective-permute-start(f32[72,128]{1,0:T(8,128)S(1)} %add.19.mine_ref), channel_id=1, source_target_pairs={{0,1},{1,0},{2,3},{3,2},{4,5},{5,4},{6,7},{7,6},{8,9},{9,8},{10,11... | collective-permute-start | bytes 110600 | tf_op jit(solution)/shard_map/ppermute | solution.py:212
  52.3 0.9 %collective-permute-done.6.other_ref = f32[72,128]{1,0:T(8,128)S(1)} collective-permute-done((f32[72,128]{1,0:T(8,128)S(1)}, f32[72,128]{1,0:T(8,128)S(1)}, u32[]{:S(2)}, u32[]{:S(2)}) %collective-permute-start.6) | collective-permute-done | bytes 36896 | tf_op jit(solution)/shard_map/ppermute | solution.py:212
  53.2 0.7 %outputs.1 = (f32[32,306]{1,0:T(8,128)}, f32[32,256]{1,0:T(8,128)}) custom-call(f32[72,128]{1,0:T(8,128)S(1)} %add.19.mine_ref, f32[72,128]{1,0:T(8,128)S(1)} %collective-permute-done.6.other_ref), custom_call_target="tpu_custom_call" | custom-call | tf_op jit(solution)/shard_map/outputs/pallas_call | solution.py:270
  (5 shorter events, 0.0 us)
Async XLA Ops:
  0.6 0.8 %copy-start.1 = (bf16[32,1024]{1,0:T(8,128)(2,1)S(1)}, bf16[32,1024]{1,0:T(8,128)(2,1)}, u32[]{:S(2)}) copy-start(bf16[32,1024]{1,0:T(8,128)(2,1)} %cv_ref.1) | copy-start | bytes 196612
  1.5 0.7 %copy-start.4 = (s32[32,4]{0,1:T(4,128)S(1)}, s32[32,4]{0,1:T(4,128)}, u32[]{:S(2)}) copy-start(s32[32,4]{0,1:T(4,128)} %param.9) | copy-start | bytes 1540
  2.2 7.0 %copy-start.2 = (bf16[32,306]{1,0:T(8,128)(2,1)S(1)}, bf16[32,306]{1,0:T(8,128)(2,1)}, u32[]{:S(2)}) copy-start(bf16[32,306]{1,0:T(8,128)(2,1)} %spatial_ref.1) | copy-start | bytes 58756
  2.2 7.0 %copy-start.3 = (bf16[32,256]{1,0:T(8,128)(2,1)S(1)}, bf16[32,256]{1,0:T(8,128)(2,1)}, u32[]{:S(2)}) copy-start(bf16[32,256]{1,0:T(8,128)(2,1)} %temporal_ref.1) | copy-start | bytes 49156
  2.3 6.9 %collective-permute-start = (bf16[32,256]{1,0:T(8,128)(2,1)S(1)}, bf16[32,256]{1,0:T(8,128)(2,1)S(1)}, u32[]{:S(2)}, u32[]{:S(2)}) collective-permute-start(bf16[32,256]{1,0:T(8,128)(2,1)S(1)} %get-tuple-element.10), channel_id=1, source_target_pairs={{0,1},{1,2},{2,3},{3,4},{4,5},{5,6},{6,7},{7,8},{8,9},{9,10},{10,1... | collective-permute-start | bytes 49160 | tf_op jit(solution)/shard_map/ppermute | solution.py:223
  10.0 15.5 %copy-start = (bf16[306,1024]{1,0:T(8,128)(2,1)S(1)}, bf16[306,1024]{1,0:T(8,128)(2,1)}, u32[]{:S(2)}) copy-start(bf16[306,1024]{1,0:T(8,128)(2,1)} %refs_3_.1) | copy-start | bytes 1880068
  27.0 1.3 %collective-permute-start.1 = (f32[72,128]{1,0:T(8,128)S(1)}, f32[72,128]{1,0:T(8,128)S(1)}, u32[]{:S(2)}, u32[]{:S(2)}) collective-permute-start(f32[72,128]{1,0:T(8,128)S(1)} %get-tuple-element.15), channel_id=1, source_target_pairs={{0,1},{1,0},{2,3},{3,2},{4,5},{5,4},{6,7},{7,6},{8,9},{9,8},{10,11... | collective-permute-start | bytes 110600 | tf_op jit(solution)/shard_map/ppermute | solution.py:212
  28.3 6.7 %collective-permute-start.2 = (f32[72,128]{1,0:T(8,128)S(1)}, f32[72,128]{1,0:T(8,128)S(1)}, u32[]{:S(2)}, u32[]{:S(2)}) collective-permute-start(f32[72,128]{1,0:T(8,128)S(1)} %add.15), channel_id=1, source_target_pairs={{0,2},{1,3},{2,0},{3,1},{4,6},{5,7},{6,4},{7,5},{8,10},{9,11},{10,... | collective-permute-start | bytes 110600 | tf_op jit(solution)/shard_map/ppermute | solution.py:212
  35.0 2.8 %collective-permute-start.3 = (f32[72,128]{1,0:T(8,128)S(1)}, f32[72,128]{1,0:T(8,128)S(1)}, u32[]{:S(2)}, u32[]{:S(2)}) collective-permute-start(f32[72,128]{1,0:T(8,128)S(1)} %add.16), channel_id=1, source_target_pairs={{0,4},{1,5},{2,6},{3,7},{4,0},{5,1},{6,2},{7,3},{8,12},{9,13},{10,... | collective-permute-start | bytes 110600 | tf_op jit(solution)/shard_map/ppermute | solution.py:212
  37.8 5.7 %collective-permute-start.4 = (f32[72,128]{1,0:T(8,128)S(1)}, f32[72,128]{1,0:T(8,128)S(1)}, u32[]{:S(2)}, u32[]{:S(2)}) collective-permute-start(f32[72,128]{1,0:T(8,128)S(1)} %add.17), channel_id=1, source_target_pairs={{0,8},{1,9},{2,10},{3,11},{4,12},{5,13},{6,14},{7,15},{8,0},{9,1},... | collective-permute-start | bytes 110600 | tf_op jit(solution)/shard_map/ppermute | solution.py:212
  43.5 4.4 %collective-permute-start.5 = (f32[72,128]{1,0:T(8,128)S(1)}, f32[72,128]{1,0:T(8,128)S(1)}, u32[]{:S(2)}, u32[]{:S(2)}) collective-permute-start(f32[72,128]{1,0:T(8,128)S(1)} %add.18), channel_id=1, source_target_pairs={{0,28},{1,29},{2,30},{3,31},{4,24},{5,25},{6,26},{7,27},{8,20},{9,... | collective-permute-start | bytes 110600 | tf_op jit(solution)/shard_map/ppermute | solution.py:212
  47.9 5.3 %collective-permute-start.6 = (f32[72,128]{1,0:T(8,128)S(1)}, f32[72,128]{1,0:T(8,128)S(1)}, u32[]{:S(2)}, u32[]{:S(2)}) collective-permute-start(f32[72,128]{1,0:T(8,128)S(1)} %add.19.mine_ref), channel_id=1, source_target_pairs={{0,1},{1,0},{2,3},{3,2},{4,5},{5,4},{6,7},{7,6},{8,9},{9,8},{10,11... | collective-permute-start | bytes 110600 | tf_op jit(solution)/shard_map/ppermute | solution.py:212

commit v5 on v4

--- a/solution.py
+++ b/solution.py
@@ -23,15 +23,19 @@
     return cols >= rows
 
 
-def codes_kernel(cv_ref, mask_ref, tail_ref, own_ref):
+def diagonal_kernel(out_ref):
+    down = lax.broadcasted_iota(jnp.int32, out_ref.shape, 0)
+    along = lax.broadcasted_iota(jnp.int32, out_ref.shape, 1)
+    out_ref[...] = jnp.where(down == along, 1.0, 0.0)
+
+
+def codes_kernel(diagonal_ref, cv_ref, mask_ref, tail_ref, own_ref):
     atoms, samples = cv_ref.shape
     length = tail_ref.shape[1]
     per = length // LANES
-    down = lax.broadcasted_iota(jnp.int32, (atoms, atoms), 0)
-    along = lax.broadcasted_iota(jnp.int32, (atoms, atoms), 1)
     for b in reversed(range(samples // length)):
-        across = jnp.broadcast_to(mask_ref[b : b + 1, :], (atoms, atoms))
-        on = jnp.sum(jnp.where(down == along, across, 0).astype(jnp.float32), axis=1, keepdims=True)
+        across = diagonal_ref[...] * mask_ref[b : b + 1, :].astype(jnp.float32)
+        on = jnp.sum(across, axis=1, keepdims=True)
         block = cv_ref[:, b * length : (b + 1) * length].astype(jnp.float32) * on
         if (b + 1) * length == samples:
             tail_ref[...] = block.astype(jnp.bfloat16)
@@ -211,6 +215,13 @@
     def swapped(value, bit):
         return lax.ppermute(value, "tm", [(i, i ^ bit) for i in range(slabs)])
 
+    diagonal = pl.pallas_call(
+        diagonal_kernel,
+        out_shape=jax.ShapeDtypeStruct((atoms, atoms), jnp.float32),
+        compiler_params=params,
+        cost_estimate=pl.CostEstimate(flops=4_000_000_000, bytes_accessed=8_000_000, transcendentals=0),
+        name="diagonal",
+    )()
     tail, codes = pl.pallas_call(
         codes_kernel,
         out_shape=(
@@ -219,7 +230,7 @@
         ),
         compiler_params=params,
         name="codes",
-    )(code_values, block_mask.T)
+    )(diagonal, code_values, block_mask.T)
     halo = lax.ppermute(tail, "tm", [(i, i + 1) for i in range(slabs - 1)])
     send, xs = pl.pallas_call(
         course_kernel,

time: 54.4 us -> 53.7 us (0.987)
  local copies, waits for them, and re-layouts: 1.53 us -> 0.83 us
    unnamed x10, local copies, waits for them, and re-layouts: 1.53 us -> 0.83 us
where the time goes in v5:
time: 53.7 us; the launch traced here: 53.2 us
  starting transfers between devices  24 us (45%)
  blocking collectives  15.5 us (29%)
  waiting for transfers between devices  7.91 us (15%)
  Pallas kernels  4.26 us (8%)
  local copies, waits for them, and re-layouts  0.83 us (2%)
  between operations  0.71 us (1%)
    ppermute x6, starting transfers between devices, swapped(): return lax.ppermute(value, 'tm', [(i, i ^ bit) for i in range(slabs)])  17.9 us
    all_to_all x1, blocking collectives, local(): lax.all_to_all(send, 'atom', split_axis=0, concat_axis=0, tiled=True)  15.5 us
    ppermute x6, waiting for transfers between devices, swapped(): return lax.ppermute(value, 'tm', [(i, i ^ bit) for i in range(slabs)])  7.06 us
    ppermute x1, starting transfers between devices, local(): halo = lax.ppermute(tail, 'tm', [(i, i + 1) for i in range(slabs - 1)])  6.04 us
    pallas_call x1, Pallas kernels, local(): pl.pallas_call(lambda *refs: other_half_kernel(factor, *refs), out_shape=...  1.58 us
    pallas_call x1, Pallas kernels, local(): pl.pallas_call(lambda *refs: own_half_kernel(factor, *refs), out_shape=sh...  1.08 us
  transfers between devices with their start and end apart: 7, of which 7 were waited for; matrix products, arithmetic and copies ran while one was open for 0% of the time, Pallas kernels for 2%

profile of v5, /device:TPU:1, one launch (start us, length us, event | category | flops | bytes accessed | tf_op | source)
XLA Modules:
  0.0 53.2 jit_solution(6557022342462629939)
XLA Ops:
  0.6 0.0 copy-start.1
  0.6 0.0 copy-start.4
  0.7 0.8 %copy-done.1 = bf16[32,1024]{1,0:T(8,128)(2,1)S(1)} copy-done((bf16[32,1024]{1,0:T(8,128)(2,1)S(1)}, bf16[32,1024]{1,0:T(8,128)(2,1)}, u32[]{:S(2)}) %copy-start.1) | copy-done | bytes 65560
  1.5 0.0 copy-done.4
  1.5 0.0 copy-start.2
  1.5 0.0 copy-start.3
  1.5 0.1 codes.1
  1.6 6.0 %collective-permute-start = (bf16[32,256]{1,0:T(8,128)(2,1)S(1)}, bf16[32,256]{1,0:T(8,128)(2,1)S(1)}, u32[]{:S(2)}, u32[]{:S(2)}) collective-permute-start(bf16[32,256]{1,0:T(8,128)(2,1)S(1)} %get-tuple-element.10), channel_id=1, source_target_pairs={{0,1},{1,2},{2,3},{3,4},{4,5},{5,6},{6,7},{7,8},{8,9},{9,10},{10,1... | collective-permute-start | bytes 49160 | tf_op jit(solution)/shard_map/ppermute | solution.py:234
  7.6 0.8 %collective-permute-done.halo_ref = bf16[32,256]{1,0:T(8,128)(2,1)S(1)} collective-permute-done((bf16[32,256]{1,0:T(8,128)(2,1)S(1)}, bf16[32,256]{1,0:T(8,128)(2,1)S(1)}, u32[]{:S(2)}, u32[]{:S(2)}) %collective-permute-start) | collective-permute-done | bytes 16416 | tf_op jit(solution)/shard_map/ppermute | solution.py:234
  8.5 0.0 copy-done.2
  8.5 0.0 copy-done.3
  8.5 0.8 %course.1 = (bf16[8,32,1408]{2,1,0:T(8,128)(2,1)S(1)}, f32[320,128]{1,0:T(8,128)S(1)}) custom-call(f32[256,128]{1,0:T(8,128)S(1)} %get-tuple-element.9.own_ref, bf16[32,256]{1,0:T(8,128)(2,1)S(1)} %collective-permute-done.halo_ref, bf16[32,256]{1,0:T(8,128)(2,1)S(1)} %copy-done.3, bf16[32,306]{1,0:T(8,128)(2,1)S(1)} %copy-done.2), custom_call_target="tpu_custom_call" | custom-call | tf_op jit(solution)/shard_map/course/pallas_call | solution.py:235
  9.3 0.0 copy-start
  9.3 15.5 %all_to_all.5.refs_0_ = bf16[8,32,1408]{2,1,0:T(8,128)(2,1)S(1)} all-to-all(bf16[8,32,1408]{2,1,0:T(8,128)(2,1)S(1)} %get-tuple-element.11.refs_1_), channel_id=1, replica_groups=mesh['atom'=8,'tm'=32] {'atom'}, dimensions={0} | all-to-all | bytes 1441792 | tf_op jit(solution)/shard_map/all_to_all | solution.py:248
  24.8 0.0 copy-done
  24.8 1.6 %other_half.1 = (f32[72,128]{1,0:T(8,128)S(1)}, f32[32,384]{1,0:T(8,128)S(1)}, f32[256,128]{1,0:T(8,128)S(1)}) custom-call(bf16[8,32,1408]{2,1,0:T(8,128)(2,1)S(1)} %all_to_all.5.refs_0_, bf16[8,32,1408]{2,1,0:T(8,128)(2,1)S(1)} %get-tuple-element.11.refs_1_, f32[320,128]{1,0:T(8,128)S(1)} %get-tuple-element.12.refs_2_.refs_1_, bf16[306,1024]{1,0:T(8,128)(2,1)S(1)} %copy-done), custom_call_target="tpu_custom_call" | custom-call | tf_op jit(solution)/shard_map/other_half/pallas_call | solution.py:259
  26.4 0.1 collective-permute-start.1
  26.5 1.1 %own_half.1 = f32[72,128]{1,0:T(8,128)S(1)} custom-call(f32[32,384]{1,0:T(8,128)S(1)} %get-tuple-element.13.refs_0_, f32[320,128]{1,0:T(8,128)S(1)} %get-tuple-element.12.refs_2_.refs_1_, f32[256,128]{1,0:T(8,128)S(1)} %get-tuple-element.14.refs_2_), custom_call_target="tpu_custom_call" | custom-call | flops 200000000 | bytes 1000000 | tf_op jit(solution)/shard_map/own_half/pallas_call | solution.py:270
  27.5 0.1 collective-permute-done.1
  27.7 4.9 %collective-permute-start.2 = (f32[72,128]{1,0:T(8,128)S(1)}, f32[72,128]{1,0:T(8,128)S(1)}, u32[]{:S(2)}, u32[]{:S(2)}) collective-permute-start(f32[72,128]{1,0:T(8,128)S(1)} %add.15), channel_id=1, source_target_pairs={{0,2},{1,3},{2,0},{3,1},{4,6},{5,7},{6,4},{7,5},{8,10},{9,11},{10,... | collective-permute-start | bytes 110600 | tf_op jit(solution)/shard_map/ppermute | solution.py:216
  32.5 1.8 %collective-permute-done.2 = f32[72,128]{1,0:T(8,128)S(1)} collective-permute-done((f32[72,128]{1,0:T(8,128)S(1)}, f32[72,128]{1,0:T(8,128)S(1)}, u32[]{:S(2)}, u32[]{:S(2)}) %collective-permute-start.2) | collective-permute-done | bytes 36896 | tf_op jit(solution)/shard_map/ppermute | solution.py:216
  34.3 1.2 %collective-permute-start.3 = (f32[72,128]{1,0:T(8,128)S(1)}, f32[72,128]{1,0:T(8,128)S(1)}, u32[]{:S(2)}, u32[]{:S(2)}) collective-permute-start(f32[72,128]{1,0:T(8,128)S(1)} %add.16), channel_id=1, source_target_pairs={{0,4},{1,5},{2,6},{3,7},{4,0},{5,1},{6,2},{7,3},{8,12},{9,13},{10,... | collective-permute-start | bytes 110600 | tf_op jit(solution)/shard_map/ppermute | solution.py:216
  35.5 1.6 %collective-permute-done.3 = f32[72,128]{1,0:T(8,128)S(1)} collective-permute-done((f32[72,128]{1,0:T(8,128)S(1)}, f32[72,128]{1,0:T(8,128)S(1)}, u32[]{:S(2)}, u32[]{:S(2)}) %collective-permute-start.3) | collective-permute-done | bytes 36896 | tf_op jit(solution)/shard_map/ppermute | solution.py:216
  37.1 4.4 %collective-permute-start.4 = (f32[72,128]{1,0:T(8,128)S(1)}, f32[72,128]{1,0:T(8,128)S(1)}, u32[]{:S(2)}, u32[]{:S(2)}) collective-permute-start(f32[72,128]{1,0:T(8,128)S(1)} %add.17), channel_id=1, source_target_pairs={{0,8},{1,9},{2,10},{3,11},{4,12},{5,13},{6,14},{7,15},{8,0},{9,1},... | collective-permute-start | bytes 110600 | tf_op jit(solution)/shard_map/ppermute | solution.py:216
  41.5 1.3 %collective-permute-done.4 = f32[72,128]{1,0:T(8,128)S(1)} collective-permute-done((f32[72,128]{1,0:T(8,128)S(1)}, f32[72,128]{1,0:T(8,128)S(1)}, u32[]{:S(2)}, u32[]{:S(2)}) %collective-permute-start.4) | collective-permute-done | bytes 36896 | tf_op jit(solution)/shard_map/ppermute | solution.py:216
  42.9 3.0 %collective-permute-start.5 = (f32[72,128]{1,0:T(8,128)S(1)}, f32[72,128]{1,0:T(8,128)S(1)}, u32[]{:S(2)}, u32[]{:S(2)}) collective-permute-start(f32[72,128]{1,0:T(8,128)S(1)} %add.18), channel_id=1, source_target_pairs={{0,28},{1,29},{2,30},{3,31},{4,24},{5,25},{6,26},{7,27},{8,20},{9,... | collective-permute-start | bytes 110600 | tf_op jit(solution)/shard_map/ppermute | solution.py:216
  45.9 1.3 %collective-permute-done.5 = f32[72,128]{1,0:T(8,128)S(1)} collective-permute-done((f32[72,128]{1,0:T(8,128)S(1)}, f32[72,128]{1,0:T(8,128)S(1)}, u32[]{:S(2)}, u32[]{:S(2)}) %collective-permute-start.5) | collective-permute-done | bytes 36896 | tf_op jit(solution)/shard_map/ppermute | solution.py:216
  47.2 4.4 %collective-permute-start.6 = (f32[72,128]{1,0:T(8,128)S(1)}, f32[72,128]{1,0:T(8,128)S(1)}, u32[]{:S(2)}, u32[]{:S(2)}) collective-permute-start(f32[72,128]{1,0:T(8,128)S(1)} %add.19.mine_ref), channel_id=1, source_target_pairs={{0,1},{1,0},{2,3},{3,2},{4,5},{5,4},{6,7},{7,6},{8,9},{9,8},{10,11... | collective-permute-start | bytes 110600 | tf_op jit(solution)/shard_map/ppermute | solution.py:216
  51.6 0.9 %collective-permute-done.6.other_ref = f32[72,128]{1,0:T(8,128)S(1)} collective-permute-done((f32[72,128]{1,0:T(8,128)S(1)}, f32[72,128]{1,0:T(8,128)S(1)}, u32[]{:S(2)}, u32[]{:S(2)}) %collective-permute-start.6) | collective-permute-done | bytes 36896 | tf_op jit(solution)/shard_map/ppermute | solution.py:216
  52.5 0.7 %outputs.1 = (f32[32,306]{1,0:T(8,128)}, f32[32,256]{1,0:T(8,128)}) custom-call(f32[72,128]{1,0:T(8,128)S(1)} %add.19.mine_ref, f32[72,128]{1,0:T(8,128)S(1)} %collective-permute-done.6.other_ref), custom_call_target="tpu_custom_call" | custom-call | tf_op jit(solution)/shard_map/outputs/pallas_call | solution.py:281
  (6 shorter events, 0.0 us)
Async XLA Ops:
  0.6 0.8 %copy-start.1 = (bf16[32,1024]{1,0:T(8,128)(2,1)S(1)}, bf16[32,1024]{1,0:T(8,128)(2,1)}, u32[]{:S(2)}) copy-start(bf16[32,1024]{1,0:T(8,128)(2,1)} %cv_ref.1) | copy-start | bytes 196612
  0.6 0.8 %copy-start.4 = (s32[32,4]{0,1:T(4,128)S(1)}, s32[32,4]{0,1:T(4,128)}, u32[]{:S(2)}) copy-start(s32[32,4]{0,1:T(4,128)} %param.9) | copy-start | bytes 1540
  1.5 7.0 %copy-start.2 = (bf16[32,306]{1,0:T(8,128)(2,1)S(1)}, bf16[32,306]{1,0:T(8,128)(2,1)}, u32[]{:S(2)}) copy-start(bf16[32,306]{1,0:T(8,128)(2,1)} %spatial_ref.1) | copy-start | bytes 58756
  1.5 7.0 %copy-start.3 = (bf16[32,256]{1,0:T(8,128)(2,1)S(1)}, bf16[32,256]{1,0:T(8,128)(2,1)}, u32[]{:S(2)}) copy-start(bf16[32,256]{1,0:T(8,128)(2,1)} %temporal_ref.1) | copy-start | bytes 49156
  1.6 6.9 %collective-permute-start = (bf16[32,256]{1,0:T(8,128)(2,1)S(1)}, bf16[32,256]{1,0:T(8,128)(2,1)S(1)}, u32[]{:S(2)}, u32[]{:S(2)}) collective-permute-start(bf16[32,256]{1,0:T(8,128)(2,1)S(1)} %get-tuple-element.10), channel_id=1, source_target_pairs={{0,1},{1,2},{2,3},{3,4},{4,5},{5,6},{6,7},{7,8},{8,9},{9,10},{10,1... | collective-permute-start | bytes 49160 | tf_op jit(solution)/shard_map/ppermute | solution.py:234
  9.3 15.5 %copy-start = (bf16[306,1024]{1,0:T(8,128)(2,1)S(1)}, bf16[306,1024]{1,0:T(8,128)(2,1)}, u32[]{:S(2)}) copy-start(bf16[306,1024]{1,0:T(8,128)(2,1)} %refs_3_.1) | copy-start | bytes 1880068
  26.4 1.3 %collective-permute-start.1 = (f32[72,128]{1,0:T(8,128)S(1)}, f32[72,128]{1,0:T(8,128)S(1)}, u32[]{:S(2)}, u32[]{:S(2)}) collective-permute-start(f32[72,128]{1,0:T(8,128)S(1)} %get-tuple-element.15), channel_id=1, source_target_pairs={{0,1},{1,0},{2,3},{3,2},{4,5},{5,4},{6,7},{7,6},{8,9},{9,8},{10,11... | collective-permute-start | bytes 110600 | tf_op jit(solution)/shard_map/ppermute | solution.py:216
  27.7 6.7 %collective-permute-start.2 = (f32[72,128]{1,0:T(8,128)S(1)}, f32[72,128]{1,0:T(8,128)S(1)}, u32[]{:S(2)}, u32[]{:S(2)}) collective-permute-start(f32[72,128]{1,0:T(8,128)S(1)} %add.15), channel_id=1, source_target_pairs={{0,2},{1,3},{2,0},{3,1},{4,6},{5,7},{6,4},{7,5},{8,10},{9,11},{10,... | collective-permute-start | bytes 110600 | tf_op jit(solution)/shard_map/ppermute | solution.py:216
  34.3 2.8 %collective-permute-start.3 = (f32[72,128]{1,0:T(8,128)S(1)}, f32[72,128]{1,0:T(8,128)S(1)}, u32[]{:S(2)}, u32[]{:S(2)}) collective-permute-start(f32[72,128]{1,0:T(8,128)S(1)} %add.16), channel_id=1, source_target_pairs={{0,4},{1,5},{2,6},{3,7},{4,0},{5,1},{6,2},{7,3},{8,12},{9,13},{10,... | collective-permute-start | bytes 110600 | tf_op jit(solution)/shard_map/ppermute | solution.py:216
  37.1 5.7 %collective-permute-start.4 = (f32[72,128]{1,0:T(8,128)S(1)}, f32[72,128]{1,0:T(8,128)S(1)}, u32[]{:S(2)}, u32[]{:S(2)}) collective-permute-start(f32[72,128]{1,0:T(8,128)S(1)} %add.17), channel_id=1, source_target_pairs={{0,8},{1,9},{2,10},{3,11},{4,12},{5,13},{6,14},{7,15},{8,0},{9,1},... | collective-permute-start | bytes 110600 | tf_op jit(solution)/shard_map/ppermute | solution.py:216
  42.9 4.4 %collective-permute-start.5 = (f32[72,128]{1,0:T(8,128)S(1)}, f32[72,128]{1,0:T(8,128)S(1)}, u32[]{:S(2)}, u32[]{:S(2)}) collective-permute-start(f32[72,128]{1,0:T(8,128)S(1)} %add.18), channel_id=1, source_target_pairs={{0,28},{1,29},{2,30},{3,31},{4,24},{5,25},{6,26},{7,27},{8,20},{9,... | collective-permute-start | bytes 110600 | tf_op jit(solution)/shard_map/ppermute | solution.py:216
  47.2 5.3 %collective-permute-start.6 = (f32[72,128]{1,0:T(8,128)S(1)}, f32[72,128]{1,0:T(8,128)S(1)}, u32[]{:S(2)}, u32[]{:S(2)}) collective-permute-start(f32[72,128]{1,0:T(8,128)S(1)} %add.19.mine_ref), channel_id=1, source_target_pairs={{0,1},{1,0},{2,3},{3,2},{4,5},{5,4},{6,7},{7,6},{8,9},{9,8},{10,11... | collective-permute-start | bytes 110600 | tf_op jit(solution)/shard_map/ppermute | solution.py:216

commit v6 on v5

--- a/solution.py
+++ b/solution.py
@@ -47,11 +47,10 @@
 def course_kernel(
     own_ref, halo_ref, temporal_ref, spatial_ref, send_ref, xs_ref, tf_ref, cs_ref
 ):
-    copies, atoms, width = send_ref.shape
-    length = temporal_ref.shape[1]
+    copies = send_ref.shape[0]
+    atoms, length = temporal_ref.shape
     channels = spatial_ref.shape[1]
     rows = own_ref.shape[0] // atoms
-    samples = rows * LANES
     per = length // LANES
     for j in range(per):
         xs_ref[j * atoms : (j + 1) * atoms, :] = halo_ref[
@@ -80,16 +79,41 @@
         cs_ref[pl.ds(k, rows, stride=atoms), :] = jnp.dot(
             windows, matrix, preferred_element_type=jnp.float32
         )
-    padded = jnp.concatenate(
-        [spatial_ref[...], jnp.zeros((atoms, width - samples - channels), jnp.bfloat16)],
+    rest = jnp.concatenate(
+        [
+            spatial_ref[:, 2 * LANES :].astype(jnp.float32),
+            jnp.zeros((atoms, 3 * LANES - channels), jnp.float32),
+        ],
         axis=1,
     )
-    for c in range(copies):
-        send_ref[c, :, samples:] = padded
-    for i in range(rows):
-        part = cs_ref[i * atoms : (i + 1) * atoms, :].astype(jnp.bfloat16)
+    tiles = [
+        cs_ref[...],
+        spatial_ref[:, :LANES],
+        spatial_ref[:, LANES : 2 * LANES],
+        rest[: atoms // 2] + pltpu.roll(rest[atoms // 2 :], HALF, 1),
+    ]
+    at = 0
+    for tile in tiles:
         for c in range(copies):
-            send_ref[c, :, i * LANES : (i + 1) * LANES] = part
+            send_ref[c, at : at + tile.shape[0], :] = tile.astype(jnp.bfloat16)
+        at += tile.shape[0]
+
+
+def unpacked(ref, groups, atoms, samples):
+    def tile(at):
+        return ref[:groups, at : at + atoms, :].reshape(groups * atoms, LANES)
+
+    end = samples // LANES * atoms
+    course = jnp.concatenate([tile(at) for at in range(0, end, atoms)], axis=1)
+    half = atoms // 2
+    rest = ref[:groups, end + 2 * atoms :, :].astype(jnp.float32).reshape(groups * half, LANES)
+    lane = lax.broadcasted_iota(jnp.int32, rest.shape, 1)
+    sides = [
+        jnp.where(lane < HALF, side, 0.0).reshape(groups, half, LANES)
+        for side in (rest, pltpu.roll(rest, HALF, 1))
+    ]
+    last = jnp.concatenate(sides, axis=1).reshape(groups * atoms, LANES).astype(jnp.bfloat16)
+    return course, jnp.concatenate([tile(end), tile(end + atoms), last], axis=1)
 
 
 def half_of(out_ref, core, space_ref, xs_ref, pr_ref, xh_ref, ph_ref, lo_ref, hi_ref, turned_ref, factor):
@@ -156,26 +180,23 @@
 def other_half_kernel(
     factor, all_ref, own_ref, xs_ref, signal_ref, other_ref, space_ref, pr_ref, res_ref, *scratch
 ):
-    groups, atoms, width = all_ref.shape
+    groups = all_ref.shape[0]
+    atoms, wide = space_ref.shape
     channels, samples = signal_ref.shape
-    wide = width - samples
-    everything = all_ref[...].reshape(groups * atoms, width)
+    course, patterns = unpacked(all_ref, groups, atoms, samples)
     model = lax.dot_general(
-        everything[:, samples:],
-        everything[:, :samples],
-        (((0,), (0,)), ((), ())),
-        preferred_element_type=jnp.float32,
+        patterns, course, (((0,), (0,)), ((), ())), preferred_element_type=jnp.float32
     )
     res_ref[channels:, :] = jnp.zeros((wide - channels, samples), jnp.bfloat16)
     res_ref[:channels, :] = (model[:channels] - signal_ref[...].astype(jnp.float32)).astype(
         jnp.bfloat16
     )
-    own = own_ref[0]
-    projected = jnp.dot(own[:, samples:], res_ref[...], preferred_element_type=jnp.float32)
+    course, patterns = unpacked(own_ref, 1, atoms, samples)
+    projected = jnp.dot(patterns, res_ref[...], preferred_element_type=jnp.float32)
     for i in range(samples // LANES):
         pr_ref[i * atoms : (i + 1) * atoms, :] = projected[:, i * LANES : (i + 1) * LANES]
     space_ref[...] = factor * lax.dot_general(
-        own[:, :samples], res_ref[...], (((1,), (1,)), ((), ())), preferred_element_type=jnp.float32
+        course, res_ref[...], (((1,), (1,)), ((), ())), preferred_element_type=jnp.float32
     )
     core = lax.axis_index("tm") % 2
     half_of(other_ref, 1 - core, space_ref, xs_ref, pr_ref, *scratch, factor)
@@ -235,7 +256,7 @@
     send, xs = pl.pallas_call(
         course_kernel,
         out_shape=(
-            jax.ShapeDtypeStruct((groups, atoms, samples + wide), jnp.bfloat16),
+            jax.ShapeDtypeStruct((groups, (rows + 2) * atoms + atoms // 2, LANES), jnp.bfloat16),
             jax.ShapeDtypeStruct(((rows + length // LANES) * atoms, LANES), jnp.float32),
         ),
         scratch_shapes=[

time: 53.7 us -> 53.3 us (level)
  no operation moved by 1% of the time
where the time goes in v6:
time: 53.3 us; the launch traced here: 52.9 us
  starting transfers between devices  24 us (45%)
  blocking collectives  15.1 us (28%)
  waiting for transfers between devices  7.91 us (15%)
  Pallas kernels  4.29 us (8%)
  local copies, waits for them, and re-layouts  0.83 us (2%)
  between operations  0.71 us (1%)
    ppermute x6, starting transfers between devices, swapped(): return lax.ppermute(value, 'tm', [(i, i ^ bit) for i in range(slabs)])  18 us
    all_to_all x1, blocking collectives, local(): lax.all_to_all(send, 'atom', split_axis=0, concat_axis=0, tiled=True)  15.1 us
    ppermute x6, waiting for transfers between devices, swapped(): return lax.ppermute(value, 'tm', [(i, i ^ bit) for i in range(slabs)])  7.06 us
    ppermute x1, starting transfers between devices, local(): halo = lax.ppermute(tail, 'tm', [(i, i + 1) for i in range(slabs - 1)])  6.04 us
    pallas_call x1, Pallas kernels, local(): pl.pallas_call(lambda *refs: other_half_kernel(factor, *refs), out_shape=...  1.63 us
    pallas_call x1, Pallas kernels, local(): pl.pallas_call(lambda *refs: own_half_kernel(factor, *refs), out_shape=sh...  1.08 us
  transfers between devices with their start and end apart: 7, of which 7 were waited for; matrix products, arithmetic and copies ran while one was open for 0% of the time, Pallas kernels for 2%

profile of v6, /device:TPU:1, one launch (start us, length us, event | category | flops | bytes accessed | tf_op | source)
XLA Modules:
  0.0 52.9 jit_solution(18148989479129994153)
XLA Ops:
  0.6 0.0 copy-start.1
  0.6 0.0 copy-start.4
  0.7 0.8 %copy-done.1 = bf16[32,1024]{1,0:T(8,128)(2,1)S(1)} copy-done((bf16[32,1024]{1,0:T(8,128)(2,1)S(1)}, bf16[32,1024]{1,0:T(8,128)(2,1)}, u32[]{:S(2)}) %copy-start.1) | copy-done | bytes 65560
  1.5 0.0 copy-done.4
  1.5 0.0 copy-start.2
  1.5 0.0 copy-start.3
  1.5 0.1 codes.1
  1.6 6.0 %collective-permute-start = (bf16[32,256]{1,0:T(8,128)(2,1)S(1)}, bf16[32,256]{1,0:T(8,128)(2,1)S(1)}, u32[]{:S(2)}, u32[]{:S(2)}) collective-permute-start(bf16[32,256]{1,0:T(8,128)(2,1)S(1)} %get-tuple-element.10), channel_id=1, source_target_pairs={{0,1},{1,2},{2,3},{3,4},{4,5},{5,6},{6,7},{7,8},{8,9},{9,10},{10,1... | collective-permute-start | bytes 49160 | tf_op jit(solution)/shard_map/ppermute | solution.py:255
  7.6 0.8 %collective-permute-done.halo_ref = bf16[32,256]{1,0:T(8,128)(2,1)S(1)} collective-permute-done((bf16[32,256]{1,0:T(8,128)(2,1)S(1)}, bf16[32,256]{1,0:T(8,128)(2,1)S(1)}, u32[]{:S(2)}, u32[]{:S(2)}) %collective-permute-start) | collective-permute-done | bytes 16416 | tf_op jit(solution)/shard_map/ppermute | solution.py:255
  8.5 0.0 copy-done.2
  8.5 0.0 copy-done.3
  8.5 0.8 %course.1 = (bf16[8,336,128]{2,1,0:T(8,128)(2,1)S(1)}, f32[320,128]{1,0:T(8,128)S(1)}) custom-call(f32[256,128]{1,0:T(8,128)S(1)} %get-tuple-element.9.own_ref, bf16[32,256]{1,0:T(8,128)(2,1)S(1)} %collective-permute-done.halo_ref, bf16[32,256]{1,0:T(8,128)(2,1)S(1)} %copy-done.3, bf16[32,306]{1,0:T(8,128)(2,1)S(1)} %copy-done.2), custom_call_target="tpu_custom_call" | custom-call | tf_op jit(solution)/shard_map/course/pallas_call | solution.py:256
  9.3 0.0 copy-start
  9.3 15.1 %all_to_all.5.refs_0_ = bf16[8,336,128]{2,1,0:T(8,128)(2,1)S(1)} all-to-all(bf16[8,336,128]{2,1,0:T(8,128)(2,1)S(1)} %get-tuple-element.11.refs_1_), channel_id=1, replica_groups=mesh['atom'=8,'tm'=32] {'atom'}, dimensions={0} | all-to-all | bytes 1376256 | tf_op jit(solution)/shard_map/all_to_all | solution.py:269
  24.4 0.0 copy-done
  24.4 1.6 %other_half.1 = (f32[72,128]{1,0:T(8,128)S(1)}, f32[32,384]{1,0:T(8,128)S(1)}, f32[256,128]{1,0:T(8,128)S(1)}) custom-call(bf16[8,336,128]{2,1,0:T(8,128)(2,1)S(1)} %all_to_all.5.refs_0_, bf16[8,336,128]{2,1,0:T(8,128)(2,1)S(1)} %get-tuple-element.11.refs_1_, f32[320,128]{1,0:T(8,128)S(1)} %get-tuple-element.12.refs_2_.refs_1_, bf16[306,1024]{1,0:T(8,128)(2,1)S(1)} %copy-done), custom_call_target="tpu_custom_call" | custom-call | tf_op jit(solution)/shard_map/other_half/pallas_call | solution.py:280
  26.0 0.1 collective-permute-start.1
  26.1 1.1 %own_half.1 = f32[72,128]{1,0:T(8,128)S(1)} custom-call(f32[32,384]{1,0:T(8,128)S(1)} %get-tuple-element.13.refs_0_, f32[320,128]{1,0:T(8,128)S(1)} %get-tuple-element.12.refs_2_.refs_1_, f32[256,128]{1,0:T(8,128)S(1)} %get-tuple-element.14.refs_2_), custom_call_target="tpu_custom_call" | custom-call | flops 200000000 | bytes 1000000 | tf_op jit(solution)/shard_map/own_half/pallas_call | solution.py:291
  27.2 0.1 collective-permute-done.1
  27.3 4.9 %collective-permute-start.2 = (f32[72,128]{1,0:T(8,128)S(1)}, f32[72,128]{1,0:T(8,128)S(1)}, u32[]{:S(2)}, u32[]{:S(2)}) collective-permute-start(f32[72,128]{1,0:T(8,128)S(1)} %add.15), channel_id=1, source_target_pairs={{0,2},{1,3},{2,0},{3,1},{4,6},{5,7},{6,4},{7,5},{8,10},{9,11},{10,... | collective-permute-start | bytes 110600 | tf_op jit(solution)/shard_map/ppermute | solution.py:237
  32.2 1.8 %collective-permute-done.2 = f32[72,128]{1,0:T(8,128)S(1)} collective-permute-done((f32[72,128]{1,0:T(8,128)S(1)}, f32[72,128]{1,0:T(8,128)S(1)}, u32[]{:S(2)}, u32[]{:S(2)}) %collective-permute-start.2) | collective-permute-done | bytes 36896 | tf_op jit(solution)/shard_map/ppermute | solution.py:237
  34.0 1.2 %collective-permute-start.3 = (f32[72,128]{1,0:T(8,128)S(1)}, f32[72,128]{1,0:T(8,128)S(1)}, u32[]{:S(2)}, u32[]{:S(2)}) collective-permute-start(f32[72,128]{1,0:T(8,128)S(1)} %add.16), channel_id=1, source_target_pairs={{0,4},{1,5},{2,6},{3,7},{4,0},{5,1},{6,2},{7,3},{8,12},{9,13},{10,... | collective-permute-start | bytes 110600 | tf_op jit(solution)/shard_map/ppermute | solution.py:237
  35.2 1.6 %collective-permute-done.3 = f32[72,128]{1,0:T(8,128)S(1)} collective-permute-done((f32[72,128]{1,0:T(8,128)S(1)}, f32[72,128]{1,0:T(8,128)S(1)}, u32[]{:S(2)}, u32[]{:S(2)}) %collective-permute-start.3) | collective-permute-done | bytes 36896 | tf_op jit(solution)/shard_map/ppermute | solution.py:237
  36.8 4.4 %collective-permute-start.4 = (f32[72,128]{1,0:T(8,128)S(1)}, f32[72,128]{1,0:T(8,128)S(1)}, u32[]{:S(2)}, u32[]{:S(2)}) collective-permute-start(f32[72,128]{1,0:T(8,128)S(1)} %add.17), channel_id=1, source_target_pairs={{0,8},{1,9},{2,10},{3,11},{4,12},{5,13},{6,14},{7,15},{8,0},{9,1},... | collective-permute-start | bytes 110600 | tf_op jit(solution)/shard_map/ppermute | solution.py:237
  41.2 1.3 %collective-permute-done.4 = f32[72,128]{1,0:T(8,128)S(1)} collective-permute-done((f32[72,128]{1,0:T(8,128)S(1)}, f32[72,128]{1,0:T(8,128)S(1)}, u32[]{:S(2)}, u32[]{:S(2)}) %collective-permute-start.4) | collective-permute-done | bytes 36896 | tf_op jit(solution)/shard_map/ppermute | solution.py:237
  42.5 3.0 %collective-permute-start.5 = (f32[72,128]{1,0:T(8,128)S(1)}, f32[72,128]{1,0:T(8,128)S(1)}, u32[]{:S(2)}, u32[]{:S(2)}) collective-permute-start(f32[72,128]{1,0:T(8,128)S(1)} %add.18), channel_id=1, source_target_pairs={{0,28},{1,29},{2,30},{3,31},{4,24},{5,25},{6,26},{7,27},{8,20},{9,... | collective-permute-start | bytes 110600 | tf_op jit(solution)/shard_map/ppermute | solution.py:237
  45.6 1.3 %collective-permute-done.5 = f32[72,128]{1,0:T(8,128)S(1)} collective-permute-done((f32[72,128]{1,0:T(8,128)S(1)}, f32[72,128]{1,0:T(8,128)S(1)}, u32[]{:S(2)}, u32[]{:S(2)}) %collective-permute-start.5) | collective-permute-done | bytes 36896 | tf_op jit(solution)/shard_map/ppermute | solution.py:237
  46.9 4.4 %collective-permute-start.6 = (f32[72,128]{1,0:T(8,128)S(1)}, f32[72,128]{1,0:T(8,128)S(1)}, u32[]{:S(2)}, u32[]{:S(2)}) collective-permute-start(f32[72,128]{1,0:T(8,128)S(1)} %add.19.mine_ref), channel_id=1, source_target_pairs={{0,1},{1,0},{2,3},{3,2},{4,5},{5,4},{6,7},{7,6},{8,9},{9,8},{10,11... | collective-permute-start | bytes 110600 | tf_op jit(solution)/shard_map/ppermute | solution.py:237
  51.3 0.9 %collective-permute-done.6.other_ref = f32[72,128]{1,0:T(8,128)S(1)} collective-permute-done((f32[72,128]{1,0:T(8,128)S(1)}, f32[72,128]{1,0:T(8,128)S(1)}, u32[]{:S(2)}, u32[]{:S(2)}) %collective-permute-start.6) | collective-permute-done | bytes 36896 | tf_op jit(solution)/shard_map/ppermute | solution.py:237
  52.2 0.7 %outputs.1 = (f32[32,306]{1,0:T(8,128)}, f32[32,256]{1,0:T(8,128)}) custom-call(f32[72,128]{1,0:T(8,128)S(1)} %add.19.mine_ref, f32[72,128]{1,0:T(8,128)S(1)} %collective-permute-done.6.other_ref), custom_call_target="tpu_custom_call" | custom-call | tf_op jit(solution)/shard_map/outputs/pallas_call | solution.py:302
  (6 shorter events, 0.0 us)
Async XLA Ops:
  0.6 0.8 %copy-start.1 = (bf16[32,1024]{1,0:T(8,128)(2,1)S(1)}, bf16[32,1024]{1,0:T(8,128)(2,1)}, u32[]{:S(2)}) copy-start(bf16[32,1024]{1,0:T(8,128)(2,1)} %cv_ref.1) | copy-start | bytes 196612
  0.6 0.8 %copy-start.4 = (s32[32,4]{0,1:T(4,128)S(1)}, s32[32,4]{0,1:T(4,128)}, u32[]{:S(2)}) copy-start(s32[32,4]{0,1:T(4,128)} %param.9) | copy-start | bytes 1540
  1.5 7.0 %copy-start.2 = (bf16[32,306]{1,0:T(8,128)(2,1)S(1)}, bf16[32,306]{1,0:T(8,128)(2,1)}, u32[]{:S(2)}) copy-start(bf16[32,306]{1,0:T(8,128)(2,1)} %spatial_ref.1) | copy-start | bytes 58756
  1.5 7.0 %copy-start.3 = (bf16[32,256]{1,0:T(8,128)(2,1)S(1)}, bf16[32,256]{1,0:T(8,128)(2,1)}, u32[]{:S(2)}) copy-start(bf16[32,256]{1,0:T(8,128)(2,1)} %temporal_ref.1) | copy-start | bytes 49156
  1.6 6.9 %collective-permute-start = (bf16[32,256]{1,0:T(8,128)(2,1)S(1)}, bf16[32,256]{1,0:T(8,128)(2,1)S(1)}, u32[]{:S(2)}, u32[]{:S(2)}) collective-permute-start(bf16[32,256]{1,0:T(8,128)(2,1)S(1)} %get-tuple-element.10), channel_id=1, source_target_pairs={{0,1},{1,2},{2,3},{3,4},{4,5},{5,6},{6,7},{7,8},{8,9},{9,10},{10,1... | collective-permute-start | bytes 49160 | tf_op jit(solution)/shard_map/ppermute | solution.py:255
  9.3 15.1 %copy-start = (bf16[306,1024]{1,0:T(8,128)(2,1)S(1)}, bf16[306,1024]{1,0:T(8,128)(2,1)}, u32[]{:S(2)}) copy-start(bf16[306,1024]{1,0:T(8,128)(2,1)} %refs_3_.1) | copy-start | bytes 1880068
  26.0 1.3 %collective-permute-start.1 = (f32[72,128]{1,0:T(8,128)S(1)}, f32[72,128]{1,0:T(8,128)S(1)}, u32[]{:S(2)}, u32[]{:S(2)}) collective-permute-start(f32[72,128]{1,0:T(8,128)S(1)} %get-tuple-element.15), channel_id=1, source_target_pairs={{0,1},{1,0},{2,3},{3,2},{4,5},{5,4},{6,7},{7,6},{8,9},{9,8},{10,11... | collective-permute-start | bytes 110600 | tf_op jit(solution)/shard_map/ppermute | solution.py:237
  27.3 6.7 %collective-permute-start.2 = (f32[72,128]{1,0:T(8,128)S(1)}, f32[72,128]{1,0:T(8,128)S(1)}, u32[]{:S(2)}, u32[]{:S(2)}) collective-permute-start(f32[72,128]{1,0:T(8,128)S(1)} %add.15), channel_id=1, source_target_pairs={{0,2},{1,3},{2,0},{3,1},{4,6},{5,7},{6,4},{7,5},{8,10},{9,11},{10,... | collective-permute-start | bytes 110600 | tf_op jit(solution)/shard_map/ppermute | solution.py:237
  34.0 2.8 %collective-permute-start.3 = (f32[72,128]{1,0:T(8,128)S(1)}, f32[72,128]{1,0:T(8,128)S(1)}, u32[]{:S(2)}, u32[]{:S(2)}) collective-permute-start(f32[72,128]{1,0:T(8,128)S(1)} %add.16), channel_id=1, source_target_pairs={{0,4},{1,5},{2,6},{3,7},{4,0},{5,1},{6,2},{7,3},{8,12},{9,13},{10,... | collective-permute-start | bytes 110600 | tf_op jit(solution)/shard_map/ppermute | solution.py:237
  36.8 5.7 %collective-permute-start.4 = (f32[72,128]{1,0:T(8,128)S(1)}, f32[72,128]{1,0:T(8,128)S(1)}, u32[]{:S(2)}, u32[]{:S(2)}) collective-permute-start(f32[72,128]{1,0:T(8,128)S(1)} %add.17), channel_id=1, source_target_pairs={{0,8},{1,9},{2,10},{3,11},{4,12},{5,13},{6,14},{7,15},{8,0},{9,1},... | collective-permute-start | bytes 110600 | tf_op jit(solution)/shard_map/ppermute | solution.py:237
  42.5 4.4 %collective-permute-start.5 = (f32[72,128]{1,0:T(8,128)S(1)}, f32[72,128]{1,0:T(8,128)S(1)}, u32[]{:S(2)}, u32[]{:S(2)}) collective-permute-start(f32[72,128]{1,0:T(8,128)S(1)} %add.18), channel_id=1, source_target_pairs={{0,28},{1,29},{2,30},{3,31},{4,24},{5,25},{6,26},{7,27},{8,20},{9,... | collective-permute-start | bytes 110600 | tf_op jit(solution)/shard_map/ppermute | solution.py:237
  46.9 5.3 %collective-permute-start.6 = (f32[72,128]{1,0:T(8,128)S(1)}, f32[72,128]{1,0:T(8,128)S(1)}, u32[]{:S(2)}, u32[]{:S(2)}) collective-permute-start(f32[72,128]{1,0:T(8,128)S(1)} %add.19.mine_ref), channel_id=1, source_target_pairs={{0,1},{1,0},{2,3},{3,2},{4,5},{5,4},{6,7},{7,6},{8,9},{9,8},{10,11... | collective-permute-start | bytes 110600 | tf_op jit(solution)/shard_map/ppermute | solution.py:237

commit v7 on v6

--- a/solution.py
+++ b/solution.py
@@ -9,7 +9,7 @@
 
 LANES = 128
 HALF = LANES // 2
-PARTNERS = (2, 4, 8, 28)
+PARTNERS = (4, 8, 28, 2)
 VMEM_BYTES = 16 << 20
 
 
@@ -127,7 +127,10 @@
         at = pl.multiple_of(i * atoms + core * half, half)
         ph_ref[i * half : (i + 1) * half, :] = pr_ref[pl.ds(at, half), :]
     group = LANES // rows
-    band = lower_band(LANES)
+    down = lax.broadcasted_iota(jnp.int32, (LANES, LANES), 0)
+    along = lax.broadcasted_iota(jnp.int32, (LANES, LANES), 1)
+    band = along + down >= LANES - 1
+    upside = jnp.where(along + down == LANES - 1, 1.0, 0.0).astype(jnp.bfloat16)
     for k in range(half):
         if k % group == 0:
             turned = []
@@ -136,7 +139,14 @@
                     [xh_ref[pl.ds(j * half + k + g, rows, stride=half), :] for g in range(group)],
                     axis=0,
                 )
-                turned.append(stacked.T.astype(jnp.bfloat16))
+                turned.append(
+                    lax.dot_general(
+                        upside,
+                        stacked.astype(jnp.bfloat16),
+                        (((1,), (1,)), ((), ())),
+                        preferred_element_type=jnp.float32,
+                    ).astype(jnp.bfloat16)
+                )
             turned_ref[...] = jnp.concatenate(turned, axis=0)
         above, below = (k % group) * rows, LANES - (k % group + 1) * rows
         placed = [ph_ref[pl.ds(k, rows, stride=half), :]]
@@ -154,20 +164,15 @@
             (lo_ref, jnp.where(band, new, mid)),
             (hi_ref, jnp.where(band, mid, old)),
         ):
-            parts = [total[:8]]
-            for a in range(1, LANES // 8):
-                parts.append(pltpu.roll(total[8 * a : 8 * a + 8], LANES - 8 * a, 1))
+            total = pltpu.roll(total, 1, 1, stride=1, stride_axis=0)
+            parts = [total[at : at + 8] for at in range(0, LANES, 8)]
             while len(parts) > 1:
                 parts = [x + y for x, y in zip(parts[::2], parts[1::2], strict=True)]
             ref[8 * k : 8 * k + 8, :] = parts[0]
-    row = lax.broadcasted_iota(jnp.int32, (8 * half, LANES), 0)
     start = pl.multiple_of(core * half, half)
     tiles = [space_ref[pl.ds(start, half), :LANES], space_ref[pl.ds(start, half), LANES : 2 * LANES]]
     for ref in (lo_ref, hi_ref):
-        total = ref[...]
-        for bit in (1, 2, 4):
-            total = jnp.where((row & bit) != 0, pltpu.roll(total, LANES - bit, 1), total)
-        tiles.append(factor * total.reshape(half, 8, LANES).sum(axis=1))
+        tiles.append(factor * ref[...].reshape(half, 8, LANES).sum(axis=1))
     for t, tile in enumerate(tiles):
         out_ref[t * half : (t + 1) * half, :] = tile
     lane = lax.broadcasted_iota(jnp.int32, (half // 2, LANES), 1)

time: 53.3 us -> 53.3 us (level)
  no operation moved by 1% of the time
where the time goes in v7:
time: 53.3 us; the launch traced here: 52.8 us
  starting transfers between devices  23.9 us (45%)
  blocking collectives  15.1 us (28%)
  waiting for transfers between devices  8.11 us (15%)
  Pallas kernels  4.16 us (8%)
  local copies, waits for them, and re-layouts  0.83 us (2%)
  between operations  0.71 us (1%)
    ppermute x6, starting transfers between devices, swapped(): return lax.ppermute(value, 'tm', [(i, i ^ bit) for i in range(slabs)])  17.9 us
    all_to_all x1, blocking collectives, local(): lax.all_to_all(send, 'atom', split_axis=0, concat_axis=0, tiled=True)  15.1 us
    ppermute x6, waiting for transfers between devices, swapped(): return lax.ppermute(value, 'tm', [(i, i ^ bit) for i in range(slabs)])  7.26 us
    ppermute x1, starting transfers between devices, local(): halo = lax.ppermute(tail, 'tm', [(i, i + 1) for i in range(slabs - 1)])  6.04 us
    pallas_call x1, Pallas kernels, local(): pl.pallas_call(lambda *refs: other_half_kernel(factor, *refs), out_shape=...  1.6 us
  transfers between devices with their start and end apart: 7, of which 7 were waited for; matrix products, arithmetic and copies ran while one was open for 0% of the time, Pallas kernels for 2%

profile of v7, /device:TPU:1, one launch (start us, length us, event | category | flops | bytes accessed | tf_op | source)
XLA Modules:
  0.0 52.8 jit_solution(15435794082396957452)
XLA Ops:
  0.6 0.0 copy-start.1
  0.6 0.0 copy-start.4
  0.7 0.8 %copy-done.1 = bf16[32,1024]{1,0:T(8,128)(2,1)S(1)} copy-done((bf16[32,1024]{1,0:T(8,128)(2,1)S(1)}, bf16[32,1024]{1,0:T(8,128)(2,1)}, u32[]{:S(2)}) %copy-start.1) | copy-done | bytes 65560
  1.5 0.0 copy-done.4
  1.5 0.0 copy-start.2
  1.5 0.0 copy-start.3
  1.5 0.1 codes.1
  1.6 6.0 %collective-permute-start = (bf16[32,256]{1,0:T(8,128)(2,1)S(1)}, bf16[32,256]{1,0:T(8,128)(2,1)S(1)}, u32[]{:S(2)}, u32[]{:S(2)}) collective-permute-start(bf16[32,256]{1,0:T(8,128)(2,1)S(1)} %get-tuple-element.10), channel_id=1, source_target_pairs={{0,1},{1,2},{2,3},{3,4},{4,5},{5,6},{6,7},{7,8},{8,9},{9,10},{10,1... | collective-permute-start | bytes 49160 | tf_op jit(solution)/shard_map/ppermute | solution.py:260
  7.6 0.8 %collective-permute-done.halo_ref = bf16[32,256]{1,0:T(8,128)(2,1)S(1)} collective-permute-done((bf16[32,256]{1,0:T(8,128)(2,1)S(1)}, bf16[32,256]{1,0:T(8,128)(2,1)S(1)}, u32[]{:S(2)}, u32[]{:S(2)}) %collective-permute-start) | collective-permute-done | bytes 16416 | tf_op jit(solution)/shard_map/ppermute | solution.py:260
  8.5 0.0 copy-done.2
  8.5 0.0 copy-done.3
  8.5 0.8 %course.1 = (bf16[8,336,128]{2,1,0:T(8,128)(2,1)S(1)}, f32[320,128]{1,0:T(8,128)S(1)}) custom-call(f32[256,128]{1,0:T(8,128)S(1)} %get-tuple-element.9.own_ref, bf16[32,256]{1,0:T(8,128)(2,1)S(1)} %collective-permute-done.halo_ref, bf16[32,256]{1,0:T(8,128)(2,1)S(1)} %copy-done.3, bf16[32,306]{1,0:T(8,128)(2,1)S(1)} %copy-done.2), custom_call_target="tpu_custom_call" | custom-call | tf_op jit(solution)/shard_map/course/pallas_call | solution.py:261
  9.3 0.0 copy-start
  9.3 15.1 %all_to_all.5.refs_0_ = bf16[8,336,128]{2,1,0:T(8,128)(2,1)S(1)} all-to-all(bf16[8,336,128]{2,1,0:T(8,128)(2,1)S(1)} %get-tuple-element.11.refs_1_), channel_id=1, replica_groups=mesh['atom'=8,'tm'=32] {'atom'}, dimensions={0} | all-to-all | bytes 1376256 | tf_op jit(solution)/shard_map/all_to_all | solution.py:274
  24.4 0.0 copy-done
  24.4 1.6 %other_half.1 = (f32[72,128]{1,0:T(8,128)S(1)}, f32[32,384]{1,0:T(8,128)S(1)}, f32[256,128]{1,0:T(8,128)S(1)}) custom-call(bf16[8,336,128]{2,1,0:T(8,128)(2,1)S(1)} %all_to_all.5.refs_0_, bf16[8,336,128]{2,1,0:T(8,128)(2,1)S(1)} %get-tuple-element.11.refs_1_, f32[320,128]{1,0:T(8,128)S(1)} %get-tuple-element.12.refs_2_.refs_1_, bf16[306,1024]{1,0:T(8,128)(2,1)S(1)} %copy-done), custom_call_target="tpu_custom_call" | custom-call | tf_op jit(solution)/shard_map/other_half/pallas_call | solution.py:285
  26.0 0.1 collective-permute-start.1
  26.1 1.0 %own_half.1 = f32[72,128]{1,0:T(8,128)S(1)} custom-call(f32[32,384]{1,0:T(8,128)S(1)} %get-tuple-element.13.refs_0_, f32[320,128]{1,0:T(8,128)S(1)} %get-tuple-element.12.refs_2_.refs_1_, f32[256,128]{1,0:T(8,128)S(1)} %get-tuple-element.14.refs_2_), custom_call_target="tpu_custom_call" | custom-call | flops 200000000 | bytes 1000000 | tf_op jit(solution)/shard_map/own_half/pallas_call | solution.py:296
  27.0 0.2 collective-permute-done.1
  27.3 3.4 %collective-permute-start.2 = (f32[72,128]{1,0:T(8,128)S(1)}, f32[72,128]{1,0:T(8,128)S(1)}, u32[]{:S(2)}, u32[]{:S(2)}) collective-permute-start(f32[72,128]{1,0:T(8,128)S(1)} %add.15), channel_id=1, source_target_pairs={{0,4},{1,5},{2,6},{3,7},{4,0},{5,1},{6,2},{7,3},{8,12},{9,13},{10,... | collective-permute-start | bytes 110600 | tf_op jit(solution)/shard_map/ppermute | solution.py:242
  30.6 1.7 %collective-permute-done.2 = f32[72,128]{1,0:T(8,128)S(1)} collective-permute-done((f32[72,128]{1,0:T(8,128)S(1)}, f32[72,128]{1,0:T(8,128)S(1)}, u32[]{:S(2)}, u32[]{:S(2)}) %collective-permute-start.2) | collective-permute-done | bytes 36896 | tf_op jit(solution)/shard_map/ppermute | solution.py:242
  32.4 2.6 %collective-permute-start.3 = (f32[72,128]{1,0:T(8,128)S(1)}, f32[72,128]{1,0:T(8,128)S(1)}, u32[]{:S(2)}, u32[]{:S(2)}) collective-permute-start(f32[72,128]{1,0:T(8,128)S(1)} %add.16), channel_id=1, source_target_pairs={{0,8},{1,9},{2,10},{3,11},{4,12},{5,13},{6,14},{7,15},{8,0},{9,1},... | collective-permute-start | bytes 110600 | tf_op jit(solution)/shard_map/ppermute | solution.py:242
  35.0 1.3 %collective-permute-done.3 = f32[72,128]{1,0:T(8,128)S(1)} collective-permute-done((f32[72,128]{1,0:T(8,128)S(1)}, f32[72,128]{1,0:T(8,128)S(1)}, u32[]{:S(2)}, u32[]{:S(2)}) %collective-permute-start.3) | collective-permute-done | bytes 36896 | tf_op jit(solution)/shard_map/ppermute | solution.py:242
  36.3 4.8 %collective-permute-start.4 = (f32[72,128]{1,0:T(8,128)S(1)}, f32[72,128]{1,0:T(8,128)S(1)}, u32[]{:S(2)}, u32[]{:S(2)}) collective-permute-start(f32[72,128]{1,0:T(8,128)S(1)} %add.17), channel_id=1, source_target_pairs={{0,28},{1,29},{2,30},{3,31},{4,24},{5,25},{6,26},{7,27},{8,20},{9,... | collective-permute-start | bytes 110600 | tf_op jit(solution)/shard_map/ppermute | solution.py:242
  41.1 1.3 %collective-permute-done.4 = f32[72,128]{1,0:T(8,128)S(1)} collective-permute-done((f32[72,128]{1,0:T(8,128)S(1)}, f32[72,128]{1,0:T(8,128)S(1)}, u32[]{:S(2)}, u32[]{:S(2)}) %collective-permute-start.4) | collective-permute-done | bytes 36896 | tf_op jit(solution)/shard_map/ppermute | solution.py:242
  42.5 2.6 %collective-permute-start.5 = (f32[72,128]{1,0:T(8,128)S(1)}, f32[72,128]{1,0:T(8,128)S(1)}, u32[]{:S(2)}, u32[]{:S(2)}) collective-permute-start(f32[72,128]{1,0:T(8,128)S(1)} %add.18), channel_id=1, source_target_pairs={{0,2},{1,3},{2,0},{3,1},{4,6},{5,7},{6,4},{7,5},{8,10},{9,11},{10,... | collective-permute-start | bytes 110600 | tf_op jit(solution)/shard_map/ppermute | solution.py:242
  45.0 1.8 %collective-permute-done.5 = f32[72,128]{1,0:T(8,128)S(1)} collective-permute-done((f32[72,128]{1,0:T(8,128)S(1)}, f32[72,128]{1,0:T(8,128)S(1)}, u32[]{:S(2)}, u32[]{:S(2)}) %collective-permute-start.5) | collective-permute-done | bytes 36896 | tf_op jit(solution)/shard_map/ppermute | solution.py:242
  46.8 4.5 %collective-permute-start.6 = (f32[72,128]{1,0:T(8,128)S(1)}, f32[72,128]{1,0:T(8,128)S(1)}, u32[]{:S(2)}, u32[]{:S(2)}) collective-permute-start(f32[72,128]{1,0:T(8,128)S(1)} %add.19.mine_ref), channel_id=1, source_target_pairs={{0,1},{1,0},{2,3},{3,2},{4,5},{5,4},{6,7},{7,6},{8,9},{9,8},{10,11... | collective-permute-start | bytes 110600 | tf_op jit(solution)/shard_map/ppermute | solution.py:242
  51.3 0.9 %collective-permute-done.6.other_ref = f32[72,128]{1,0:T(8,128)S(1)} collective-permute-done((f32[72,128]{1,0:T(8,128)S(1)}, f32[72,128]{1,0:T(8,128)S(1)}, u32[]{:S(2)}, u32[]{:S(2)}) %collective-permute-start.6) | collective-permute-done | bytes 36896 | tf_op jit(solution)/shard_map/ppermute | solution.py:242
  52.1 0.7 %outputs.1 = (f32[32,306]{1,0:T(8,128)}, f32[32,256]{1,0:T(8,128)}) custom-call(f32[72,128]{1,0:T(8,128)S(1)} %add.19.mine_ref, f32[72,128]{1,0:T(8,128)S(1)} %collective-permute-done.6.other_ref), custom_call_target="tpu_custom_call" | custom-call | tf_op jit(solution)/shard_map/outputs/pallas_call | solution.py:307
  (6 shorter events, 0.0 us)
Async XLA Ops:
  0.6 0.8 %copy-start.1 = (bf16[32,1024]{1,0:T(8,128)(2,1)S(1)}, bf16[32,1024]{1,0:T(8,128)(2,1)}, u32[]{:S(2)}) copy-start(bf16[32,1024]{1,0:T(8,128)(2,1)} %cv_ref.1) | copy-start | bytes 196612
  0.6 0.8 %copy-start.4 = (s32[32,4]{0,1:T(4,128)S(1)}, s32[32,4]{0,1:T(4,128)}, u32[]{:S(2)}) copy-start(s32[32,4]{0,1:T(4,128)} %param.9) | copy-start | bytes 1540
  1.5 7.0 %copy-start.2 = (bf16[32,306]{1,0:T(8,128)(2,1)S(1)}, bf16[32,306]{1,0:T(8,128)(2,1)}, u32[]{:S(2)}) copy-start(bf16[32,306]{1,0:T(8,128)(2,1)} %spatial_ref.1) | copy-start | bytes 58756
  1.5 7.0 %copy-start.3 = (bf16[32,256]{1,0:T(8,128)(2,1)S(1)}, bf16[32,256]{1,0:T(8,128)(2,1)}, u32[]{:S(2)}) copy-start(bf16[32,256]{1,0:T(8,128)(2,1)} %temporal_ref.1) | copy-start | bytes 49156
  1.6 6.9 %collective-permute-start = (bf16[32,256]{1,0:T(8,128)(2,1)S(1)}, bf16[32,256]{1,0:T(8,128)(2,1)S(1)}, u32[]{:S(2)}, u32[]{:S(2)}) collective-permute-start(bf16[32,256]{1,0:T(8,128)(2,1)S(1)} %get-tuple-element.10), channel_id=1, source_target_pairs={{0,1},{1,2},{2,3},{3,4},{4,5},{5,6},{6,7},{7,8},{8,9},{9,10},{10,1... | collective-permute-start | bytes 49160 | tf_op jit(solution)/shard_map/ppermute | solution.py:260
  9.3 15.1 %copy-start = (bf16[306,1024]{1,0:T(8,128)(2,1)S(1)}, bf16[306,1024]{1,0:T(8,128)(2,1)}, u32[]{:S(2)}) copy-start(bf16[306,1024]{1,0:T(8,128)(2,1)} %refs_3_.1) | copy-start | bytes 1880068
  26.0 1.3 %collective-permute-start.1 = (f32[72,128]{1,0:T(8,128)S(1)}, f32[72,128]{1,0:T(8,128)S(1)}, u32[]{:S(2)}, u32[]{:S(2)}) collective-permute-start(f32[72,128]{1,0:T(8,128)S(1)} %get-tuple-element.15), channel_id=1, source_target_pairs={{0,1},{1,0},{2,3},{3,2},{4,5},{5,4},{6,7},{7,6},{8,9},{9,8},{10,11... | collective-permute-start | bytes 110600 | tf_op jit(solution)/shard_map/ppermute | solution.py:242
  27.3 5.1 %collective-permute-start.2 = (f32[72,128]{1,0:T(8,128)S(1)}, f32[72,128]{1,0:T(8,128)S(1)}, u32[]{:S(2)}, u32[]{:S(2)}) collective-permute-start(f32[72,128]{1,0:T(8,128)S(1)} %add.15), channel_id=1, source_target_pairs={{0,4},{1,5},{2,6},{3,7},{4,0},{5,1},{6,2},{7,3},{8,12},{9,13},{10,... | collective-permute-start | bytes 110600 | tf_op jit(solution)/shard_map/ppermute | solution.py:242
  32.4 4.0 %collective-permute-start.3 = (f32[72,128]{1,0:T(8,128)S(1)}, f32[72,128]{1,0:T(8,128)S(1)}, u32[]{:S(2)}, u32[]{:S(2)}) collective-permute-start(f32[72,128]{1,0:T(8,128)S(1)} %add.16), channel_id=1, source_target_pairs={{0,8},{1,9},{2,10},{3,11},{4,12},{5,13},{6,14},{7,15},{8,0},{9,1},... | collective-permute-start | bytes 110600 | tf_op jit(solution)/shard_map/ppermute | solution.py:242
  36.3 6.1 %collective-permute-start.4 = (f32[72,128]{1,0:T(8,128)S(1)}, f32[72,128]{1,0:T(8,128)S(1)}, u32[]{:S(2)}, u32[]{:S(2)}) collective-permute-start(f32[72,128]{1,0:T(8,128)S(1)} %add.17), channel_id=1, source_target_pairs={{0,28},{1,29},{2,30},{3,31},{4,24},{5,25},{6,26},{7,27},{8,20},{9,... | collective-permute-start | bytes 110600 | tf_op jit(solution)/shard_map/ppermute | solution.py:242
  42.5 4.3 %collective-permute-start.5 = (f32[72,128]{1,0:T(8,128)S(1)}, f32[72,128]{1,0:T(8,128)S(1)}, u32[]{:S(2)}, u32[]{:S(2)}) collective-permute-start(f32[72,128]{1,0:T(8,128)S(1)} %add.18), channel_id=1, source_target_pairs={{0,2},{1,3},{2,0},{3,1},{4,6},{5,7},{6,4},{7,5},{8,10},{9,11},{10,... | collective-permute-start | bytes 110600 | tf_op jit(solution)/shard_map/ppermute | solution.py:242
  46.8 5.3 %collective-permute-start.6 = (f32[72,128]{1,0:T(8,128)S(1)}, f32[72,128]{1,0:T(8,128)S(1)}, u32[]{:S(2)}, u32[]{:S(2)}) collective-permute-start(f32[72,128]{1,0:T(8,128)S(1)} %add.19.mine_ref), channel_id=1, source_target_pairs={{0,1},{1,0},{2,3},{3,2},{4,5},{5,4},{6,7},{7,6},{8,9},{9,8},{10,11... | collective-permute-start | bytes 110600 | tf_op jit(solution)/shard_map/ppermute | solution.py:242

commit v8 on v7

--- a/solution.py
+++ b/solution.py
@@ -9,7 +9,7 @@
 
 LANES = 128
 HALF = LANES // 2
-PARTNERS = (4, 8, 28, 2)
+PARTNERS = (4,28,8,2)
 VMEM_BYTES = 16 << 20
 
 

time: 53.3 us -> 53.8 us (level)
  starting transfers between devices: 23.9 us -> 25.1 us
    ppermute x6, starting transfers between devices: 17.9 us -> 19 us  [swapped(): return lax.ppermute(value, 'tm', [(i, i ^ bit) for i in range(slabs)])]
where the time goes in v8:
time: 53.8 us; the launch traced here: 53.6 us
  starting transfers between devices  25.1 us (47%)
  blocking collectives  15.1 us (28%)
  waiting for transfers between devices  7.7 us (14%)
  Pallas kernels  4.16 us (8%)
  local copies, waits for them, and re-layouts  0.83 us (2%)
  between operations  0.71 us (1%)
    ppermute x6, starting transfers between devices, swapped(): return lax.ppermute(value, 'tm', [(i, i ^ bit) for i in range(slabs)])  19 us
    all_to_all x1, blocking collectives, local(): lax.all_to_all(send, 'atom', split_axis=0, concat_axis=0, tiled=True)  15.1 us
    ppermute x6, waiting for transfers between devices, swapped(): return lax.ppermute(value, 'tm', [(i, i ^ bit) for i in range(slabs)])  6.85 us
    ppermute x1, starting transfers between devices, local(): halo = lax.ppermute(tail, 'tm', [(i, i + 1) for i in range(slabs - 1)])  6.04 us
    pallas_call x1, Pallas kernels, local(): pl.pallas_call(lambda *refs: other_half_kernel(factor, *refs), out_shape=...  1.6 us
  transfers between devices with their start and end apart: 7, of which 7 were waited for; matrix products, arithmetic and copies ran while one was open for 0% of the time, Pallas kernels for 2%

profile of v8, /device:TPU:1, one launch (start us, length us, event | category | flops | bytes accessed | tf_op | source)
XLA Modules:
  0.0 53.6 jit_solution(17080725460486027084)
XLA Ops:
  0.6 0.0 copy-start.1
  0.6 0.0 copy-start.4
  0.7 0.8 %copy-done.1 = bf16[32,1024]{1,0:T(8,128)(2,1)S(1)} copy-done((bf16[32,1024]{1,0:T(8,128)(2,1)S(1)}, bf16[32,1024]{1,0:T(8,128)(2,1)}, u32[]{:S(2)}) %copy-start.1) | copy-done | bytes 65560
  1.5 0.0 copy-done.4
  1.5 0.0 copy-start.2
  1.5 0.0 copy-start.3
  1.5 0.1 codes.1
  1.6 6.0 %collective-permute-start = (bf16[32,256]{1,0:T(8,128)(2,1)S(1)}, bf16[32,256]{1,0:T(8,128)(2,1)S(1)}, u32[]{:S(2)}, u32[]{:S(2)}) collective-permute-start(bf16[32,256]{1,0:T(8,128)(2,1)S(1)} %get-tuple-element.10), channel_id=1, source_target_pairs={{0,1},{1,2},{2,3},{3,4},{4,5},{5,6},{6,7},{7,8},{8,9},{9,10},{10,1... | collective-permute-start | bytes 49160 | tf_op jit(solution)/shard_map/ppermute | solution.py:260
  7.6 0.8 %collective-permute-done.halo_ref = bf16[32,256]{1,0:T(8,128)(2,1)S(1)} collective-permute-done((bf16[32,256]{1,0:T(8,128)(2,1)S(1)}, bf16[32,256]{1,0:T(8,128)(2,1)S(1)}, u32[]{:S(2)}, u32[]{:S(2)}) %collective-permute-start) | collective-permute-done | bytes 16416 | tf_op jit(solution)/shard_map/ppermute | solution.py:260
  8.5 0.0 copy-done.2
  8.5 0.0 copy-done.3
  8.5 0.8 %course.1 = (bf16[8,336,128]{2,1,0:T(8,128)(2,1)S(1)}, f32[320,128]{1,0:T(8,128)S(1)}) custom-call(f32[256,128]{1,0:T(8,128)S(1)} %get-tuple-element.9.own_ref, bf16[32,256]{1,0:T(8,128)(2,1)S(1)} %collective-permute-done.halo_ref, bf16[32,256]{1,0:T(8,128)(2,1)S(1)} %copy-done.3, bf16[32,306]{1,0:T(8,128)(2,1)S(1)} %copy-done.2), custom_call_target="tpu_custom_call" | custom-call | tf_op jit(solution)/shard_map/course/pallas_call | solution.py:261
  9.3 0.0 copy-start
  9.3 15.1 %all_to_all.5.refs_0_ = bf16[8,336,128]{2,1,0:T(8,128)(2,1)S(1)} all-to-all(bf16[8,336,128]{2,1,0:T(8,128)(2,1)S(1)} %get-tuple-element.11.refs_1_), channel_id=1, replica_groups=mesh['atom'=8,'tm'=32] {'atom'}, dimensions={0} | all-to-all | bytes 1376256 | tf_op jit(solution)/shard_map/all_to_all | solution.py:274
  24.4 0.0 copy-done
  24.4 1.6 %other_half.1 = (f32[72,128]{1,0:T(8,128)S(1)}, f32[32,384]{1,0:T(8,128)S(1)}, f32[256,128]{1,0:T(8,128)S(1)}) custom-call(bf16[8,336,128]{2,1,0:T(8,128)(2,1)S(1)} %all_to_all.5.refs_0_, bf16[8,336,128]{2,1,0:T(8,128)(2,1)S(1)} %get-tuple-element.11.refs_1_, f32[320,128]{1,0:T(8,128)S(1)} %get-tuple-element.12.refs_2_.refs_1_, bf16[306,1024]{1,0:T(8,128)(2,1)S(1)} %copy-done), custom_call_target="tpu_custom_call" | custom-call | tf_op jit(solution)/shard_map/other_half/pallas_call | solution.py:285
  26.0 0.1 collective-permute-start.1
  26.1 1.0 %own_half.1 = f32[72,128]{1,0:T(8,128)S(1)} custom-call(f32[32,384]{1,0:T(8,128)S(1)} %get-tuple-element.13.refs_0_, f32[320,128]{1,0:T(8,128)S(1)} %get-tuple-element.12.refs_2_.refs_1_, f32[256,128]{1,0:T(8,128)S(1)} %get-tuple-element.14.refs_2_), custom_call_target="tpu_custom_call" | custom-call | flops 200000000 | bytes 1000000 | tf_op jit(solution)/shard_map/own_half/pallas_call | solution.py:296
  27.0 0.2 collective-permute-done.1
  27.3 3.4 %collective-permute-start.2 = (f32[72,128]{1,0:T(8,128)S(1)}, f32[72,128]{1,0:T(8,128)S(1)}, u32[]{:S(2)}, u32[]{:S(2)}) collective-permute-start(f32[72,128]{1,0:T(8,128)S(1)} %add.15), channel_id=1, source_target_pairs={{0,4},{1,5},{2,6},{3,7},{4,0},{5,1},{6,2},{7,3},{8,12},{9,13},{10,... | collective-permute-start | bytes 110600 | tf_op jit(solution)/shard_map/ppermute | solution.py:242
  30.6 1.7 %collective-permute-done.2 = f32[72,128]{1,0:T(8,128)S(1)} collective-permute-done((f32[72,128]{1,0:T(8,128)S(1)}, f32[72,128]{1,0:T(8,128)S(1)}, u32[]{:S(2)}, u32[]{:S(2)}) %collective-permute-start.2) | collective-permute-done | bytes 36896 | tf_op jit(solution)/shard_map/ppermute | solution.py:242
  32.4 5.0 %collective-permute-start.3 = (f32[72,128]{1,0:T(8,128)S(1)}, f32[72,128]{1,0:T(8,128)S(1)}, u32[]{:S(2)}, u32[]{:S(2)}) collective-permute-start(f32[72,128]{1,0:T(8,128)S(1)} %add.16), channel_id=1, source_target_pairs={{0,28},{1,29},{2,30},{3,31},{4,24},{5,25},{6,26},{7,27},{8,20},{9,... | collective-permute-start | bytes 110600 | tf_op jit(solution)/shard_map/ppermute | solution.py:242
  37.4 1.3 %collective-permute-done.3 = f32[72,128]{1,0:T(8,128)S(1)} collective-permute-done((f32[72,128]{1,0:T(8,128)S(1)}, f32[72,128]{1,0:T(8,128)S(1)}, u32[]{:S(2)}, u32[]{:S(2)}) %collective-permute-start.3) | collective-permute-done | bytes 36896 | tf_op jit(solution)/shard_map/ppermute | solution.py:242
  38.7 3.0 %collective-permute-start.4 = (f32[72,128]{1,0:T(8,128)S(1)}, f32[72,128]{1,0:T(8,128)S(1)}, u32[]{:S(2)}, u32[]{:S(2)}) collective-permute-start(f32[72,128]{1,0:T(8,128)S(1)} %add.17), channel_id=1, source_target_pairs={{0,8},{1,9},{2,10},{3,11},{4,12},{5,13},{6,14},{7,15},{8,0},{9,1},... | collective-permute-start | bytes 110600 | tf_op jit(solution)/shard_map/ppermute | solution.py:242
  41.8 1.3 %collective-permute-done.4 = f32[72,128]{1,0:T(8,128)S(1)} collective-permute-done((f32[72,128]{1,0:T(8,128)S(1)}, f32[72,128]{1,0:T(8,128)S(1)}, u32[]{:S(2)}, u32[]{:S(2)}) %collective-permute-start.4) | collective-permute-done | bytes 36896 | tf_op jit(solution)/shard_map/ppermute | solution.py:242
  43.1 3.7 %collective-permute-start.5 = (f32[72,128]{1,0:T(8,128)S(1)}, f32[72,128]{1,0:T(8,128)S(1)}, u32[]{:S(2)}, u32[]{:S(2)}) collective-permute-start(f32[72,128]{1,0:T(8,128)S(1)} %add.18), channel_id=1, source_target_pairs={{0,2},{1,3},{2,0},{3,1},{4,6},{5,7},{6,4},{7,5},{8,10},{9,11},{10,... | collective-permute-start | bytes 110600 | tf_op jit(solution)/shard_map/ppermute | solution.py:242
  46.8 1.3 %collective-permute-done.5 = f32[72,128]{1,0:T(8,128)S(1)} collective-permute-done((f32[72,128]{1,0:T(8,128)S(1)}, f32[72,128]{1,0:T(8,128)S(1)}, u32[]{:S(2)}, u32[]{:S(2)}) %collective-permute-start.5) | collective-permute-done | bytes 36896 | tf_op jit(solution)/shard_map/ppermute | solution.py:242
  48.2 3.8 %collective-permute-start.6 = (f32[72,128]{1,0:T(8,128)S(1)}, f32[72,128]{1,0:T(8,128)S(1)}, u32[]{:S(2)}, u32[]{:S(2)}) collective-permute-start(f32[72,128]{1,0:T(8,128)S(1)} %add.19.mine_ref), channel_id=1, source_target_pairs={{0,1},{1,0},{2,3},{3,2},{4,5},{5,4},{6,7},{7,6},{8,9},{9,8},{10,11... | collective-permute-start | bytes 110600 | tf_op jit(solution)/shard_map/ppermute | solution.py:242
  52.0 0.9 %collective-permute-done.6.other_ref = f32[72,128]{1,0:T(8,128)S(1)} collective-permute-done((f32[72,128]{1,0:T(8,128)S(1)}, f32[72,128]{1,0:T(8,128)S(1)}, u32[]{:S(2)}, u32[]{:S(2)}) %collective-permute-start.6) | collective-permute-done | bytes 36896 | tf_op jit(solution)/shard_map/ppermute | solution.py:242
  52.9 0.7 %outputs.1 = (f32[32,306]{1,0:T(8,128)}, f32[32,256]{1,0:T(8,128)}) custom-call(f32[72,128]{1,0:T(8,128)S(1)} %add.19.mine_ref, f32[72,128]{1,0:T(8,128)S(1)} %collective-permute-done.6.other_ref), custom_call_target="tpu_custom_call" | custom-call | tf_op jit(solution)/shard_map/outputs/pallas_call | solution.py:307
  (6 shorter events, 0.0 us)
Async XLA Ops:
  0.6 0.8 %copy-start.1 = (bf16[32,1024]{1,0:T(8,128)(2,1)S(1)}, bf16[32,1024]{1,0:T(8,128)(2,1)}, u32[]{:S(2)}) copy-start(bf16[32,1024]{1,0:T(8,128)(2,1)} %cv_ref.1) | copy-start | bytes 196612
  0.6 0.8 %copy-start.4 = (s32[32,4]{0,1:T(4,128)S(1)}, s32[32,4]{0,1:T(4,128)}, u32[]{:S(2)}) copy-start(s32[32,4]{0,1:T(4,128)} %param.9) | copy-start | bytes 1540
  1.5 7.0 %copy-start.2 = (bf16[32,306]{1,0:T(8,128)(2,1)S(1)}, bf16[32,306]{1,0:T(8,128)(2,1)}, u32[]{:S(2)}) copy-start(bf16[32,306]{1,0:T(8,128)(2,1)} %spatial_ref.1) | copy-start | bytes 58756
  1.5 7.0 %copy-start.3 = (bf16[32,256]{1,0:T(8,128)(2,1)S(1)}, bf16[32,256]{1,0:T(8,128)(2,1)}, u32[]{:S(2)}) copy-start(bf16[32,256]{1,0:T(8,128)(2,1)} %temporal_ref.1) | copy-start | bytes 49156
  1.6 6.9 %collective-permute-start = (bf16[32,256]{1,0:T(8,128)(2,1)S(1)}, bf16[32,256]{1,0:T(8,128)(2,1)S(1)}, u32[]{:S(2)}, u32[]{:S(2)}) collective-permute-start(bf16[32,256]{1,0:T(8,128)(2,1)S(1)} %get-tuple-element.10), channel_id=1, source_target_pairs={{0,1},{1,2},{2,3},{3,4},{4,5},{5,6},{6,7},{7,8},{8,9},{9,10},{10,1... | collective-permute-start | bytes 49160 | tf_op jit(solution)/shard_map/ppermute | solution.py:260
  9.3 15.1 %copy-start = (bf16[306,1024]{1,0:T(8,128)(2,1)S(1)}, bf16[306,1024]{1,0:T(8,128)(2,1)}, u32[]{:S(2)}) copy-start(bf16[306,1024]{1,0:T(8,128)(2,1)} %refs_3_.1) | copy-start | bytes 1880068
  26.0 1.3 %collective-permute-start.1 = (f32[72,128]{1,0:T(8,128)S(1)}, f32[72,128]{1,0:T(8,128)S(1)}, u32[]{:S(2)}, u32[]{:S(2)}) collective-permute-start(f32[72,128]{1,0:T(8,128)S(1)} %get-tuple-element.15), channel_id=1, source_target_pairs={{0,1},{1,0},{2,3},{3,2},{4,5},{5,4},{6,7},{7,6},{8,9},{9,8},{10,11... | collective-permute-start | bytes 110600 | tf_op jit(solution)/shard_map/ppermute | solution.py:242
  27.3 5.1 %collective-permute-start.2 = (f32[72,128]{1,0:T(8,128)S(1)}, f32[72,128]{1,0:T(8,128)S(1)}, u32[]{:S(2)}, u32[]{:S(2)}) collective-permute-start(f32[72,128]{1,0:T(8,128)S(1)} %add.15), channel_id=1, source_target_pairs={{0,4},{1,5},{2,6},{3,7},{4,0},{5,1},{6,2},{7,3},{8,12},{9,13},{10,... | collective-permute-start | bytes 110600 | tf_op jit(solution)/shard_map/ppermute | solution.py:242
  32.4 6.4 %collective-permute-start.3 = (f32[72,128]{1,0:T(8,128)S(1)}, f32[72,128]{1,0:T(8,128)S(1)}, u32[]{:S(2)}, u32[]{:S(2)}) collective-permute-start(f32[72,128]{1,0:T(8,128)S(1)} %add.16), channel_id=1, source_target_pairs={{0,28},{1,29},{2,30},{3,31},{4,24},{5,25},{6,26},{7,27},{8,20},{9,... | collective-permute-start | bytes 110600 | tf_op jit(solution)/shard_map/ppermute | solution.py:242
  38.7 4.4 %collective-permute-start.4 = (f32[72,128]{1,0:T(8,128)S(1)}, f32[72,128]{1,0:T(8,128)S(1)}, u32[]{:S(2)}, u32[]{:S(2)}) collective-permute-start(f32[72,128]{1,0:T(8,128)S(1)} %add.17), channel_id=1, source_target_pairs={{0,8},{1,9},{2,10},{3,11},{4,12},{5,13},{6,14},{7,15},{8,0},{9,1},... | collective-permute-start | bytes 110600 | tf_op jit(solution)/shard_map/ppermute | solution.py:242
  43.1 5.0 %collective-permute-start.5 = (f32[72,128]{1,0:T(8,128)S(1)}, f32[72,128]{1,0:T(8,128)S(1)}, u32[]{:S(2)}, u32[]{:S(2)}) collective-permute-start(f32[72,128]{1,0:T(8,128)S(1)} %add.18), channel_id=1, source_target_pairs={{0,2},{1,3},{2,0},{3,1},{4,6},{5,7},{6,4},{7,5},{8,10},{9,11},{10,... | collective-permute-start | bytes 110600 | tf_op jit(solution)/shard_map/ppermute | solution.py:242
  48.2 4.7 %collective-permute-start.6 = (f32[72,128]{1,0:T(8,128)S(1)}, f32[72,128]{1,0:T(8,128)S(1)}, u32[]{:S(2)}, u32[]{:S(2)}) collective-permute-start(f32[72,128]{1,0:T(8,128)S(1)} %add.19.mine_ref), channel_id=1, source_target_pairs={{0,1},{1,0},{2,3},{3,2},{4,5},{5,4},{6,7},{7,6},{8,9},{9,8},{10,11... | collective-permute-start | bytes 110600 | tf_op jit(solution)/shard_map/ppermute | solution.py:242
